TPU v7x, 32 devices: a whole 2x2x4 slice. The times are simulated.
32 devices in a mesh: groups: 2 (over x), tiles: 16 (over z, y, core).
Axes of the slice: x: 2, y: 2, z: 4, core: 2. Of those that a mesh axis runs over, the one named last changes fastest.
Arguments:
- ocean_state: bfloat16 [32, 32, 128, 128], P(('groups', 'tiles')), parts along dimension 0, may hold values from -6 to 6
- cotangent: bfloat16 [32, 32, 128, 128], P(('groups', 'tiles')), parts along dimension 0, may hold values from -6 to 6
- first_kernel: bfloat16 [3, 3, 32, 128], replicated, may hold values from -0.375 to 0.375
- second_kernel: bfloat16 [3, 3, 32, 128], replicated, may hold values from -0.375 to 0.375
- neighbours: int32 [16, 8], P('tiles'), may hold values from -1 to 15, as said below
Outputs:
- state_grad: bfloat16 [32, 32, 128, 128], P(('groups', 'tiles')), parts along dimension 0
- first_grad: float32 [6, 3, 32, 128], P('groups'), parts along dimension 0
- second_grad: float32 [6, 3, 32, 128], P('groups'), parts along dimension 0
There are 2 independent parts, one for each index of `groups`. A program takes and returns all parts, laid end to end along the dimension named above; an argument that names none is the same for every part. Nothing has to cross between parts.
Inputs may be any that keep to these rules, and one draw needn't show every extreme that they name: `neighbours`: ocean tiles are numbered along a curve over a grid of 4 x 5 tiles that leaves out 4 land tiles. Row t lists the tiles above, below, left, right, above left, above right, below left and below right of tile t, -1 for land or the grid's edge; the relation is symmetric; the tile above and the tile below are each t - 1 or t + 1; tiles to the right (entries 3, 5, 7) have higher numbers than t and tiles to the left (entries 2, 4, 6) lower ones; every listed tile differs from t by at most 7, and that distance is reached in every draw.
All inputs are finite; a program needn't handle non-finite values.
Results may differ from a plain program's by a relative error of at most 0.0034.
Values may be sent and summed in bfloat16 or wider, within the bound.
No kernel may reach another device: no remote copies, remote signals or barrier semaphores. Data moves between devices by JAX's collectives and lax.ppermute only.
A program may use at most 128 MiB of HBM per device.

v0:
```python
import math

import jax
import jax.numpy as jnp
from jax import lax
from jax.sharding import PartitionSpec as P

GRID_ROWS = 4


cycle_sources = ((0, 1), (0, 0), (1, 1), (1, 0), (2, 3), (2, 2), (2, 1), (2, 0))


def as_sent(x):

    def short(part):
        return part.astype(jnp.bfloat16) if part.dtype == jnp.float32 else part

    return jax.tree.map(short, x)


def passed_along(value, axis, steps):
    count = lax.axis_size(axis)
    first, last = (max(0, -steps), min(count, count - steps))
    return lax.ppermute(value, axis, [(source, source + steps) for source in range(first, last)])


def gelu_tanh(values):
    return jax.nn.gelu(values, approximate=True)


def tile_rims(field):
    edge_rows = jnp.stack([field[:, 0], field[:, -1]], 1)
    edge_columns = jnp.stack([field[:, :, 0], field[:, :, -1]], 1)
    corners = jnp.stack([field[:, 0, 0], field[:, 0, -1], field[:, -1, 0], field[:, -1, -1]], 1)
    return (edge_rows, edge_columns, corners)


def collect(rims, send_whole, reach_dev):
    offsets = [offset for offset in range(-reach_dev, reach_dev + 1) if offset != 0]
    received = {}
    for offset in offsets:
        delta = -offset
        received[delta] = send_whole(rims, offset)
    order = sorted(received.keys())
    return tuple((jnp.stack([received[delta][member] for delta in order]) for member in range(3)))


def cycle_pieces(stacks, tile_links, own_index, field_no, reach_dev):
    pieces = []
    for direction in range(8):
        member, part_no = cycle_sources[direction]
        target = tile_links[direction]
        delta = target - own_index
        slot_no = jnp.clip(delta + reach_dev - (delta > 0).astype(jnp.int32), 0, 2 * reach_dev - 1)
        piece = lax.dynamic_index_in_dim(stacks[member], slot_no, 0, keepdims=False)[
            field_no, part_no
        ]
        pieces.append(jnp.where(target >= 0, piece, jnp.zeros_like(piece)))
    return pieces


def assemble(own_tile, pieces):
    above_row, below_row, left_col, right_col, upper_left, upper_right, lower_left, lower_right = (
        pieces
    )
    top_line = jnp.concatenate([upper_left[None], above_row, upper_right[None]], 0)
    bottom_line = jnp.concatenate([lower_left[None], below_row, lower_right[None]], 0)
    middle = jnp.concatenate([left_col[:, None], own_tile, right_col[:, None]], 1)
    return jnp.concatenate([top_line[None], middle, bottom_line[None]], 0)


def grouped(padded, kernel):
    groups_n = kernel.shape[3] // kernel.shape[2]
    result = lax.conv_general_dilated(
        padded[None],
        kernel,
        (1, 1),
        "VALID",
        dimension_numbers=("NHWC", "HWIO", "NHWC"),
        feature_group_count=groups_n,
        preferred_element_type=jnp.float32,
    )
    return result[0]


def flipped(kernel):
    width = kernel.shape[2]
    levels_n = kernel.shape[3] // width
    mirror = kernel[::-1, ::-1].reshape(3, 3, width, levels_n, width)
    return mirror.transpose(0, 1, 4, 3, 2).reshape(3, 3, width, levels_n * width)


def weight_grad(padded, cot_tile, width):
    rows_n, cols_n = (cot_tile.shape[0], cot_tile.shape[1])
    grads = cot_tile.reshape(rows_n, cols_n, -1, width)
    lines = []
    for shift_y in range(3):
        entries = []
        for shift_x in range(3):
            window = padded[shift_y : shift_y + rows_n, shift_x : shift_x + cols_n].reshape(
                rows_n, cols_n, -1, width
            )
            product = jnp.einsum(
                "hwli,hwlo->lio", window, grads, preferred_element_type=jnp.float32
            )
            entries.append(product.transpose(1, 0, 2).reshape(width, -1))
        lines.append(jnp.stack(entries))
    return jnp.stack(lines)


def local(ocean_state, cotangent, first_kernel, second_kernel, neighbours):
    width = first_kernel.shape[2]
    state_tile = ocean_state[0]
    cot_tile = cotangent[0]
    tile_links = neighbours[0]
    own_index = lax.axis_index("tiles")
    reach_dev = 2 * GRID_ROWS - 1

    def input_whole(package, offset):
        return jax.tree.map(
            lambda part, own: part.astype(own.dtype),
            passed_along(as_sent(package), "tiles", offset),
            package,
        )

    input_stacks = collect(tile_rims(jnp.stack([state_tile, cot_tile])), input_whole, reach_dev)
    padded_state = assemble(
        state_tile, cycle_pieces(input_stacks, tile_links, own_index, 0, reach_dev)
    )
    padded_cot = assemble(cot_tile, cycle_pieces(input_stacks, tile_links, own_index, 1, reach_dev))
    pre = grouped(padded_state, first_kernel)
    hidden = gelu_tanh(pre).astype(jnp.bfloat16)
    back_hidden = grouped(padded_cot, flipped(second_kernel))
    pullback = jax.vjp(gelu_tanh, pre)[1]
    pre_grad = pullback(back_hidden)[0].astype(jnp.bfloat16)

    def hidden_whole(package, offset):
        return jax.tree.map(
            lambda part, own: part.astype(own.dtype),
            passed_along(as_sent(package), "tiles", offset),
            package,
        )

    def grad_whole(package, offset):
        return jax.tree.map(
            lambda part, own: part.astype(own.dtype),
            passed_along(as_sent(package), "tiles", offset),
            package,
        )

    hidden_stacks = collect(tile_rims(hidden[None]), hidden_whole, reach_dev)
    grad_stacks = collect(tile_rims(pre_grad[None]), grad_whole, reach_dev)
    hidden_no = 0
    grad_no = 0
    padded_hidden = assemble(
        hidden, cycle_pieces(hidden_stacks, tile_links, own_index, hidden_no, reach_dev)
    )
    second_local = weight_grad(padded_hidden, cot_tile, width)
    first_local = weight_grad(padded_state, pre_grad, width)
    padded_grad = assemble(
        pre_grad, cycle_pieces(grad_stacks, tile_links, own_index, grad_no, reach_dev)
    )
    back_state = grouped(padded_grad, flipped(first_kernel))
    state_grad = (cot_tile.astype(jnp.float32) + back_state).astype(jnp.bfloat16)
    first_sum, second_sum = lax.psum((first_local, second_local), "tiles")
    scale = 1.0 / math.sqrt(lax.axis_size("tiles") * state_tile.shape[0] * state_tile.shape[1])
    return (state_grad[None], first_sum * scale, second_sum * scale)


def solution(mesh):
    placed = (
        P(("groups", "tiles"), None, None, None),
        P(("groups", "tiles"), None, None, None),
        P(),
        P(),
        P("tiles", None),
    )
    return jax.shard_map(
        local,
        mesh=mesh,
        in_specs=placed,
        out_specs=(
            P(("groups", "tiles"), None, None, None),
            P("groups", None, None, None),
            P("groups", None, None, None),
        ),
        check_vma=False,
    )
```

profile of v0, /device:TPU:0, one launch (start us, length us, event | category | flops | bytes accessed | tf_op | source)
XLA Modules:
  0.0 1123.0 jit_solution(8775320451122514439)
XLA Ops:
  61.8 11.4 %collective-permute-start.28 = (bf16[2,2,32,128]{3,0,2,1:T(2,128)(2,1)S(1)}, bf16[2,2,32,128]{3,0,2,1:T(2,128)(2,1)S(1)}, u32[]{:S(2)}, u32[]{:S(2)}) collective-permute-start(bf16[2,2,32,128]{3,0,2,1:T(2,128)(2,1)S(1)} %pad_maximum_fusion.10), channel_id=1, source_target_pairs={{0,7},{1,8},{2,9},{3,10},{4,11},{5,12},{6,13},{7,14},{8,15},{16,23... | collective-permute-start | bytes 98312 | tf_op jit(solution)/shard_map/ppermute | solution.py:25
  106.2 11.8 %collective-permute-start.14 = (bf16[2,2,128,128]{3,0,2,1:T(2,128)(2,1)}, bf16[2,2,128,128]{3,0,2,1:T(2,128)(2,1)}, u32[]{:S(2)}, u32[]{:S(2)}) collective-permute-start(bf16[2,2,128,128]{3,0,2,1:T(2,128)(2,1)} %fusion.50), channel_id=1, source_target_pairs={{0,7},{1,8},{2,9},{3,10},{4,11},{5,12},{6,13},{7,14},{8,15},{16,23... | collective-permute-start | bytes 393224 | tf_op jit(solution)/shard_map/ppermute | solution.py:25
  118.1 5.5 collective-permute-start.15
  167.5 5.9 collective-permute-done.24
  189.6 19.9 %copy.402 = bf16[1,34,130,4,32]{4,0,3,2,1:T(2,128)(2,1)} copy(bf16[1,34,130,4,32]{2,4,3,1,0:T(8,128)(2,1)} %maximum_maximum_fusion) | data formatting | bytes 2263040 | tf_op jit(solution)/shard_map/concatenate | solution.py:70
  209.5 109.9 %fusion.43 = f32[1,32,128,4,32]{4,0,3,2,1:T(1,128)} fusion(bf16[1,34,130,4,32]{4,0,3,2,1:T(2,128)(2,1)} %copy.402, bf16[3,3,32,4,32]{4,3,2,1,0:T(4,128)(2,1)S(1)} %reshape.724), kind=kOutput, calls=%fused_computation.88 | convolution fusion | flops 301989888 | bytes 3302400 | tf_op jit(solution)/shard_map/conv_general_dilated | solution.py:75
  319.4 17.6 %copy.404 = f32[1,32,128,4,32]{2,4,3,1,0:T(8,128)} copy(f32[1,32,128,4,32]{4,0,3,2,1:T(1,128)} %fusion.43) | data formatting | bytes 4194304 | tf_op jit(solution)/shard_map/conv_general_dilated | solution.py:75
  341.0 15.7 %copy.414 = bf16[1,34,130,4,32]{4,0,3,2,1:T(2,128)(2,1)} copy(bf16[1,34,130,4,32]{2,4,3,1,0:T(8,128)(2,1)S(1)} %maximum_maximum_fusion.1) | data formatting | bytes 2263040 | tf_op jit(solution)/shard_map/concatenate | solution.py:70
  356.7 32.7 %fusion.41 = f32[1,32,128,4,32]{4,0,3,2,1:T(1,128)} fusion(bf16[1,34,130,4,32]{4,0,3,2,1:T(2,128)(2,1)} %copy.414, bf16[3,3,32,4,32]{4,3,2,1,0:T(4,128)(2,1)S(1)} %copy-done.13), kind=kOutput, calls=%fused_computation.86 | convolution fusion | flops 301989888 | bytes 3302400 | tf_op jit(solution)/shard_map/conv_general_dilated | solution.py:75
  389.4 16.1 %copy.416 = f32[1,32,128,4,32]{2,4,3,1,0:T(8,128)S(1)} copy(f32[1,32,128,4,32]{4,0,3,2,1:T(1,128)} %fusion.41) | data formatting | bytes 4194304 | tf_op jit(solution)/shard_map/conv_general_dilated | solution.py:75
  410.3 5.8 collective-permute-start.98
  421.1 6.1 collective-permute-start.101
  439.8 5.4 maximum_maximum_fusion.3
  476.2 7.3 collective-permute-start.87
  498.0 6.1 collective-permute-done.91
  505.4 5.4 collective-permute-done.92
  512.1 7.4 collective-permute-done.93
  538.0 5.8 collective-permute-done.97
  585.2 7.0 collective-permute-done.51
  635.2 6.6 collective-permute-start.115
  657.2 5.9 collective-permute-done.119
  664.4 5.5 collective-permute-done.120
  671.2 7.3 collective-permute-done.121
  697.3 5.9 collective-permute-done.125
  740.6 5.7 collective-permute-done.78
  747.6 7.5 collective-permute-done.79
  811.9 11.2 collective-permute-start.56
  823.1 5.4 collective-permute-start.57
  876.4 15.7 %copy.434 = bf16[1,34,130,4,32]{4,0,3,2,1:T(2,128)(2,1)} copy(bf16[1,34,130,4,32]{2,4,3,1,0:T(8,128)(2,1)S(1)} %maximum_maximum_fusion.2) | data formatting | bytes 2263040 | tf_op jit(solution)/shard_map/concatenate | solution.py:70
  892.1 109.5 %fusion.39 = f32[1,32,128,4,32]{4,0,3,2,1:T(1,128)} fusion(bf16[1,34,130,4,32]{4,0,3,2,1:T(2,128)(2,1)} %copy.434, bf16[3,3,32,4,32]{4,3,2,1,0:T(4,128)(2,1)} %reshape.725), kind=kOutput, calls=%fused_computation.84 | convolution fusion | flops 301989888 | bytes 3302400 | tf_op jit(solution)/shard_map/conv_general_dilated | solution.py:75
  1001.6 16.1 %copy.436 = f32[1,32,128,4,32]{2,4,3,1,0:T(8,128)S(1)} copy(f32[1,32,128,4,32]{4,0,3,2,1:T(1,128)} %fusion.39) | data formatting | bytes 4194304 | tf_op jit(solution)/shard_map/conv_general_dilated | solution.py:75
  1022.1 90.5 %all-reduce.3.cloned.1.call-done = (f32[3,3,32,128]{3,2,1,0:T(8,128)}, f32[3,3,32,128]{3,2,1,0:T(8,128)}) async-done(((f32[3,3,32,128]{3,2,1,0:T(8,128)}, f32[3,3,32,128]{3,2,1,0:T(8,128)}), (f32[3,3,32,128]{3,2,1,0:T(8,128)}, f32[3,3,32,128]{3,2,1,0:T(8,128)})) %all-reduce.3.cloned.1.call-update) | async-done | bytes 294928 | tf_op jit(solution)/shard_map/psum | solution.py:166
  (602 shorter events, 500.1 us)
Async XLA Ops:
  7.2 1105.4 %all-reduce.3.cloned.1.call-start = ((), (), s32[]{:S(2)}) async-start(), calls=%async_computation | async-start | bytes 589824 | tf_op jit(solution)/shard_map/psum | solution.py:166
  14.0 33.6 %collective-permute-start = (bf16[2,4,128]{2,0,1:T(2,128)(2,1)S(1)}, bf16[2,4,128]{2,0,1:T(2,128)(2,1)S(1)}, u32[]{:S(2)}, u32[]{:S(2)}) collective-permute-start(bf16[2,4,128]{2,0,1:T(2,128)(2,1)S(1)} %pad_maximum_fusion.14), channel_id=1, source_target_pairs={{0,7},{1,8},{2,9},{3,10},{4,11},{5,12},{6,13},{7,14},{8,15},{16,23... | collective-permute-start | bytes 6152 | tf_op jit(solution)/shard_map/ppermute | solution.py:25
  19.4 30.4 %collective-permute-start.1 = (bf16[2,4,128]{2,0,1:T(2,128)(2,1)S(1)}, bf16[2,4,128]{2,0,1:T(2,128)(2,1)S(1)}, u32[]{:S(2)}, u32[]{:S(2)}) collective-permute-start(bf16[2,4,128]{2,0,1:T(2,128)(2,1)S(1)} %pad_maximum_fusion.14), channel_id=1, source_target_pairs={{0,6},{1,7},{2,8},{3,9},{4,10},{5,11},{6,12},{7,13},{8,14},{9,15},... | collective-permute-start | bytes 6152 | tf_op jit(solution)/shard_map/ppermute | solution.py:25
  23.8 27.8 %collective-permute-start.2 = (bf16[2,4,128]{2,0,1:T(2,128)(2,1)S(1)}, bf16[2,4,128]{2,0,1:T(2,128)(2,1)S(1)}, u32[]{:S(2)}, u32[]{:S(2)}) collective-permute-start(bf16[2,4,128]{2,0,1:T(2,128)(2,1)S(1)} %pad_maximum_fusion.14), channel_id=1, source_target_pairs={{0,5},{1,6},{2,7},{3,8},{4,9},{5,10},{6,11},{7,12},{8,13},{9,14},{... | collective-permute-start | bytes 6152 | tf_op jit(solution)/shard_map/ppermute | solution.py:25
  25.1 27.8 %collective-permute-start.3 = (bf16[2,4,128]{2,0,1:T(2,128)(2,1)S(1)}, bf16[2,4,128]{2,0,1:T(2,128)(2,1)S(1)}, u32[]{:S(2)}, u32[]{:S(2)}) collective-permute-start(bf16[2,4,128]{2,0,1:T(2,128)(2,1)S(1)} %pad_maximum_fusion.14), channel_id=1, source_target_pairs={{0,4},{1,5},{2,6},{3,7},{4,8},{5,9},{6,10},{7,11},{8,12},{9,13},{1... | collective-permute-start | bytes 6152 | tf_op jit(solution)/shard_map/ppermute | solution.py:25
  27.4 26.9 %collective-permute-start.4 = (bf16[2,4,128]{2,0,1:T(2,128)(2,1)S(1)}, bf16[2,4,128]{2,0,1:T(2,128)(2,1)S(1)}, u32[]{:S(2)}, u32[]{:S(2)}) collective-permute-start(bf16[2,4,128]{2,0,1:T(2,128)(2,1)S(1)} %pad_maximum_fusion.14), channel_id=1, source_target_pairs={{0,3},{1,4},{2,5},{3,6},{4,7},{5,8},{6,9},{7,10},{8,11},{9,12},{10... | collective-permute-start | bytes 6152 | tf_op jit(solution)/shard_map/ppermute | solution.py:25
  56.9 21.1 %collective-permute-start.11 = (bf16[2,4,128]{2,0,1:T(2,128)(2,1)S(1)}, bf16[2,4,128]{2,0,1:T(2,128)(2,1)S(1)}, u32[]{:S(2)}, u32[]{:S(2)}) collective-permute-start(bf16[2,4,128]{2,0,1:T(2,128)(2,1)S(1)} %pad_maximum_fusion.14), channel_id=1, source_target_pairs={{5,0},{6,1},{7,2},{8,3},{9,4},{10,5},{11,6},{12,7},{13,8},{14,9},{... | collective-permute-start | bytes 6152 | tf_op jit(solution)/shard_map/ppermute | solution.py:25
  58.2 21.1 %collective-permute-start.12 = (bf16[2,4,128]{2,0,1:T(2,128)(2,1)S(1)}, bf16[2,4,128]{2,0,1:T(2,128)(2,1)S(1)}, u32[]{:S(2)}, u32[]{:S(2)}) collective-permute-start(bf16[2,4,128]{2,0,1:T(2,128)(2,1)S(1)} %pad_maximum_fusion.14), channel_id=1, source_target_pairs={{6,0},{7,1},{8,2},{9,3},{10,4},{11,5},{12,6},{13,7},{14,8},{15,9},... | collective-permute-start | bytes 6152 | tf_op jit(solution)/shard_map/ppermute | solution.py:25
  60.4 21.2 %collective-permute-start.13 = (bf16[2,4,128]{2,0,1:T(2,128)(2,1)S(1)}, bf16[2,4,128]{2,0,1:T(2,128)(2,1)S(1)}, u32[]{:S(2)}, u32[]{:S(2)}) collective-permute-start(bf16[2,4,128]{2,0,1:T(2,128)(2,1)S(1)} %pad_maximum_fusion.14), channel_id=1, source_target_pairs={{7,0},{8,1},{9,2},{10,3},{11,4},{12,5},{13,6},{14,7},{15,8},{23,16... | collective-permute-start | bytes 6152 | tf_op jit(solution)/shard_map/ppermute | solution.py:25
  61.8 30.1 %collective-permute-start.28 = (bf16[2,2,32,128]{3,0,2,1:T(2,128)(2,1)S(1)}, bf16[2,2,32,128]{3,0,2,1:T(2,128)(2,1)S(1)}, u32[]{:S(2)}, u32[]{:S(2)}) collective-permute-start(bf16[2,2,32,128]{3,0,2,1:T(2,128)(2,1)S(1)} %pad_maximum_fusion.10), channel_id=1, source_target_pairs={{0,7},{1,8},{2,9},{3,10},{4,11},{5,12},{6,13},{7,14},{8,15},{16,23... | collective-permute-start | bytes 98312 | tf_op jit(solution)/shard_map/ppermute | solution.py:25
  73.2 20.9 %collective-permute-start.29 = (bf16[2,2,32,128]{3,0,2,1:T(2,128)(2,1)S(1)}, bf16[2,2,32,128]{3,0,2,1:T(2,128)(2,1)S(1)}, u32[]{:S(2)}, u32[]{:S(2)}) collective-permute-start(bf16[2,2,32,128]{3,0,2,1:T(2,128)(2,1)S(1)} %pad_maximum_fusion.10), channel_id=1, source_target_pairs={{0,6},{1,7},{2,8},{3,9},{4,10},{5,11},{6,12},{7,13},{8,14},{9,15},... | collective-permute-start | bytes 98312 | tf_op jit(solution)/shard_map/ppermute | solution.py:25
  101.3 22.3 %collective-permute-start.39 = (bf16[2,2,32,128]{3,0,2,1:T(2,128)(2,1)S(1)}, bf16[2,2,32,128]{3,0,2,1:T(2,128)(2,1)S(1)}, u32[]{:S(2)}, u32[]{:S(2)}) collective-permute-start(bf16[2,2,32,128]{3,0,2,1:T(2,128)(2,1)S(1)} %pad_maximum_fusion.10), channel_id=1, source_target_pairs={{5,0},{6,1},{7,2},{8,3},{9,4},{10,5},{11,6},{12,7},{13,8},{14,9},{... | collective-permute-start | bytes 98312 | tf_op jit(solution)/shard_map/ppermute | solution.py:25
  102.7 22.9 %collective-permute-start.40 = (bf16[2,2,32,128]{3,0,2,1:T(2,128)(2,1)S(1)}, bf16[2,2,32,128]{3,0,2,1:T(2,128)(2,1)S(1)}, u32[]{:S(2)}, u32[]{:S(2)}) collective-permute-start(bf16[2,2,32,128]{3,0,2,1:T(2,128)(2,1)S(1)} %pad_maximum_fusion.10), channel_id=1, source_target_pairs={{6,0},{7,1},{8,2},{9,3},{10,4},{11,5},{12,6},{13,7},{14,8},{15,9},... | collective-permute-start | bytes 98312 | tf_op jit(solution)/shard_map/ppermute | solution.py:25
  104.8 22.8 %collective-permute-start.41 = (bf16[2,2,32,128]{3,0,2,1:T(2,128)(2,1)S(1)}, bf16[2,2,32,128]{3,0,2,1:T(2,128)(2,1)S(1)}, u32[]{:S(2)}, u32[]{:S(2)}) collective-permute-start(bf16[2,2,32,128]{3,0,2,1:T(2,128)(2,1)S(1)} %pad_maximum_fusion.10), channel_id=1, source_target_pairs={{7,0},{8,1},{9,2},{10,3},{11,4},{12,5},{13,6},{14,7},{15,8},{23,16... | collective-permute-start | bytes 98312 | tf_op jit(solution)/shard_map/ppermute | solution.py:25
  106.2 43.0 %collective-permute-start.14 = (bf16[2,2,128,128]{3,0,2,1:T(2,128)(2,1)}, bf16[2,2,128,128]{3,0,2,1:T(2,128)(2,1)}, u32[]{:S(2)}, u32[]{:S(2)}) collective-permute-start(bf16[2,2,128,128]{3,0,2,1:T(2,128)(2,1)} %fusion.50), channel_id=1, source_target_pairs={{0,7},{1,8},{2,9},{3,10},{4,11},{5,12},{6,13},{7,14},{8,15},{16,23... | collective-permute-start | bytes 393224 | tf_op jit(solution)/shard_map/ppermute | solution.py:25
  118.1 33.7 %collective-permute-start.15 = (bf16[2,2,128,128]{3,0,2,1:T(2,128)(2,1)}, bf16[2,2,128,128]{3,0,2,1:T(2,128)(2,1)}, u32[]{:S(2)}, u32[]{:S(2)}) collective-permute-start(bf16[2,2,128,128]{3,0,2,1:T(2,128)(2,1)} %fusion.50), channel_id=1, source_target_pairs={{0,6},{1,7},{2,8},{3,9},{4,10},{5,11},{6,12},{7,13},{8,14},{9,15},... | collective-permute-start | bytes 393224 | tf_op jit(solution)/shard_map/ppermute | solution.py:25
  123.6 31.0 %collective-permute-start.16 = (bf16[2,2,128,128]{3,0,2,1:T(2,128)(2,1)}, bf16[2,2,128,128]{3,0,2,1:T(2,128)(2,1)}, u32[]{:S(2)}, u32[]{:S(2)}) collective-permute-start(bf16[2,2,128,128]{3,0,2,1:T(2,128)(2,1)} %fusion.50), channel_id=1, source_target_pairs={{0,5},{1,6},{2,7},{3,8},{4,9},{5,10},{6,11},{7,12},{8,13},{9,14},{... | collective-permute-start | bytes 393224 | tf_op jit(solution)/shard_map/ppermute | solution.py:25
  125.6 31.3 %collective-permute-start.17 = (bf16[2,2,128,128]{3,0,2,1:T(2,128)(2,1)}, bf16[2,2,128,128]{3,0,2,1:T(2,128)(2,1)}, u32[]{:S(2)}, u32[]{:S(2)}) collective-permute-start(bf16[2,2,128,128]{3,0,2,1:T(2,128)(2,1)} %fusion.50), channel_id=1, source_target_pairs={{0,4},{1,5},{2,6},{3,7},{4,8},{5,9},{6,10},{7,11},{8,12},{9,13},{1... | collective-permute-start | bytes 393224 | tf_op jit(solution)/shard_map/ppermute | solution.py:25
  127.6 31.6 %collective-permute-start.18 = (bf16[2,2,128,128]{3,0,2,1:T(2,128)(2,1)}, bf16[2,2,128,128]{3,0,2,1:T(2,128)(2,1)}, u32[]{:S(2)}, u32[]{:S(2)}) collective-permute-start(bf16[2,2,128,128]{3,0,2,1:T(2,128)(2,1)} %fusion.50), channel_id=1, source_target_pairs={{0,3},{1,4},{2,5},{3,6},{4,7},{5,8},{6,9},{7,10},{8,11},{9,12},{10... | collective-permute-start | bytes 393224 | tf_op jit(solution)/shard_map/ppermute | solution.py:25
  410.3 381.6 %collective-permute-start.98 = (bf16[1,2,128,128]{2,3,1,0:T(8,128)(2,1)}, bf16[1,2,128,128]{2,3,1,0:T(8,128)(2,1)}, u32[]{:S(2)}, u32[]{:S(2)}) collective-permute-start(bf16[1,2,128,128]{2,3,1,0:T(8,128)(2,1)} %pad_maximum_fusion.9), channel_id=1, source_target_pairs={{0,7},{1,8},{2,9},{3,10},{4,11},{5,12},{6,13},{7,14},{8,15},{16,23... | collective-permute-start | bytes 196616 | tf_op jit(solution)/shard_map/ppermute | solution.py:25
  416.1 378.4 %collective-permute-start.99 = (bf16[1,2,128,128]{2,3,1,0:T(8,128)(2,1)}, bf16[1,2,128,128]{2,3,1,0:T(8,128)(2,1)}, u32[]{:S(2)}, u32[]{:S(2)}) collective-permute-start(bf16[1,2,128,128]{2,3,1,0:T(8,128)(2,1)} %pad_maximum_fusion.9), channel_id=1, source_target_pairs={{0,6},{1,7},{2,8},{3,9},{4,10},{5,11},{6,12},{7,13},{8,14},{9,15},... | collective-permute-start | bytes 196616 | tf_op jit(solution)/shard_map/ppermute | solution.py:25
  419.2 380.3 %collective-permute-start.100 = (bf16[1,2,128,128]{2,3,1,0:T(8,128)(2,1)}, bf16[1,2,128,128]{2,3,1,0:T(8,128)(2,1)}, u32[]{:S(2)}, u32[]{:S(2)}) collective-permute-start(bf16[1,2,128,128]{2,3,1,0:T(8,128)(2,1)} %pad_maximum_fusion.9), channel_id=1, source_target_pairs={{0,5},{1,6},{2,7},{3,8},{4,9},{5,10},{6,11},{7,12},{8,13},{9,14},{... | collective-permute-start | bytes 196616 | tf_op jit(solution)/shard_map/ppermute | solution.py:25
  421.1 380.6 %collective-permute-start.101 = (bf16[1,2,128,128]{2,3,1,0:T(8,128)(2,1)}, bf16[1,2,128,128]{2,3,1,0:T(8,128)(2,1)}, u32[]{:S(2)}, u32[]{:S(2)}) collective-permute-start(bf16[1,2,128,128]{2,3,1,0:T(8,128)(2,1)} %pad_maximum_fusion.9), channel_id=1, source_target_pairs={{0,4},{1,5},{2,6},{3,7},{4,8},{5,9},{6,10},{7,11},{8,12},{9,13},{1... | collective-permute-start | bytes 196616 | tf_op jit(solution)/shard_map/ppermute | solution.py:25
  434.1 31.1 %collective-permute-start.84 = (bf16[1,4,128]{2,1,0:T(4,128)(2,1)}, bf16[1,4,128]{2,1,0:T(4,128)(2,1)}, u32[]{:S(2)}, u32[]{:S(2)}) collective-permute-start(bf16[1,4,128]{2,1,0:T(4,128)(2,1)} %pad_maximum_fusion.16), channel_id=1, source_target_pairs={{0,7},{1,8},{2,9},{3,10},{4,11},{5,12},{6,13},{7,14},{8,15},{16,23... | collective-permute-start | bytes 3080 | tf_op jit(solution)/shard_map/ppermute | solution.py:25
  780.8 23.1 %collective-permute-start.102 = (bf16[1,2,128,128]{2,3,1,0:T(8,128)(2,1)}, bf16[1,2,128,128]{2,3,1,0:T(8,128)(2,1)S(1)}, u32[]{:S(2)}, u32[]{:S(2)}) collective-permute-start(bf16[1,2,128,128]{2,3,1,0:T(8,128)(2,1)} %pad_maximum_fusion.9), channel_id=1, source_target_pairs={{0,3},{1,4},{2,5},{3,6},{4,7},{5,8},{6,9},{7,10},{8,11},{9,12},{10... | collective-permute-start | bytes 196616 | tf_op jit(solution)/shard_map/ppermute | solution.py:25
  806.5 22.0 %collective-permute-start.109 = (bf16[1,2,128,128]{2,3,1,0:T(8,128)(2,1)}, bf16[1,2,128,128]{2,3,1,0:T(8,128)(2,1)S(1)}, u32[]{:S(2)}, u32[]{:S(2)}) collective-permute-start(bf16[1,2,128,128]{2,3,1,0:T(8,128)(2,1)} %pad_maximum_fusion.9), channel_id=1, source_target_pairs={{5,0},{6,1},{7,2},{8,3},{9,4},{10,5},{11,6},{12,7},{13,8},{14,9},{... | collective-permute-start | bytes 196616 | tf_op jit(solution)/shard_map/ppermute | solution.py:25
  807.9 22.6 %collective-permute-start.110 = (bf16[1,2,128,128]{2,3,1,0:T(8,128)(2,1)}, bf16[1,2,128,128]{2,3,1,0:T(8,128)(2,1)S(1)}, u32[]{:S(2)}, u32[]{:S(2)}) collective-permute-start(bf16[1,2,128,128]{2,3,1,0:T(8,128)(2,1)} %pad_maximum_fusion.9), channel_id=1, source_target_pairs={{6,0},{7,1},{8,2},{9,3},{10,4},{11,5},{12,6},{13,7},{14,8},{15,9},... | collective-permute-start | bytes 196616 | tf_op jit(solution)/shard_map/ppermute | solution.py:25
  809.8 22.6 %collective-permute-start.111 = (bf16[1,2,128,128]{2,3,1,0:T(8,128)(2,1)}, bf16[1,2,128,128]{2,3,1,0:T(8,128)(2,1)S(1)}, u32[]{:S(2)}, u32[]{:S(2)}) collective-permute-start(bf16[1,2,128,128]{2,3,1,0:T(8,128)(2,1)} %pad_maximum_fusion.9), channel_id=1, source_target_pairs={{7,0},{8,1},{9,2},{10,3},{11,4},{12,5},{13,6},{14,7},{15,8},{23,16... | collective-permute-start | bytes 196616 | tf_op jit(solution)/shard_map/ppermute | solution.py:25
  811.9 31.2 %collective-permute-start.56 = (bf16[1,2,128,128]{2,3,1,0:T(8,128)(2,1)}, bf16[1,2,128,128]{2,3,1,0:T(8,128)(2,1)}, u32[]{:S(2)}, u32[]{:S(2)}) collective-permute-start(bf16[1,2,128,128]{2,3,1,0:T(8,128)(2,1)} %pad_maximum_fusion.8), channel_id=1, source_target_pairs={{0,7},{1,8},{2,9},{3,10},{4,11},{5,12},{6,13},{7,14},{8,15},{16,23... | collective-permute-start | bytes 196616 | tf_op jit(solution)/shard_map/ppermute | solution.py:25
  823.1 22.5 %collective-permute-start.57 = (bf16[1,2,128,128]{2,3,1,0:T(8,128)(2,1)}, bf16[1,2,128,128]{2,3,1,0:T(8,128)(2,1)}, u32[]{:S(2)}, u32[]{:S(2)}) collective-permute-start(bf16[1,2,128,128]{2,3,1,0:T(8,128)(2,1)} %pad_maximum_fusion.8), channel_id=1, source_target_pairs={{0,6},{1,7},{2,8},{3,9},{4,10},{5,11},{6,12},{7,13},{8,14},{9,15},... | collective-permute-start | bytes 196616 | tf_op jit(solution)/shard_map/ppermute | solution.py:25
  830.5 19.9 %collective-permute-start.59 = (bf16[1,2,128,128]{2,3,1,0:T(8,128)(2,1)}, bf16[1,2,128,128]{2,3,1,0:T(8,128)(2,1)}, u32[]{:S(2)}, u32[]{:S(2)}) collective-permute-start(bf16[1,2,128,128]{2,3,1,0:T(8,128)(2,1)} %pad_maximum_fusion.8), channel_id=1, source_target_pairs={{0,4},{1,5},{2,6},{3,7},{4,8},{5,9},{6,10},{7,11},{8,12},{9,13},{1... | collective-permute-start | bytes 196616 | tf_op jit(solution)/shard_map/ppermute | solution.py:25
  832.4 20.1 %collective-permute-start.60 = (bf16[1,2,128,128]{2,3,1,0:T(8,128)(2,1)}, bf16[1,2,128,128]{2,3,1,0:T(8,128)(2,1)}, u32[]{:S(2)}, u32[]{:S(2)}) collective-permute-start(bf16[1,2,128,128]{2,3,1,0:T(8,128)(2,1)} %pad_maximum_fusion.8), channel_id=1, source_target_pairs={{0,3},{1,4},{2,5},{3,6},{4,7},{5,8},{6,9},{7,10},{8,11},{9,12},{10... | collective-permute-start | bytes 196616 | tf_op jit(solution)/shard_map/ppermute | solution.py:25
  (125 other events, 1746.0 us)
Sparse Core Ops, SparseCore 0:
  1018.7 93.8 all-reduce.2
where the time goes:
time: 1140 us; the launch traced here: 1120 us
  starting transfers between devices  307 us (27%)
  waiting for transfers between devices  283 us (25%)
  matrix products  267 us (23%)
  local copies, waits for them, and re-layouts  184 us (16%)
  other arithmetic  54.9 us (5%)
  between operations  27.4 us (2%)
    ppermute x126, starting transfers between devices, passed_along(): lax.ppermute(value, axis, [(source, source + steps) for source in range(f...  307 us
    conv_general_dilated x3, matrix products, grouped(): lax.conv_general_dilated(padded[None], kernel, (1, 1), 'VALID', dimension...  252 us
    ppermute x126, waiting for transfers between devices, passed_along(): lax.ppermute(value, axis, [(source, source + steps) for source in range(f...  193 us
    psum x1, waiting for transfers between devices, local(): first_sum, second_sum = lax.psum((first_local, second_local), 'tiles')  90.5 us
    concatenate x3, local copies, waits for them, and re-layouts, assemble(): return jnp.concatenate([top_line[None], middle, bottom_line[None]], 0)  51.3 us
    conv_general_dilated x3, local copies, waits for them, and re-layouts, grouped(): lax.conv_general_dilated(padded[None], kernel, (1, 1), 'VALID', dimension...  49.9 us
    select_n x28, local copies, waits for them, and re-layouts, cycle_pieces(): pieces.append(jnp.where(target >= 0, piece, jnp.zeros_like(piece)))  32.3 us
    unnamed x182, local copies, waits for them, and re-layouts  28.5 us
  transfers between devices with their start and end apart: 127, of which 69 were waited for; matrix products, arithmetic and copies ran while one was open for 11% of the time, Pallas kernels for 0%

commit v1 on v0

v1 whole, which is shorter than its diff:
```python
import functools
import math

import jax
import jax.numpy as jnp
from jax import lax
from jax.experimental import pallas as pl
from jax.experimental.pallas import tpu as pltpu
from jax.sharding import PartitionSpec as P

CUBE = 0.044715
ROOT = math.sqrt(2.0 / math.pi)
VMEM_LIMIT = 56 * 1024 * 1024
SMEM = pl.BlockSpec(memory_space=pltpu.SMEM)
VMEM = pl.BlockSpec(memory_space=pltpu.VMEM)


def shape_of(dims, dtype):
    return jax.ShapeDtypeStruct(dims, dtype)


def partners(me):
    odd = lax.rem(me, 2)
    return me + 1 - 2 * odd, me - 1 + 2 * odd


def gelu_pair(v):
    square = v * v
    t = jnp.tanh(ROOT * v * (1.0 + CUBE * square))
    half = 0.5 * (1.0 + t)
    slope = half + (0.5 * ROOT) * v * (1.0 - t * t) * (1.0 + (3.0 * CUBE) * square)
    return v * half, slope


def pack_kernel(tiles, links, me_ref, *refs):
    blocks, (send, own, on_out, off_out) = refs[:8], refs[8:]
    me = me_ref[0]
    sides = ([], [])
    for f in range(2):
        top, bottom, left, right = blocks[4 * f : 4 * f + 4]
        width = right.shape[1]
        for side, block, first in ((0, left, 0), (1, right, width - 2)):
            values = block[...].astype(jnp.float32)
            pair = jnp.stack([values[:, first + c, :] for c in range(2)], 0).astype(jnp.bfloat16)
            own[side, f] = pair
            sides[side].append(pair)
    left_pair, right_pair = (jnp.stack(side, 0) for side in sides)

    def fill(j, carry):
        send[j] = jnp.where(j > me, right_pair, left_pair)
        return carry

    lax.fori_loop(0, tiles, fill, 0)
    for target, out in zip(partners(me), (on_out, off_out)):
        for f in range(2):
            top, bottom = blocks[4 * f][...], blocks[4 * f + 1][...]
            rows = jnp.where(links[0, 1] == target, bottom, jnp.zeros_like(bottom))
            out[f] = jnp.where(links[0, 0] == target, top, rows)


def pack(tiles, links, me, state, cot):
    rows_n, cols_n, chans = state.shape
    specs = [
        pl.BlockSpec((2, cols_n, chans), lambda i: (0, 0, 0)),
        pl.BlockSpec((2, cols_n, chans), lambda i: (rows_n // 2 - 1, 0, 0)),
        pl.BlockSpec((rows_n, 16, chans), lambda i: (0, 0, 0)),
        pl.BlockSpec((rows_n, 16, chans), lambda i: (0, cols_n // 16 - 1, 0)),
    ]
    return pl.pallas_call(
        functools.partial(pack_kernel, tiles),
        grid=(1,),
        in_specs=[SMEM, SMEM] + specs * 2,
        out_specs=[VMEM] * 4,
        out_shape=[
            shape_of((tiles, 2, 2, rows_n, chans), jnp.bfloat16),
            shape_of((2, 2, 2, rows_n, chans), jnp.bfloat16),
            shape_of((2, 2, cols_n, chans), jnp.bfloat16),
            shape_of((2, 2, cols_n, chans), jnp.bfloat16),
        ],
        compiler_params=pltpu.CompilerParams(vmem_limit_bytes=VMEM_LIMIT),
        name="pack",
    )(links, me, *([state] * 4), *([cot] * 4))


def halo_rows(links, me, on_in, off_in, f):
    found = []
    for link in (0, 1):
        rows = jnp.zeros(on_in.shape[1:], on_in.dtype)
        for source, packet in zip(partners(me), (on_in, off_in)):
            rows = jnp.where(links[0, link] == source, packet[f], rows)
        found.append(rows)
    return found


def same_level(width, chans):
    down = lax.broadcasted_iota(jnp.int32, (chans, chans), 0) // width
    across = lax.broadcasted_iota(jnp.int32, (chans, chans), 1) // width
    return down == across


def diagonal(product, mask, width):
    kept = jnp.where(mask, product, 0.0)
    return sum(kept[at : at + width] for at in range(0, product.shape[0], width))


def thirds(ref, row, values):
    count, cols_n, chans = values.shape
    flat = values.reshape(count * cols_n, chans).astype(jnp.float32)
    left = pltpu.roll(flat, 1, 0).astype(ref.dtype).reshape(values.shape)
    right = pltpu.roll(flat, count * cols_n - 1, 0).astype(ref.dtype).reshape(values.shape)
    ref[pl.ds(row, count), :, 0:chans] = left
    ref[pl.ds(row, count), :, chans : 2 * chans] = values
    ref[pl.ds(row, count), :, 2 * chans : 3 * chans] = right


def windows(ref, starts, count):
    parts = []
    for start in starts:
        rows = ref[pl.ds(start, count)]
        parts.append(rows.reshape(rows.shape[0] * rows.shape[1], rows.shape[2]))
    return jnp.concatenate(parts, 1)


def dot(a, b):
    return jnp.dot(a, b, preferred_element_type=jnp.float32)


def main_kernel(
    chunk, links, me_ref, state, cot, on_in, off_in, first_k, second_k,
    grad, first_acc, second_acc, w_pre, w_back, w_state, s3, c3, acc1, acc2,
):
    me = me_ref[0]
    rows_n, cols_n, chans = state.shape
    width = first_k.shape[2]
    mask = same_level(width, chans)
    for tap in range(9):
        for kernel, plain, turned in ((first_k, w_pre, w_state), (second_k, None, w_back)):
            block = kernel[tap // 3, tap % 3].astype(jnp.float32)
            dense = jnp.where(mask, jnp.concatenate([block] * (chans // width), 0), 0.0)
            if plain is not None:
                plain[pl.ds(tap * chans, chans)] = dense.astype(jnp.bfloat16)
            turned[pl.ds((8 - tap) * chans, chans)] = dense.T.astype(jnp.bfloat16)
    for f, (field, store) in enumerate(((state, s3), (cot, c3))):
        above, below = halo_rows(links, me, on_in, off_in, f)
        thirds(store, 0, above)
        thirds(store, rows_n + 2, below)

        def spread(i, carry, field=field, store=store):
            row = i * chunk
            thirds(store, row + 2, field[pl.ds(row, chunk)])
            return carry

        lax.fori_loop(0, rows_n // chunk, spread, 0)

    def fields(starts, count):
        near_state, near_cot = windows(s3, starts, count), windows(c3, starts, count)
        hidden, slope = gelu_pair(dot(near_state, w_pre[...]))
        return near_state, near_cot, hidden, dot(near_cot, w_back[...]) * slope

    x = lax.rem(lax.broadcasted_iota(jnp.int32, (chunk * cols_n, chans), 0), cols_n)
    inner = (x > 0) & (x < cols_n - 1)
    acc1[...] = jnp.zeros_like(acc1)
    acc2[...] = jnp.zeros_like(acc2)

    def step(i, carry):
        row = i * chunk
        near_state, near_cot, hidden, grads = fields([row + 1 + a for a in range(3)], chunk)
        grads = jnp.where(inner, grads, 0.0).astype(jnp.bfloat16)
        hidden = jnp.where(inner, hidden, 0.0).astype(jnp.bfloat16)
        grad[pl.ds(row + 1, chunk)] = grads.reshape(chunk, cols_n, chans)
        acc1[...] += dot(grads.T, near_state)
        acc2[...] += dot(hidden.T, near_cot)
        return carry

    lax.fori_loop(0, rows_n // chunk, step, 0)
    for link, row, at in ((0, 0, 0), (1, rows_n + 1, rows_n + 1)):
        grads = fields([row + a for a in range(3)], 1)[3]
        grads = jnp.where(links[0, link] >= 0, grads, 0.0)
        grad[at] = grads.astype(jnp.bfloat16)
    for tap in range(9):
        part = slice(tap * chans, (tap + 1) * chans)
        first_acc[tap] = diagonal(acc1[:, part].T, mask, width)
        second_acc[8 - tap] = diagonal(acc2[:, part], mask, width)


def main_part(links, me, state, cot, on_in, off_in, first_k, second_k):
    rows_n, cols_n, chans = state.shape
    width = first_k.shape[2]
    chunk = 4
    flops = 2 * rows_n * cols_n * 9 * chans * chans * 4
    return pl.pallas_call(
        functools.partial(main_kernel, chunk),
        in_specs=[SMEM, SMEM] + [VMEM] * 6,
        out_specs=[VMEM] * 6,
        out_shape=[
            shape_of((rows_n + 2, cols_n, chans), jnp.bfloat16),
            shape_of((9, width, chans), jnp.float32),
            shape_of((9, width, chans), jnp.float32),
            shape_of((9 * chans, chans), jnp.bfloat16),
            shape_of((9 * chans, chans), jnp.bfloat16),
            shape_of((9 * chans, chans), jnp.bfloat16),
        ],
        scratch_shapes=[
            pltpu.VMEM((rows_n + 4, cols_n, 3 * chans), jnp.bfloat16),
            pltpu.VMEM((rows_n + 4, cols_n, 3 * chans), jnp.bfloat16),
            pltpu.VMEM((chans, 9 * chans), jnp.float32),
            pltpu.VMEM((chans, 9 * chans), jnp.float32),
        ],
        compiler_params=pltpu.CompilerParams(vmem_limit_bytes=VMEM_LIMIT),
        cost_estimate=pl.CostEstimate(flops=flops, bytes_accessed=5 << 20, transcendentals=1 << 19),
        name="main",
    )(links, me, state, cot, on_in, off_in, first_k, second_k)


BASE = 16


def edge_kernel(
    links, me_ref, own, received, on_in, off_in, w_pre, w_back, first_acc, second_acc,
    keep, pass_on, edge_grad, store, lhs_s, lhs_c,
):
    me = me_ref[0]
    rows_n, chans = own.shape[3], own.shape[4]
    cols_n = on_in.shape[2]
    width = first_acc.shape[1]
    span = rows_n + 16
    store[...] = jnp.zeros_like(store)
    low, high = pl.ds(BASE - 2, 2), pl.ds(BASE + rows_n, 2)
    for f in range(2):
        rows = halo_rows(links, me, on_in, off_in, f)
        for side, link, over, under in ((0, 2, 4, 6), (1, 3, 5, 7)):
            outer, mine = (0, 2) if side == 0 else (6, 4)

            def sent(entry):
                tile = links[0, entry]
                piece = received[jnp.maximum(tile, 0), f].astype(jnp.float32)
                return jnp.where(tile >= 0, piece, 0.0)

            beside, corner_over, corner_under = sent(link), sent(over), sent(under)
            for c in range(2):
                store[f, mine + c, pl.ds(BASE, rows_n)] = own[side, f, c].astype(jnp.float32)
                store[f, outer + c, pl.ds(BASE, rows_n)] = beside[c]
                store[f, outer + c, low] = corner_over[c, rows_n - 2 : rows_n]
                store[f, outer + c, high] = corner_under[c, 0:2]
            at = 0 if side == 0 else cols_n - 16
            first = 0 if side == 0 else 14
            for where, halo in ((BASE - 2, rows[0]), (BASE + rows_n, rows[1])):
                edge = halo[:, at : at + 16].astype(jnp.float32)
                for r in range(2):
                    for c in range(2):
                        store[f, mine + c, pl.ds(where + r, 1)] = edge[r, first + c : first + c + 1]
        target = (lhs_s, lhs_c)[f]
        for column, base in enumerate((0, 1, 4, 5)):
            for a in range(3):
                for b in range(3):
                    lanes = pl.ds((3 * a + b) * chans, chans)
                    column_in = store.at[f, base + b]
                    target[pl.ds(column * span, rows_n), lanes] = column_in[
                        pl.ds(BASE - 1 + a, rows_n)
                    ].astype(jnp.bfloat16)
                    ends = [column_in[pl.ds(BASE - 2 + a, 8)], column_in[pl.ds(BASE + rows_n - 1 + a, 8)]]
                    target[pl.ds(column * span + rows_n, 16), lanes] = jnp.concatenate(ends, 0).astype(
                        jnp.bfloat16
                    )
    hidden, slope = gelu_pair(dot(lhs_s[...], w_pre[...]))
    grads = dot(lhs_c[...], w_back[...]) * slope
    valid = ((2, 4, 6), (None, 0, 1), (None, 0, 1), (3, 5, 7))
    for column in range(4):
        spans = ((0, rows_n), (rows_n, 8), (rows_n + 8, 8))
        for entry, (start, count) in zip(valid[column], spans):
            start += column * span
            piece = grads[start : start + count]
            if entry is not None:
                piece = jnp.where(links[0, entry] >= 0, piece, 0.0)
            edge_grad[pl.ds(start, count)] = piece.astype(jnp.bfloat16).astype(jnp.float32)

    def inner(values):
        return jnp.concatenate([values[span : span + rows_n], values[2 * span : 2 * span + rows_n]], 0)

    def inner_of(ref):
        return jnp.concatenate([ref[pl.ds(span, rows_n)], ref[pl.ds(2 * span, rows_n)]], 0)

    def over_cells(a, b):
        return lax.dot_general(a, b, (((0,), (0,)), ((), ())), preferred_element_type=jnp.float32)

    mask = same_level(width, chans)
    first_p = over_cells(inner_of(lhs_s), inner(grads).astype(jnp.bfloat16))
    second_p = over_cells(inner(hidden).astype(jnp.bfloat16), inner_of(lhs_c))
    even = lax.rem(me, 2) == 0
    for tap in range(9):
        part = slice(tap * chans, (tap + 1) * chans)
        first = first_acc[tap] + diagonal(first_p[part], mask, width)
        turned = slice((8 - tap) * chans, (9 - tap) * chans)
        second = second_acc[tap] + diagonal(second_p[:, turned], mask, width)
        keep[tap] = jnp.where(even, first, second)
        pass_on[tap] = jnp.where(even, second, first)


def edge_part(links, me, own, received, on_in, off_in, w_pre, w_back, first_acc, second_acc):
    rows_n, chans = own.shape[3:]
    cells = 4 * (rows_n + 16)
    return pl.pallas_call(
        edge_kernel,
        in_specs=[SMEM, SMEM] + [VMEM] * 8,
        out_specs=[VMEM] * 3,
        out_shape=[
            shape_of(first_acc.shape, jnp.float32),
            shape_of(first_acc.shape, jnp.float32),
            shape_of((cells, chans), jnp.float32),
        ],
        scratch_shapes=[
            pltpu.VMEM((2, 8, rows_n + 32, chans), jnp.float32),
            pltpu.VMEM((cells, 9 * chans), jnp.bfloat16),
            pltpu.VMEM((cells, 9 * chans), jnp.bfloat16),
        ],
        compiler_params=pltpu.CompilerParams(vmem_limit_bytes=VMEM_LIMIT),
        cost_estimate=pl.CostEstimate(flops=200 << 20, bytes_accessed=3 << 20, transcendentals=1 << 15),
        name="edge",
    )(links, me, own, received, on_in, off_in, w_pre, w_back, first_acc, second_acc)


def state_kernel(chunk, grad, edge_grad, w_state, cot, out, g3):
    rows_n, cols_n, chans = cot.shape
    span = rows_n + 16
    x = lax.broadcasted_iota(jnp.int32, (cols_n, chans), 0)
    at_left, at_right = x == 0, x == cols_n - 1

    def place(row, at):
        def column(number):
            return edge_grad[pl.ds(number * span + at, 1)]

        values = grad[row].astype(jnp.float32)
        values = jnp.where(at_left, column(1), jnp.where(at_right, column(2), values))
        left = jnp.where(at_left, column(0), pltpu.roll(values, 1, 0))
        right = jnp.where(at_right, column(3), pltpu.roll(values, cols_n - 1, 0))
        g3[row, :, 0:chans] = left.astype(g3.dtype)
        g3[row, :, chans : 2 * chans] = values.astype(g3.dtype)
        g3[row, :, 2 * chans : 3 * chans] = right.astype(g3.dtype)

    def spread(i, carry):
        for r in range(chunk):
            place(i * chunk + r + 1, i * chunk + r)
        return carry

    lax.fori_loop(0, rows_n // chunk, spread, 0)
    place(0, rows_n)
    place(rows_n + 1, rows_n + 8)

    def step(i, carry):
        row = i * chunk
        back = dot(windows(g3, [row + a for a in range(3)], chunk), w_state[...])
        own = cot[pl.ds(row, chunk)].astype(jnp.float32)
        out[pl.ds(row, chunk)] = (own + back.reshape(own.shape)).astype(out.dtype)
        return carry

    lax.fori_loop(0, rows_n // chunk, step, 0)


def state_part(grad, edge_grad, w_state, cot):
    rows_n, cols_n, chans = cot.shape
    return pl.pallas_call(
        functools.partial(state_kernel, 4),
        in_specs=[VMEM] * 4,
        out_specs=VMEM,
        out_shape=shape_of(cot.shape, jnp.bfloat16),
        scratch_shapes=[pltpu.VMEM((rows_n + 2, cols_n, 3 * chans), jnp.bfloat16)],
        compiler_params=pltpu.CompilerParams(vmem_limit_bytes=VMEM_LIMIT),
        cost_estimate=pl.CostEstimate(flops=1200 << 20, bytes_accessed=3 << 20, transcendentals=0),
        name="state",
    )(grad, edge_grad, w_state, cot)


def exchanged(value, tiles, pairs):
    both = [(a, b) for a, b in pairs if a < tiles and b < tiles]
    return lax.ppermute(value, "tiles", both + [(b, a) for a, b in both])


def summed(keep, pass_on, me, tiles, scale):
    even = lax.rem(me, 2) == 0
    if tiles & (tiles - 1):
        first, second = jnp.where(even, keep, pass_on), jnp.where(even, pass_on, keep)
        first, second = lax.psum((first, second), "tiles")
        return first * scale, second * scale
    on_chip = [(t, t + 1) for t in range(0, tiles, 2)]
    total = keep + exchanged(pass_on, tiles, on_chip)
    distance = 2
    while distance < tiles:
        pairs = [(t, t + distance) for t in range(tiles) if not t & distance]
        total = total + exchanged(total, tiles, pairs)
        distance *= 2
    total = total * scale
    other = exchanged(total, tiles, on_chip)
    return jnp.where(even, total, other), jnp.where(even, other, total)


def local(ocean_state, cotangent, first_kernel, second_kernel, neighbours):
    state, cot = ocean_state[0], cotangent[0]
    rows_n, cols_n, chans = state.shape
    tiles = lax.axis_size("tiles")
    index = lax.axis_index("tiles")
    me = jnp.reshape(index, (1,)).astype(jnp.int32)
    send, own, on_out, off_out = pack(tiles, neighbours, me, state, cot)
    received = lax.all_to_all(send, "tiles", 0, 0)
    on_in = exchanged(on_out, tiles, [(t, t + 1) for t in range(0, tiles, 2)])
    off_in = exchanged(off_out, tiles, [(t, t + 1) for t in range(1, tiles, 2)])
    grad, first_acc, second_acc, w_pre, w_back, w_state = main_part(
        neighbours, me, state, cot, on_in, off_in, first_kernel, second_kernel
    )
    keep, pass_on, edge_grad = edge_part(
        neighbours, me, own, received, on_in, off_in, w_pre, w_back, first_acc, second_acc
    )
    state_grad = state_part(grad, edge_grad, w_state, cot)
    scale = 1.0 / math.sqrt(tiles * rows_n * cols_n)
    first, second = summed(keep, pass_on, index, tiles, scale)
    shape = first_kernel.shape
    return state_grad[None], first.reshape(shape), second.reshape(shape)


def solution(mesh):
    placed = (
        P(("groups", "tiles"), None, None, None),
        P(("groups", "tiles"), None, None, None),
        P(),
        P(),
        P("tiles", None),
    )
    return jax.shard_map(
        local,
        mesh=mesh,
        in_specs=placed,
        out_specs=(
            P(("groups", "tiles"), None, None, None),
            P("groups", None, None, None),
            P("groups", None, None, None),
        ),
        check_vma=False,
    )
```

time: 1140 us -> 78.1 us (0.07); the launches traced: 1120 us -> 77.6 us
  starting transfers between devices: 307 us -> 27.8 us
  matrix products: 267 us -> 0 us
  waiting for transfers between devices: 283 us -> 16.2 us
  local copies, waits for them, and re-layouts: 184 us -> 2.06 us
  other arithmetic: 54.9 us -> 1.73 us
  Pallas kernels: 0 us -> 29.2 us
  between operations: 27.4 us -> 0.7 us
    ppermute x126 -> x7, starting transfers between devices: 307 us -> 20.4 us  [exchanged(): return lax.ppermute(value, 'tiles', both + [(b, a) for a, b in both])]
    conv_general_dilated x3 -> x0, matrix products: 252 us -> none  [grouped(): lax.conv_general_dilated(padded[None], kernel, (1, 1), 'VALID', dimension...]
    ppermute x126 -> x7, waiting for transfers between devices: 193 us -> 16.2 us  [exchanged(): return lax.ppermute(value, 'tiles', both + [(b, a) for a, b in both])]
    psum x1 -> x0, waiting for transfers between devices: 90.5 us -> none  [local(): first_sum, second_sum = lax.psum((first_local, second_local), 'tiles')]
    concatenate x3 -> x0, local copies, waits for them, and re-layouts: 51.3 us -> none  [assemble(): return jnp.concatenate([top_line[None], middle, bottom_line[None]], 0)]
    conv_general_dilated x3 -> x0, local copies, waits for them, and re-layouts: 49.9 us -> none  [grouped(): lax.conv_general_dilated(padded[None], kernel, (1, 1), 'VALID', dimension...]
    select_n x28 -> x0, local copies, waits for them, and re-layouts: 32.3 us -> none  [cycle_pieces(): pieces.append(jnp.where(target >= 0, piece, jnp.zeros_like(piece)))]
    pallas_call x0 -> x4, Pallas kernels: none -> 29.2 us  [the longest x1 15.4 us: main_part(): pl.pallas_call(functools.partial(main_kernel, chunk), in_specs=[SMEM, SME...]
  transfers between devices with their start and end apart: 127 -> 8, of which waited for: 69 -> 5; matrix products, arithmetic and copies ran while one was open for 11% -> 0% of each run, Pallas kernels for 0% -> 29%
where the time goes in v1:
time: 78.1 us; the launch traced here: 77.6 us
  Pallas kernels  29.2 us (37%)
  starting transfers between devices  27.8 us (36%)
  waiting for transfers between devices  16.2 us (21%)
  local copies, waits for them, and re-layouts  2.06 us (3%)
  other arithmetic  1.73 us (2%)
    ppermute x7, starting transfers between devices, exchanged(): return lax.ppermute(value, 'tiles', both + [(b, a) for a, b in both])  20.4 us
    ppermute x7, waiting for transfers between devices, exchanged(): return lax.ppermute(value, 'tiles', both + [(b, a) for a, b in both])  16.2 us
    pallas_call x1, Pallas kernels, main_part(): pl.pallas_call(functools.partial(main_kernel, chunk), in_specs=[SMEM, SME...  15.4 us
    all_to_all x1, starting transfers between devices, local(): received = lax.all_to_all(send, 'tiles', 0, 0)  7.39 us
    pallas_call x1, Pallas kernels, state_part(): pl.pallas_call(functools.partial(state_kernel, 4), in_specs=[VMEM] * 4, o...  7.17 us
    pallas_call x1, Pallas kernels, pack(): pl.pallas_call(functools.partial(pack_kernel, tiles), grid=(1,), in_specs...  3.79 us
    pallas_call x1, Pallas kernels, edge_part(): pl.pallas_call(edge_kernel, in_specs=[SMEM, SMEM] + [VMEM] * 8, out_specs...  2.85 us
    unnamed x6, local copies, waits for them, and re-layouts  2.06 us
  transfers between devices with their start and end apart: 8, of which 5 were waited for; matrix products, arithmetic and copies ran while one was open for 0% of the time, Pallas kernels for 29%

profile of v1, /device:TPU:0, one launch (start us, length us, event | category | flops | bytes accessed | tf_op | source)
XLA Modules:
  0.0 77.6 jit_solution(4792086505989344005)
XLA Ops:
  0.6 3.8 %pack.1 = (bf16[16,2,2,32,128]{4,3,2,1,0:T(8,128)(2,1)}, bf16[2,2,2,32,128]{4,3,2,1,0:T(8,128)(2,1)}, bf16[2,2,128,128]{3,2,1,0:T(8,128)(2,1)}, bf16[2,2,128,128]{3,2,1,0:T(8,128)(2,1)}) custom-call(s32[1,8]{1,0:T(1,128)} %links.5, s32[1]{0:T(128)} %bitcast.me_ref, bf16[32,128,128]{2,1,0:T(8,128)(2,1)} %bitcast.6, bf16[32,128,128]{2,1,0:T(8,128)(2,1)} %bitcast.7, ...), custom_call_target="tpu_custom_call" | custom-call | tf_op jit(solution)/shard_map/pack/pallas_call | solution.py:69
  4.4 7.4 %all-to-all-start = ((bf16[16,2,2,32,128]{4,3,2,1,0:T(8,128)(2,1)}), bf16[16,2,2,32,128]{4,3,2,1,0:T(8,128)(2,1)S(1)}, u32[]{:S(2)}, u32[]{:S(2)}) async-start(bf16[16,2,2,32,128]{4,3,2,1,0:T(8,128)(2,1)} %get-tuple-element.20), calls=%async_computation | async-start | bytes 1048576 | tf_op jit(solution)/shard_map/all_to_all | solution.py:403
  11.8 0.4 collective-permute-start
  12.2 0.7 collective-permute-start.1
  12.9 0.5 collective-permute-done.on_in
  13.4 0.0 copy-start.1
  13.4 0.0 collective-permute-done.1.off_in
  13.4 0.6 copy-done.1
  14.1 0.0 copy-start.2
  14.1 0.6 copy-done.2
  14.7 15.4 %main.1 = (bf16[34,128,128]{2,1,0:T(8,128)(2,1)}, f32[9,32,128]{2,1,0:T(8,128)}, f32[9,32,128]{2,1,0:T(8,128)}, bf16[1152,128]{1,0:T(8,128)(2,1)}, bf16[1152,128]{1,0:T(8,128)(2,1)}, /*index=5*/bf16[1152,128]{1,0:T(8,128)(2,1)}) custom-call(s32[1,8]{1,0:T(1,128)} %links.5, s32[1]{0:T(128)} %bitcast.me_ref, bf16[32,128,128]{2,1,0:T(8,128)(2,1)} %bitcast.10, ...), custom_call_target="tpu_custom_call" | custom-call | flops 4831838208 | bytes 5242880 | tf_op jit(solution)/shard_map/main/pallas_call | solution.py:191
  30.1 0.0 all-to-all-done.received
  30.1 0.0 copy-start
  30.1 0.8 %copy-done = bf16[16,2,2,32,128]{4,3,2,1,0:T(8,128)(2,1)} copy-done((bf16[16,2,2,32,128]{4,3,2,1,0:T(8,128)(2,1)}, bf16[16,2,2,32,128]{4,3,2,1,0:T(8,128)(2,1)S(1)}, u32[]{:S(2)}) %copy-start) | copy-done | bytes 524312
  30.9 2.9 %edge.1 = (f32[9,32,128]{2,1,0:T(8,128)}, f32[9,32,128]{2,1,0:T(8,128)}, f32[192,128]{1,0:T(8,128)}) custom-call(s32[1,8]{1,0:T(1,128)} %links.5, s32[1]{0:T(128)} %bitcast.me_ref, bf16[2,2,2,32,128]{4,3,2,1,0:T(8,128)(2,1)} %get-tuple-element.19.own, bf16[16,2,2,32,128]{4,3,2,1,0:T(8,128)(2,1)} %copy-done, bf16[2,2,128,128]{3,2,1,0:T(8,128)(2,1)} %copy-done.1, ...), custom_call_target="tpu_custom_call" | custom-call | flops 209715200 | bytes 3145728 | tf_op jit(solution)/shard_map/edge/pallas_call | solution.py:302
  33.7 6.1 %collective-permute-start.2 = (f32[9,32,128]{2,1,0:T(8,128)}, f32[9,32,128]{2,1,0:T(8,128)S(1)}, u32[]{:S(2)}, u32[]{:S(2)}) collective-permute-start(f32[9,32,128]{2,1,0:T(8,128)} %get-tuple-element.28), channel_id=1, source_target_pairs={{0,1},{2,3},{4,5},{6,7},{8,9},{10,11},{12,13},{14,15},{1,0},{3,2},... | collective-permute-start | bytes 442376 | tf_op jit(solution)/shard_map/ppermute | solution.py:375
  39.8 1.2 %collective-permute-done.2 = f32[9,32,128]{2,1,0:T(8,128)S(1)} collective-permute-done((f32[9,32,128]{2,1,0:T(8,128)}, f32[9,32,128]{2,1,0:T(8,128)S(1)}, u32[]{:S(2)}, u32[]{:S(2)}) %collective-permute-start.2) | collective-permute-done | bytes 147488 | tf_op jit(solution)/shard_map/ppermute | solution.py:375
  41.0 0.9 %add.12 = f32[9,32,128]{2,1,0:T(8,128)S(1)} add(f32[9,32,128]{2,1,0:T(8,128)} %get-tuple-element.27, f32[9,32,128]{2,1,0:T(8,128)S(1)} %collective-permute-done.2) | non-fusion elementwise | flops 36864 | bytes 442368 | tf_op jit(solution)/shard_map/add | solution.py:385
  42.0 4.6 %collective-permute-start.3 = (f32[9,32,128]{2,1,0:T(8,128)S(1)}, f32[9,32,128]{2,1,0:T(8,128)S(1)}, u32[]{:S(2)}, u32[]{:S(2)}) collective-permute-start(f32[9,32,128]{2,1,0:T(8,128)S(1)} %add.12), channel_id=1, source_target_pairs={{0,2},{1,3},{4,6},{5,7},{8,10},{9,11},{12,14},{13,15},{2,0},{3,1},... | collective-permute-start | bytes 442376 | tf_op jit(solution)/shard_map/ppermute | solution.py:375
  46.6 4.4 %collective-permute-done.3 = f32[9,32,128]{2,1,0:T(8,128)S(1)} collective-permute-done((f32[9,32,128]{2,1,0:T(8,128)S(1)}, f32[9,32,128]{2,1,0:T(8,128)S(1)}, u32[]{:S(2)}, u32[]{:S(2)}) %collective-permute-start.3) | collective-permute-done | bytes 147488 | tf_op jit(solution)/shard_map/ppermute | solution.py:375
  51.0 5.7 %collective-permute-start.4 = (f32[9,32,128]{2,1,0:T(8,128)S(1)}, f32[9,32,128]{2,1,0:T(8,128)S(1)}, u32[]{:S(2)}, u32[]{:S(2)}) collective-permute-start(f32[9,32,128]{2,1,0:T(8,128)S(1)} %add.13), channel_id=1, source_target_pairs={{0,4},{1,5},{2,6},{3,7},{8,12},{9,13},{10,14},{11,15},{4,0},{5,1},... | collective-permute-start | bytes 442376 | tf_op jit(solution)/shard_map/ppermute | solution.py:375
  56.7 3.8 %collective-permute-done.4 = f32[9,32,128]{2,1,0:T(8,128)S(1)} collective-permute-done((f32[9,32,128]{2,1,0:T(8,128)S(1)}, f32[9,32,128]{2,1,0:T(8,128)S(1)}, u32[]{:S(2)}, u32[]{:S(2)}) %collective-permute-start.4) | collective-permute-done | bytes 147488 | tf_op jit(solution)/shard_map/ppermute | solution.py:375
  60.5 2.9 %collective-permute-start.5 = (f32[9,32,128]{2,1,0:T(8,128)S(1)}, f32[9,32,128]{2,1,0:T(8,128)S(1)}, u32[]{:S(2)}, u32[]{:S(2)}) collective-permute-start(f32[9,32,128]{2,1,0:T(8,128)S(1)} %add.14), channel_id=1, source_target_pairs={{0,8},{1,9},{2,10},{3,11},{4,12},{5,13},{6,14},{7,15},{8,0},{9,1},... | collective-permute-start | bytes 442376 | tf_op jit(solution)/shard_map/ppermute | solution.py:375
  63.4 6.2 %collective-permute-done.5 = f32[9,32,128]{2,1,0:T(8,128)S(1)} collective-permute-done((f32[9,32,128]{2,1,0:T(8,128)S(1)}, f32[9,32,128]{2,1,0:T(8,128)S(1)}, u32[]{:S(2)}, u32[]{:S(2)}) %collective-permute-start.5) | collective-permute-done | bytes 147488 | tf_op jit(solution)/shard_map/ppermute | solution.py:375
  69.7 0.1 collective-permute-start.6
  69.7 7.2 %state.1 = bf16[32,128,128]{2,1,0:T(8,128)(2,1)} custom-call(bf16[34,128,128]{2,1,0:T(8,128)(2,1)} %get-tuple-element.18.grad, f32[192,128]{1,0:T(8,128)} %get-tuple-element.25.edge_grad, bf16[1152,128]{1,0:T(8,128)(2,1)} %get-tuple-element.26.w_state, bf16[32,128,128]{2,1,0:T(8,128)(2,1)} %bitcast.16), custom_call_target="tpu_custom_call" | custom-call | flops 1258291200 | bytes 3145728 | tf_op jit(solution)/shard_map/state/pallas_call | solution.py:361
  76.9 0.0 collective-permute-done.6
  76.9 0.7 broadcast_select_fusion
  (3 shorter events, 0.1 us)
Async XLA Ops:
  4.4 25.7 %all-to-all-start = ((bf16[16,2,2,32,128]{4,3,2,1,0:T(8,128)(2,1)}), bf16[16,2,2,32,128]{4,3,2,1,0:T(8,128)(2,1)S(1)}, u32[]{:S(2)}, u32[]{:S(2)}) async-start(bf16[16,2,2,32,128]{4,3,2,1,0:T(8,128)(2,1)} %get-tuple-element.20), calls=%async_computation | async-start | bytes 1048576 | tf_op jit(solution)/shard_map/all_to_all | solution.py:403
  11.8 1.6 %collective-permute-start = (bf16[2,2,128,128]{3,2,1,0:T(8,128)(2,1)}, bf16[2,2,128,128]{3,2,1,0:T(8,128)(2,1)S(1)}, u32[]{:S(2)}, u32[]{:S(2)}) collective-permute-start(bf16[2,2,128,128]{3,2,1,0:T(8,128)(2,1)} %get-tuple-element.16), channel_id=1, source_target_pairs={{0,1},{2,3},{4,5},{6,7},{8,9},{10,11},{12,13},{14,15},{1,0},{3,2},... | collective-permute-start | bytes 393224 | tf_op jit(solution)/shard_map/ppermute | solution.py:375
  12.2 1.2 %collective-permute-start.1 = (bf16[2,2,128,128]{3,2,1,0:T(8,128)(2,1)}, bf16[2,2,128,128]{3,2,1,0:T(8,128)(2,1)S(1)}, u32[]{:S(2)}, u32[]{:S(2)}) collective-permute-start(bf16[2,2,128,128]{3,2,1,0:T(8,128)(2,1)} %get-tuple-element.17), channel_id=1, source_target_pairs={{1,2},{3,4},{5,6},{7,8},{9,10},{11,12},{13,14},{2,1},{4,3},{6,5},{... | collective-permute-start | bytes 393224 | tf_op jit(solution)/shard_map/ppermute | solution.py:375
  13.4 0.6 copy-start.1
  14.1 0.6 copy-start.2
  30.1 0.8 %copy-start = (bf16[16,2,2,32,128]{4,3,2,1,0:T(8,128)(2,1)}, bf16[16,2,2,32,128]{4,3,2,1,0:T(8,128)(2,1)S(1)}, u32[]{:S(2)}) copy-start(bf16[16,2,2,32,128]{4,3,2,1,0:T(8,128)(2,1)S(1)} %all-to-all-done.received) | copy-start | bytes 1572868
  33.7 7.3 %collective-permute-start.2 = (f32[9,32,128]{2,1,0:T(8,128)}, f32[9,32,128]{2,1,0:T(8,128)S(1)}, u32[]{:S(2)}, u32[]{:S(2)}) collective-permute-start(f32[9,32,128]{2,1,0:T(8,128)} %get-tuple-element.28), channel_id=1, source_target_pairs={{0,1},{2,3},{4,5},{6,7},{8,9},{10,11},{12,13},{14,15},{1,0},{3,2},... | collective-permute-start | bytes 442376 | tf_op jit(solution)/shard_map/ppermute | solution.py:375
  42.0 9.0 %collective-permute-start.3 = (f32[9,32,128]{2,1,0:T(8,128)S(1)}, f32[9,32,128]{2,1,0:T(8,128)S(1)}, u32[]{:S(2)}, u32[]{:S(2)}) collective-permute-start(f32[9,32,128]{2,1,0:T(8,128)S(1)} %add.12), channel_id=1, source_target_pairs={{0,2},{1,3},{4,6},{5,7},{8,10},{9,11},{12,14},{13,15},{2,0},{3,1},... | collective-permute-start | bytes 442376 | tf_op jit(solution)/shard_map/ppermute | solution.py:375
  51.0 9.5 %collective-permute-start.4 = (f32[9,32,128]{2,1,0:T(8,128)S(1)}, f32[9,32,128]{2,1,0:T(8,128)S(1)}, u32[]{:S(2)}, u32[]{:S(2)}) collective-permute-start(f32[9,32,128]{2,1,0:T(8,128)S(1)} %add.13), channel_id=1, source_target_pairs={{0,4},{1,5},{2,6},{3,7},{8,12},{9,13},{10,14},{11,15},{4,0},{5,1},... | collective-permute-start | bytes 442376 | tf_op jit(solution)/shard_map/ppermute | solution.py:375
  60.5 9.1 %collective-permute-start.5 = (f32[9,32,128]{2,1,0:T(8,128)S(1)}, f32[9,32,128]{2,1,0:T(8,128)S(1)}, u32[]{:S(2)}, u32[]{:S(2)}) collective-permute-start(f32[9,32,128]{2,1,0:T(8,128)S(1)} %add.14), channel_id=1, source_target_pairs={{0,8},{1,9},{2,10},{3,11},{4,12},{5,13},{6,14},{7,15},{8,0},{9,1},... | collective-permute-start | bytes 442376 | tf_op jit(solution)/shard_map/ppermute | solution.py:375
  69.7 7.3 %collective-permute-start.6 = (f32[9,32,128]{2,1,0:T(8,128)S(1)}, f32[9,32,128]{2,1,0:T(8,128)S(1)}, u32[]{:S(2)}, u32[]{:S(2)}) collective-permute-start(f32[9,32,128]{2,1,0:T(8,128)S(1)} %add_multiply_fusion), channel_id=1, source_target_pairs={{0,1},{2,3},{4,5},{6,7},{8,9},{10,11},{12,13},{14,15},{1,0},{3,2},... | collective-permute-start | bytes 442376 | tf_op jit(solution)/shard_map/ppermute | solution.py:375

commit v2 on v1

v2 whole, which is shorter than its diff:
```python
import functools
import math

import jax
import jax.numpy as jnp
from jax import lax
from jax.experimental import pallas as pl
from jax.experimental.pallas import tpu as pltpu
from jax.sharding import PartitionSpec as P

CUBE = 0.044715
ROOT = math.sqrt(2.0 / math.pi)
MIB = 1 << 20
SMEM = pl.BlockSpec(memory_space=pltpu.SMEM)
VMEM = pl.BlockSpec(memory_space=pltpu.VMEM)


def shape_of(dims, dtype):
    return jax.ShapeDtypeStruct(dims, dtype)


def partners(me):
    odd = lax.rem(me, 2)
    return me + 1 - 2 * odd, me - 1 + 2 * odd


def gelu_pair(v):
    square = v * v
    t = jnp.tanh(ROOT * v * (1.0 + CUBE * square))
    half = 0.5 * (1.0 + t)
    slope = half + (0.5 * ROOT) * v * (1.0 - t * t) * (1.0 + (3.0 * CUBE) * square)
    return v * half, slope


def row_kernel(links, me_ref, *refs):
    blocks, outs = refs[:4], refs[4:]
    for target, out in zip(partners(me_ref[0]), outs):
        for f in range(2):
            top, bottom = blocks[2 * f][...], blocks[2 * f + 1][...]
            rows = jnp.where(links[0, 1] == target, bottom, jnp.zeros_like(bottom))
            out[f] = jnp.where(links[0, 0] == target, top, rows)


def pack_rows(links, me, state, cot):
    rows_n, cols_n, chans = state.shape
    specs = [
        pl.BlockSpec((2, cols_n, chans), lambda i: (0, 0, 0)),
        pl.BlockSpec((2, cols_n, chans), lambda i: (rows_n // 2 - 1, 0, 0)),
    ]
    return pl.pallas_call(
        row_kernel,
        grid=(1,),
        in_specs=[SMEM, SMEM] + specs * 2,
        out_specs=[VMEM] * 2,
        out_shape=[shape_of((2, 2, cols_n, chans), jnp.bfloat16)] * 2,
        compiler_params=pltpu.CompilerParams(vmem_limit_bytes=60 * MIB),
        name="pack_rows",
    )(links, me, *([state] * 2), *([cot] * 2))


def column_kernel(tiles, me_ref, after, *refs):
    blocks, (send, own) = refs[:4], refs[4:]
    me = me_ref[0]
    for f in range(2):
        for side, first in ((0, 0), (1, 14)):
            values = blocks[2 * f + side][...].astype(jnp.float32)
            for c in range(2):
                own[side, f, c] = values[:, first + c, :].astype(jnp.bfloat16)
    left, right = own[0], own[1]

    def fill(j, carry):
        send[j] = jnp.where(j > me, right, left)
        return carry

    lax.fori_loop(0, tiles, fill, 0)


def pack_columns(tiles, me, after, state, cot):
    rows_n, cols_n, chans = state.shape
    specs = [
        pl.BlockSpec((rows_n, 16, chans), lambda i: (0, 0, 0)),
        pl.BlockSpec((rows_n, 16, chans), lambda i: (0, cols_n // 16 - 1, 0)),
    ]
    return pl.pallas_call(
        functools.partial(column_kernel, tiles),
        grid=(1,),
        in_specs=[SMEM, pl.BlockSpec(memory_space=pl.ANY)] + specs * 2,
        out_specs=[VMEM] * 2,
        out_shape=[
            shape_of((tiles, 2, 2, rows_n, chans), jnp.bfloat16),
            shape_of((2, 2, 2, rows_n, chans), jnp.bfloat16),
        ],
        compiler_params=pltpu.CompilerParams(vmem_limit_bytes=60 * MIB),
        name="pack_columns",
    )(me, after, *([state] * 2), *([cot] * 2))


def halo_rows(links, me, on_in, off_in, f):
    found = []
    for link in (0, 1):
        rows = jnp.zeros(on_in.shape[1:], on_in.dtype)
        for source, packet in zip(partners(me), (on_in, off_in)):
            rows = jnp.where(links[0, link] == source, packet[f], rows)
        found.append(rows)
    return found


def same_level(width, chans):
    down = lax.broadcasted_iota(jnp.int32, (chans, chans), 0) // width
    across = lax.broadcasted_iota(jnp.int32, (chans, chans), 1) // width
    return down == across


def diagonal(product, mask, width):
    kept = jnp.where(mask, product, 0.0)
    return sum(kept[at : at + width] for at in range(0, product.shape[0], width))


def thirds(ref, row, values):
    count, cols_n, chans = values.shape
    flat = values.reshape(count * cols_n, chans).astype(jnp.float32)
    left = pltpu.roll(flat, 1, 0).astype(ref.dtype)
    right = pltpu.roll(flat, count * cols_n - 1, 0).astype(ref.dtype)
    for part, piece in enumerate((left, values, right)):
        lanes = slice(part * chans, (part + 1) * chans)
        ref[pl.ds(row // 2, count // 2), :, :, lanes] = piece.reshape(count // 2, 2, cols_n, chans)


def windows(ref, pair, count):
    parts = []
    for row in range(4):
        rows = ref[pl.ds(pair + row // 2, count), row % 2]
        parts.append(rows.reshape(count * rows.shape[1], rows.shape[2]))
    return jnp.concatenate(parts, 1)


def dot(a, b):
    return jnp.dot(a, b, preferred_element_type=jnp.float32)


def spans_of(total, most):
    count = pl.cdiv(total, most)
    bounds = [total * i // count for i in range(count + 1)]
    return [(lo, hi - lo) for lo, hi in zip(bounds, bounds[1:])]


def level_blocks(kernel, tap, mask):
    block = kernel[tap // 3, tap % 3].astype(jnp.float32)
    return jnp.where(mask, jnp.concatenate([block] * (mask.shape[0] // block.shape[0]), 0), 0.0)


def fill_paired(ref, kernel, mask, turned):
    chans = mask.shape[0]
    none = jnp.zeros((3 * chans, chans), ref.dtype)
    ref[9 * chans : 12 * chans, 0:chans] = none
    ref[0 : 3 * chans, chans : 2 * chans] = none
    for tap in range(9):
        dense = level_blocks(kernel, tap, mask)
        if turned:
            paired(ref, 8 - tap, dense.T.astype(ref.dtype))
        else:
            paired(ref, tap, dense.astype(ref.dtype))


def paired(ref, tap, dense):
    chans = dense.shape[0]
    for row in range(2):
        ref[pl.ds((tap + 3 * row) * chans, chans), row * chans : (row + 1) * chans] = dense


def main_kernel(
    links, me_ref, state, cot, on_in, off_in, first_k, second_k,
    grad, first_acc, second_acc, w_pre, w_back, s3, c3, acc1, acc2,
):
    me = me_ref[0]
    rows_n, cols_n, chans = state.shape
    width = first_k.shape[2]
    mask = same_level(width, chans)
    fill_paired(w_pre, first_k, mask, False)
    fill_paired(w_back, second_k, mask, True)
    for f, (field, store) in enumerate(((state, s3), (cot, c3))):
        above, below = halo_rows(links, me, on_in, off_in, f)
        thirds(store, 0, above)
        thirds(store, rows_n + 2, below)
        for row, count in spans_of(rows_n // 2, 4):
            thirds(store, 2 * row + 2, field[pl.ds(2 * row, 2 * count)])

    acc1[...] = jnp.zeros_like(acc1)
    acc2[...] = jnp.zeros_like(acc2)
    pairs_n = rows_n // 2 + 1
    for pair, count in spans_of(pairs_n, PAIRS):
        near_state, near_cot = windows(s3, pair, count), windows(c3, pair, count)
        hidden, slope = gelu_pair(dot(near_state, w_pre[...]))
        grads = dot(near_cot, w_back[...]) * slope
        cell = lax.broadcasted_iota(jnp.int32, grads.shape, 0)
        lane = lax.broadcasted_iota(jnp.int32, grads.shape, 1)
        x = lax.rem(cell, cols_n)
        inner = (x > 0) & (x < cols_n - 1)
        if pair == 0:
            outside = (cell < cols_n) & (lane < chans)
            inner = inner & ~outside
            grads = jnp.where(outside & (links[0, 0] < 0), 0.0, grads)
        if pair + count == pairs_n:
            outside = (cell >= (count - 1) * cols_n) & (lane >= chans)
            inner = inner & ~outside
            grads = jnp.where(outside & (links[0, 1] < 0), 0.0, grads)
        for row in range(2):
            piece = grads[:, row * chans : (row + 1) * chans].astype(jnp.bfloat16)
            grad[pl.ds(pair, count), row] = piece.reshape(count, cols_n, chans)
        grads = jnp.where(inner, grads, 0.0).astype(jnp.bfloat16)
        hidden = jnp.where(inner, hidden, 0.0).astype(jnp.bfloat16)
        acc1[...] += dot(grads.T, near_state)
        acc2[...] += dot(hidden.T, near_cot)
    for tap in range(9):
        one, two = (slice((tap + 3 * r) * chans, (tap + 3 * r + 1) * chans) for r in range(2))
        first = acc1[0:chans, one] + acc1[chans : 2 * chans, two]
        second = acc2[0:chans, one] + acc2[chans : 2 * chans, two]
        first_acc[tap] = diagonal(first.T, mask, width)
        second_acc[8 - tap] = diagonal(second, mask, width)


PAIRS = 9


def main_part(links, me, state, cot, on_in, off_in, first_k, second_k):
    rows_n, cols_n, chans = state.shape
    width = first_k.shape[2]
    flops = 2 * rows_n * cols_n * 9 * chans * chans * 4
    return pl.pallas_call(
        main_kernel,
        in_specs=[SMEM, SMEM] + [VMEM] * 6,
        out_specs=[VMEM] * 3,
        out_shape=[
            shape_of((rows_n // 2 + 1, 2, cols_n, chans), jnp.bfloat16),
            shape_of((9, width, chans), jnp.float32),
            shape_of((9, width, chans), jnp.float32),
        ],
        scratch_shapes=[
            pltpu.VMEM((12 * chans, 2 * chans), jnp.bfloat16),
            pltpu.VMEM((12 * chans, 2 * chans), jnp.bfloat16),
            pltpu.VMEM((rows_n // 2 + 2, 2, cols_n, 3 * chans), jnp.bfloat16),
            pltpu.VMEM((rows_n // 2 + 2, 2, cols_n, 3 * chans), jnp.bfloat16),
            pltpu.VMEM((2 * chans, 12 * chans), jnp.float32),
            pltpu.VMEM((2 * chans, 12 * chans), jnp.float32),
        ],
        compiler_params=pltpu.CompilerParams(vmem_limit_bytes=24 * MIB),
        cost_estimate=pl.CostEstimate(flops=20 * flops, bytes_accessed=5 << 20, transcendentals=1 << 19),
        name="main",
    )(links, me, state, cot, on_in, off_in, first_k, second_k)


BASE = 16


def edge_kernel(
    links, me_ref, own, received, on_in, off_in, first_k, second_k, first_acc, second_acc,
    keep, pass_on, edge_grad, store, lhs_s, lhs_c, w_pre, w_back,
):
    me = me_ref[0]
    rows_n, chans = own.shape[3], own.shape[4]
    cols_n = on_in.shape[2]
    width = first_acc.shape[1]
    span = rows_n + 16
    mask = same_level(width, chans)
    for tap in range(9):
        at = slice(tap * chans, (tap + 1) * chans)
        w_pre[at] = level_blocks(first_k, tap, mask).astype(w_pre.dtype)
        w_back[at] = level_blocks(second_k, 8 - tap, mask).T.astype(w_back.dtype)
    store[...] = jnp.zeros_like(store)
    low, high = pl.ds(BASE - 2, 2), pl.ds(BASE + rows_n, 2)
    for f in range(2):
        rows = halo_rows(links, me, on_in, off_in, f)
        for side, link, over, under in ((0, 2, 4, 6), (1, 3, 5, 7)):
            outer, mine = (0, 2) if side == 0 else (6, 4)

            def sent(entry):
                tile = links[0, entry]
                piece = received[jnp.maximum(tile, 0), f].astype(jnp.float32)
                return jnp.where(tile >= 0, piece, 0.0)

            beside, corner_over, corner_under = sent(link), sent(over), sent(under)
            for c in range(2):
                store[f, mine + c, pl.ds(BASE, rows_n)] = own[side, f, c].astype(jnp.float32)
                store[f, outer + c, pl.ds(BASE, rows_n)] = beside[c]
                store[f, outer + c, low] = corner_over[c, rows_n - 2 : rows_n]
                store[f, outer + c, high] = corner_under[c, 0:2]
            at = 0 if side == 0 else cols_n - 16
            first = 0 if side == 0 else 14
            for where, halo in ((BASE - 2, rows[0]), (BASE + rows_n, rows[1])):
                edge = halo[:, at : at + 16].astype(jnp.float32)
                for r in range(2):
                    for c in range(2):
                        store[f, mine + c, pl.ds(where + r, 1)] = edge[r, first + c : first + c + 1]
        target = (lhs_s, lhs_c)[f]
        for column, base in enumerate((0, 1, 4, 5)):
            for a in range(3):
                for b in range(3):
                    lanes = pl.ds((3 * a + b) * chans, chans)
                    column_in = store.at[f, base + b]
                    target[pl.ds(column * span, rows_n), lanes] = column_in[
                        pl.ds(BASE - 1 + a, rows_n)
                    ].astype(jnp.bfloat16)
                    ends = [column_in[pl.ds(BASE - 2 + a, 8)], column_in[pl.ds(BASE + rows_n - 1 + a, 8)]]
                    target[pl.ds(column * span + rows_n, 16), lanes] = jnp.concatenate(ends, 0).astype(
                        jnp.bfloat16
                    )
    hidden, slope = gelu_pair(dot(lhs_s[...], w_pre[...]))
    grads = dot(lhs_c[...], w_back[...]) * slope
    valid = ((2, 4, 6), (None, 0, 1), (None, 0, 1), (3, 5, 7))
    for column in range(4):
        spans = ((0, rows_n), (rows_n, 8), (rows_n + 8, 8))
        for entry, (start, count) in zip(valid[column], spans):
            start += column * span
            piece = grads[start : start + count]
            if entry is not None:
                piece = jnp.where(links[0, entry] >= 0, piece, 0.0)
            edge_grad[pl.ds(start, count)] = piece.astype(jnp.bfloat16).astype(jnp.float32)

    def inner(values):
        return jnp.concatenate([values[span : span + rows_n], values[2 * span : 2 * span + rows_n]], 0)

    def inner_of(ref):
        return jnp.concatenate([ref[pl.ds(span, rows_n)], ref[pl.ds(2 * span, rows_n)]], 0)

    def over_cells(a, b):
        return lax.dot_general(a, b, (((0,), (0,)), ((), ())), preferred_element_type=jnp.float32)

    first_p = over_cells(inner_of(lhs_s), inner(grads).astype(jnp.bfloat16))
    second_p = over_cells(inner(hidden).astype(jnp.bfloat16), inner_of(lhs_c))
    even = lax.rem(me, 2) == 0
    for tap in range(9):
        part = slice(tap * chans, (tap + 1) * chans)
        first = first_acc[tap] + diagonal(first_p[part], mask, width)
        turned = slice((8 - tap) * chans, (9 - tap) * chans)
        second = second_acc[tap] + diagonal(second_p[:, turned], mask, width)
        keep[tap] = jnp.where(even, first, second)
        pass_on[tap] = jnp.where(even, second, first)


def edge_part(links, me, own, received, on_in, off_in, first_k, second_k, first_acc, second_acc):
    rows_n, chans = own.shape[3:]
    cells = 4 * (rows_n + 16)
    return pl.pallas_call(
        edge_kernel,
        in_specs=[SMEM, SMEM] + [VMEM] * 8,
        out_specs=[VMEM] * 3,
        out_shape=[
            shape_of(first_acc.shape, jnp.float32),
            shape_of(first_acc.shape, jnp.float32),
            shape_of((cells, chans), jnp.float32),
        ],
        scratch_shapes=[
            pltpu.VMEM((2, 8, rows_n + 32, chans), jnp.float32),
            pltpu.VMEM((cells, 9 * chans), jnp.bfloat16),
            pltpu.VMEM((cells, 9 * chans), jnp.bfloat16),
            pltpu.VMEM((9 * chans, chans), jnp.bfloat16),
            pltpu.VMEM((9 * chans, chans), jnp.bfloat16),
        ],
        compiler_params=pltpu.CompilerParams(vmem_limit_bytes=8 * MIB),
        cost_estimate=pl.CostEstimate(flops=200 << 20, bytes_accessed=3 << 20, transcendentals=1 << 15),
        name="edge",
    )(links, me, own, received, on_in, off_in, first_k, second_k, first_acc, second_acc)


def state_kernel(grad, edge_grad, first_k, cot, out, g3, w_state):
    rows_n, cols_n, chans = cot.shape
    fill_paired(w_state, first_k, same_level(first_k.shape[2], chans), True)
    span = rows_n + 16
    x = lax.broadcasted_iota(jnp.int32, (cols_n, chans), 0)
    at_left, at_right = x == 0, x == cols_n - 1

    for row in range(rows_n + 2):
        at = rows_n if row == 0 else rows_n + 8 if row == rows_n + 1 else row - 1
        ends = [edge_grad[number * span + at : number * span + at + 1] for number in range(4)]
        values = grad[row // 2, row % 2].astype(jnp.float32)
        values = jnp.where(at_left, ends[1], jnp.where(at_right, ends[2], values))
        left = jnp.where(at_left, ends[0], pltpu.roll(values, 1, 0))
        right = jnp.where(at_right, ends[3], pltpu.roll(values, cols_n - 1, 0))
        for part, piece in enumerate((left, values, right)):
            g3[row // 2, row % 2, :, part * chans : (part + 1) * chans] = piece.astype(g3.dtype)
    for pair, count in spans_of(rows_n // 2, 4):
        back = dot(windows(g3, pair, count), w_state[...])
        for row in range(2):
            piece = back[:, row * chans : (row + 1) * chans].reshape(count, cols_n, chans)
            for k in range(count):
                y = 2 * (pair + k) + row
                out[y] = (cot[y].astype(jnp.float32) + piece[k]).astype(out.dtype)


def state_part(grad, edge_grad, first_k, cot):
    rows_n, cols_n, chans = cot.shape
    return pl.pallas_call(
        state_kernel,
        in_specs=[VMEM] * 4,
        out_specs=VMEM,
        out_shape=shape_of(cot.shape, jnp.bfloat16),
        scratch_shapes=[
            pltpu.VMEM((rows_n // 2 + 1, 2, cols_n, 3 * chans), jnp.bfloat16),
            pltpu.VMEM((12 * chans, 2 * chans), jnp.bfloat16),
        ],
        compiler_params=pltpu.CompilerParams(vmem_limit_bytes=12 * MIB),
        cost_estimate=pl.CostEstimate(flops=1200 << 20, bytes_accessed=3 << 20, transcendentals=0),
        name="state",
    )(grad, edge_grad, first_k, cot)


def exchanged(value, tiles, pairs):
    both = [(a, b) for a, b in pairs if a < tiles and b < tiles]
    return lax.ppermute(value, "tiles", both + [(b, a) for a, b in both])


def summed(keep, pass_on, me, tiles, scale, edges, state_of):
    even = lax.rem(me, 2) == 0
    if tiles & (tiles - 1):
        first, second = jnp.where(even, keep, pass_on), jnp.where(even, pass_on, keep)
        first, second = lax.psum((first, second), "tiles")
        return first * scale, second * scale, state_of(edges)
    on_chip = [(t, t + 1) for t in range(0, tiles, 2)]
    total = keep + exchanged(pass_on, tiles, on_chip)
    distance = 2
    while distance < tiles:
        last = 2 * distance >= tiles
        if last:
            total, edges = lax.optimization_barrier((total, edges))
        other = exchanged(total, tiles, [(t, t + distance) for t in range(tiles) if not t & distance])
        if last:
            other, state_grad = lax.optimization_barrier((other, state_of(edges)))
        total = total + other
        distance *= 2
    total = total * scale
    other = exchanged(total, tiles, on_chip)
    return jnp.where(even, total, other), jnp.where(even, other, total), state_grad


def local(ocean_state, cotangent, first_kernel, second_kernel, neighbours):
    state, cot = ocean_state[0], cotangent[0]
    rows_n, cols_n, chans = state.shape
    tiles = lax.axis_size("tiles")
    index = lax.axis_index("tiles")
    me = jnp.reshape(index, (1,)).astype(jnp.int32)
    on_out, off_out = pack_rows(neighbours, me, state, cot)
    on_in = exchanged(on_out, tiles, [(t, t + 1) for t in range(0, tiles, 2)])
    off_in = exchanged(off_out, tiles, [(t, t + 1) for t in range(1, tiles, 2)])
    send, own = pack_columns(tiles, me, off_out, state, cot)
    received = lax.all_to_all(send, "tiles", 0, 0)
    grad, first_acc, second_acc = main_part(
        neighbours, me, state, cot, on_in, off_in, first_kernel, second_kernel
    )
    keep, pass_on, edge_grad = edge_part(
        neighbours, me, own, received, on_in, off_in, first_kernel, second_kernel, first_acc, second_acc
    )
    scale = 1.0 / math.sqrt(tiles * rows_n * cols_n)

    def state_of(edges):
        return state_part(grad, edges, first_kernel, cot)

    first, second, state_grad = summed(keep, pass_on, index, tiles, scale, edge_grad, state_of)
    shape = first_kernel.shape
    return state_grad[None], first.reshape(shape), second.reshape(shape)


def solution(mesh):
    placed = (
        P(("groups", "tiles"), None, None, None),
        P(("groups", "tiles"), None, None, None),
        P(),
        P(),
        P("tiles", None),
    )
    return jax.shard_map(
        local,
        mesh=mesh,
        in_specs=placed,
        out_specs=(
            P(("groups", "tiles"), None, None, None),
            P("groups", None, None, None),
            P("groups", None, None, None),
        ),
        check_vma=False,
    )
```

time: 78.1 us -> 53.7 us (0.69)
  starting transfers between devices: 27.8 us -> 15.1 us
  Pallas kernels: 29.2 us -> 17.4 us
  waiting for transfers between devices: 16.2 us -> 18.3 us
  local copies, waits for them, and re-layouts: 2.06 us -> 1.04 us
  other arithmetic: 1.73 us -> 0.83 us
    ppermute x7, starting transfers between devices: 20.4 us -> 6.26 us  [exchanged(): return lax.ppermute(value, 'tiles', both + [(b, a) for a, b in both])]
    pallas_call x3 -> x4, Pallas kernels: 26.3 us -> 16.1 us  [the longest x1 9.19 us: main_part(): pl.pallas_call(main_kernel, in_specs=[SMEM, SMEM] + [VMEM] * 6, out_specs...]
    all_to_all x1, waiting for transfers between devices: 0.01 us -> 4.16 us  [local(): received = lax.all_to_all(send, 'tiles', 0, 0)]
    ppermute x7, waiting for transfers between devices: 16.2 us -> 14.1 us  [exchanged(): return lax.ppermute(value, 'tiles', both + [(b, a) for a, b in both])]
    pallas_call x1, Pallas kernels: 2.85 us -> 1.31 us  [edge_part(): pl.pallas_call(edge_kernel, in_specs=[SMEM, SMEM] + [VMEM] * 8, out_specs...]
    all_to_all x1, starting transfers between devices: 7.39 us -> 8.79 us  [local(): received = lax.all_to_all(send, 'tiles', 0, 0)]
    unnamed x6 -> x16, local copies, waits for them, and re-layouts: 2.06 us -> 1.04 us
    add x1, other arithmetic: 0.93 us -> 0.03 us  [summed(): total = keep + exchanged(pass_on, tiles, on_chip)]
  transfers between devices with their start and end apart: 8 -> 8, of which waited for: 5 -> 6; matrix products, arithmetic and copies ran while one was open for 0% -> 0% of each run, Pallas kernels for 29% -> 27%
where the time goes in v2:
time: 53.7 us; the launch traced here: 53.4 us
  waiting for transfers between devices  18.3 us (34%)
  Pallas kernels  17.4 us (32%)
  starting transfers between devices  15.1 us (28%)
  local copies, waits for them, and re-layouts  1.04 us (2%)
  other arithmetic  0.83 us (2%)
  between operations  0.78 us (1%)
    ppermute x7, waiting for transfers between devices, exchanged(): return lax.ppermute(value, 'tiles', both + [(b, a) for a, b in both])  14.1 us
    pallas_call x1, Pallas kernels, main_part(): pl.pallas_call(main_kernel, in_specs=[SMEM, SMEM] + [VMEM] * 6, out_specs...  9.19 us
    all_to_all x1, starting transfers between devices, local(): received = lax.all_to_all(send, 'tiles', 0, 0)  8.79 us
    ppermute x7, starting transfers between devices, exchanged(): return lax.ppermute(value, 'tiles', both + [(b, a) for a, b in both])  6.26 us
    all_to_all x1, waiting for transfers between devices, local(): received = lax.all_to_all(send, 'tiles', 0, 0)  4.16 us
    pallas_call x1, Pallas kernels, state_part(): pl.pallas_call(state_kernel, in_specs=[VMEM] * 4, out_specs=VMEM, out_sha...  3.07 us
    pallas_call x1, Pallas kernels, pack_columns(): pl.pallas_call(functools.partial(column_kernel, tiles), grid=(1,), in_spe...  2.16 us
    pallas_call x1, Pallas kernels, pack_rows(): pl.pallas_call(row_kernel, grid=(1,), in_specs=[SMEM, SMEM] + specs * 2,...  1.7 us
  transfers between devices with their start and end apart: 8, of which 6 were waited for; matrix products, arithmetic and copies ran while one was open for 0% of the time, Pallas kernels for 27%

profile of v2, /device:TPU:0, one launch (start us, length us, event | category | flops | bytes accessed | tf_op | source)
XLA Modules:
  0.0 53.4 jit_solution(11821019019556998060)
XLA Ops:
  0.6 1.7 %pack_rows.1 = (bf16[2,2,128,128]{3,2,1,0:T(8,128)(2,1)}, bf16[2,2,128,128]{3,2,1,0:T(8,128)(2,1)}) custom-call(s32[1,8]{1,0:T(1,128)} %links.5, s32[1]{0:T(128)} %bitcast.me_ref, bf16[32,128,128]{2,1,0:T(8,128)(2,1)} %bitcast.6, bf16[32,128,128]{2,1,0:T(8,128)(2,1)} %bitcast.7, bf16[32,128,128]{2,1,0:T(8,128)(2,1)} %bitcast.11, bf16[32,128,128]{2,1,0:T(8,128)(2,1)} %bitcast.12), custom_call_target="tpu_custom_call" | custom-call | tf_op jit(solution)/shard_map/pack_rows/pallas_call | solution.py:50
  2.3 0.5 collective-permute-start
  2.8 0.0 copy-start.5
  2.8 0.8 %collective-permute-start.1 = (bf16[2,2,128,128]{3,2,1,0:T(8,128)(2,1)}, bf16[2,2,128,128]{3,2,1,0:T(8,128)(2,1)S(1)}, u32[]{:S(2)}, u32[]{:S(2)}) collective-permute-start(bf16[2,2,128,128]{3,2,1,0:T(8,128)(2,1)} %get-tuple-element.17.after), channel_id=1, source_target_pairs={{1,2},{3,4},{5,6},{7,8},{9,10},{11,12},{13,14},{2,1},{4,3},{6,5},{... | collective-permute-start | bytes 393224 | tf_op jit(solution)/shard_map/ppermute | solution.py:409
  3.6 2.2 %pack_columns.1 = (bf16[16,2,2,32,128]{4,3,2,1,0:T(8,128)(2,1)}, bf16[2,2,2,32,128]{4,3,2,1,0:T(8,128)(2,1)}) custom-call(s32[1]{0:T(128)} %bitcast.me_ref, bf16[2,2,128,128]{3,2,1,0:T(8,128)(2,1)} %get-tuple-element.17.after, bf16[32,128,128]{2,1,0:T(8,128)(2,1)} %bitcast.8, bf16[32,128,128]{2,1,0:T(8,128)(2,1)} %bitcast.9, bf16[32,128,128]{2,1,0:T(8,128)(2,1)} %bitcast.13, ...), custom_call_target="tpu_custom_call" | custom-call | tf_op jit(solution)/shard_map/pack_columns/pallas_call | solution.py:84
  5.8 8.8 %all-to-all-start = ((bf16[16,2,2,32,128]{4,3,2,1,0:T(8,128)(2,1)}), bf16[16,2,2,32,128]{4,3,2,1,0:T(8,128)(2,1)S(1)}, u32[]{:S(2)}, u32[]{:S(2)}) async-start(bf16[16,2,2,32,128]{4,3,2,1,0:T(8,128)(2,1)} %get-tuple-element.19), calls=%async_computation | async-start | bytes 1048576 | tf_op jit(solution)/shard_map/all_to_all | solution.py:445
  14.6 0.0 copy-start.4
  14.6 0.0 collective-permute-done.on_in
  14.6 0.0 collective-permute-done.1.off_in
  14.6 0.0 copy-done
  14.6 0.0 copy-done.1
  14.6 0.0 copy-done.2
  14.6 0.0 copy-done.3
  14.7 0.0 copy-done.5
  14.7 9.2 %main.1 = (bf16[17,2,128,128]{3,2,1,0:T(8,128)(2,1)S(1)}, f32[9,32,128]{2,1,0:T(8,128)S(1)}, f32[9,32,128]{2,1,0:T(8,128)S(1)}) custom-call(s32[1,8]{1,0:T(1,128)S(1)} %copy-done.5, s32[1]{0:T(128)} %bitcast.me_ref, bf16[32,128,128]{2,1,0:T(8,128)(2,1)S(1)} %bitcast.10, bf16[32,128,128]{2,1,0:T(8,128)(2,1)S(1)} %bitcast.15, ...), custom_call_target="tpu_custom_call" | custom-call | flops 96636764160 | bytes 5242880 | tf_op jit(solution)/shard_map/main/pallas_call | solution.py:229
  23.9 0.0 copy-start.6
  23.9 1.0 %copy-done.6 = bf16[17,2,128,128]{3,2,1,0:T(8,128)(2,1)} copy-done((bf16[17,2,128,128]{3,2,1,0:T(8,128)(2,1)}, bf16[17,2,128,128]{3,2,1,0:T(8,128)(2,1)S(1)}, u32[]{:S(2)}) %copy-start.6) | copy-done | bytes 1114136
  24.9 4.2 %all-to-all-done.received = bf16[16,2,2,32,128]{4,3,2,1,0:T(8,128)(2,1)S(1)} async-done(((bf16[16,2,2,32,128]{4,3,2,1,0:T(8,128)(2,1)}), bf16[16,2,2,32,128]{4,3,2,1,0:T(8,128)(2,1)S(1)}, u32[]{:S(2)}, u32[]{:S(2)}) %all-to-all-start) | async-done | bytes 524320 | tf_op jit(solution)/shard_map/all_to_all | solution.py:445
  29.1 0.0 copy-done.4
  29.1 1.3 %edge.1 = (f32[9,32,128]{2,1,0:T(8,128)S(1)}, f32[9,32,128]{2,1,0:T(8,128)S(1)}, f32[192,128]{1,0:T(8,128)S(1)}) custom-call(s32[1,8]{1,0:T(1,128)S(1)} %copy-done.5, s32[1]{0:T(128)} %bitcast.me_ref, bf16[2,2,2,32,128]{4,3,2,1,0:T(8,128)(2,1)S(1)} %copy-done.4, bf16[16,2,2,32,128]{4,3,2,1,0:T(8,128)(2,1)S(1)} %all-to-all-done.received, ...), custom_call_target="tpu_custom_call" | custom-call | flops 209715200 | bytes 3145728 | tf_op jit(solution)/shard_map/edge/pallas_call | solution.py:343
  30.4 0.1 collective-permute-start.2
  30.5 1.4 %collective-permute-done.2 = f32[9,32,128]{2,1,0:T(8,128)S(1)} collective-permute-done((f32[9,32,128]{2,1,0:T(8,128)S(1)}, f32[9,32,128]{2,1,0:T(8,128)S(1)}, u32[]{:S(2)}, u32[]{:S(2)}) %collective-permute-start.2) | collective-permute-done | bytes 147488 | tf_op jit(solution)/shard_map/ppermute | solution.py:409
  31.8 0.9 %collective-permute-start.3 = (f32[9,32,128]{2,1,0:T(8,128)S(1)}, f32[9,32,128]{2,1,0:T(8,128)S(1)}, u32[]{:S(2)}, u32[]{:S(2)}) collective-permute-start(f32[9,32,128]{2,1,0:T(8,128)S(1)} %add.12), channel_id=1, source_target_pairs={{0,2},{1,3},{4,6},{5,7},{8,10},{9,11},{12,14},{13,15},{2,0},{3,1},... | collective-permute-start | bytes 442376 | tf_op jit(solution)/shard_map/ppermute | solution.py:409
  32.7 5.1 %collective-permute-done.3 = f32[9,32,128]{2,1,0:T(8,128)S(1)} collective-permute-done((f32[9,32,128]{2,1,0:T(8,128)S(1)}, f32[9,32,128]{2,1,0:T(8,128)S(1)}, u32[]{:S(2)}, u32[]{:S(2)}) %collective-permute-start.3) | collective-permute-done | bytes 147488 | tf_op jit(solution)/shard_map/ppermute | solution.py:409
  37.8 1.7 %collective-permute-start.4 = (f32[9,32,128]{2,1,0:T(8,128)S(1)}, f32[9,32,128]{2,1,0:T(8,128)S(1)}, u32[]{:S(2)}, u32[]{:S(2)}) collective-permute-start(f32[9,32,128]{2,1,0:T(8,128)S(1)} %add.13), channel_id=1, source_target_pairs={{0,4},{1,5},{2,6},{3,7},{8,12},{9,13},{10,14},{11,15},{4,0},{5,1},... | collective-permute-start | bytes 442376 | tf_op jit(solution)/shard_map/ppermute | solution.py:409
  39.5 3.6 %collective-permute-done.4 = f32[9,32,128]{2,1,0:T(8,128)S(1)} collective-permute-done((f32[9,32,128]{2,1,0:T(8,128)S(1)}, f32[9,32,128]{2,1,0:T(8,128)S(1)}, u32[]{:S(2)}, u32[]{:S(2)}) %collective-permute-start.4) | collective-permute-done | bytes 147488 | tf_op jit(solution)/shard_map/ppermute | solution.py:409
  43.1 2.3 %collective-permute-start.5 = (f32[9,32,128]{2,1,0:T(8,128)S(1)}, f32[9,32,128]{2,1,0:T(8,128)S(1)}, u32[]{:S(2)}, u32[]{:S(2)}) collective-permute-start(f32[9,32,128]{2,1,0:T(8,128)S(1)} %add.14), channel_id=1, source_target_pairs={{0,8},{1,9},{2,10},{3,11},{4,12},{5,13},{6,14},{7,15},{8,0},{9,1},... | collective-permute-start | bytes 442376 | tf_op jit(solution)/shard_map/ppermute | solution.py:409
  45.4 3.1 %state.1 = bf16[32,128,128]{2,1,0:T(8,128)(2,1)} custom-call(bf16[17,2,128,128]{3,2,1,0:T(8,128)(2,1)S(1)} %copy-done.7, f32[192,128]{1,0:T(8,128)S(1)} %get-tuple-element.28.edge_grad, bf16[3,3,32,128]{3,2,1,0:T(8,128)(2,1)S(1)} %copy-done.3, bf16[32,128,128]{2,1,0:T(8,128)(2,1)S(1)} %bitcast.16), custom_call_target="tpu_custom_call" | custom-call | flops 1258291200 | bytes 3145728 | tf_op jit(solution)/shard_map/state/pallas_call | solution.py:392
  48.5 2.7 %collective-permute-done.5 = f32[9,32,128]{2,1,0:T(8,128)S(1)} collective-permute-done((f32[9,32,128]{2,1,0:T(8,128)S(1)}, f32[9,32,128]{2,1,0:T(8,128)S(1)}, u32[]{:S(2)}, u32[]{:S(2)}) %collective-permute-start.5) | collective-permute-done | bytes 147488 | tf_op jit(solution)/shard_map/ppermute | solution.py:409
  51.2 0.1 collective-permute-start.6
  51.3 1.4 %collective-permute-done.6 = f32[9,32,128]{2,1,0:T(8,128)S(1)} collective-permute-done((f32[9,32,128]{2,1,0:T(8,128)S(1)}, f32[9,32,128]{2,1,0:T(8,128)S(1)}, u32[]{:S(2)}, u32[]{:S(2)}) %collective-permute-start.6) | collective-permute-done | bytes 147488 | tf_op jit(solution)/shard_map/ppermute | solution.py:409
  52.7 0.7 %broadcast_select_fusion = (f32[9,32,128]{2,1,0:T(8,128)}, f32[9,32,128]{2,1,0:T(8,128)}) fusion(f32[9,32,128]{2,1,0:T(8,128)S(1)} %collective-permute-done.6, f32[9,32,128]{2,1,0:T(8,128)S(1)} %add_multiply_fusion, pred[]{:T(512)S(6)} %eq.3), kind=kLoop, calls=%fused_computation.1 | loop fusion | flops 73728 | bytes 589825 | tf_op jit(solution)/shard_map/jit(_where)/select_n | solution.py:432
  (10 shorter events, 0.1 us)
Async XLA Ops:
  2.3 12.3 %collective-permute-start = (bf16[2,2,128,128]{3,2,1,0:T(8,128)(2,1)}, bf16[2,2,128,128]{3,2,1,0:T(8,128)(2,1)S(1)}, u32[]{:S(2)}, u32[]{:S(2)}) collective-permute-start(bf16[2,2,128,128]{3,2,1,0:T(8,128)(2,1)} %get-tuple-element.20), channel_id=1, source_target_pairs={{0,1},{2,3},{4,5},{6,7},{8,9},{10,11},{12,13},{14,15},{1,0},{3,2},... | collective-permute-start | bytes 393224 | tf_op jit(solution)/shard_map/ppermute | solution.py:409
  2.8 11.8 %copy-start = (bf16[1,32,128,128]{3,2,1,0:T(8,128)(2,1)S(1)}, bf16[1,32,128,128]{3,2,1,0:T(8,128)(2,1)}, u32[]{:S(2)}) copy-start(bf16[1,32,128,128]{3,2,1,0:T(8,128)(2,1)} %param.5) | copy-start | bytes 3145732
  2.8 11.8 %copy-start.1 = (bf16[1,32,128,128]{3,2,1,0:T(8,128)(2,1)S(1)}, bf16[1,32,128,128]{3,2,1,0:T(8,128)(2,1)}, u32[]{:S(2)}) copy-start(bf16[1,32,128,128]{3,2,1,0:T(8,128)(2,1)} %param.6) | copy-start | bytes 3145732
  2.8 11.8 %copy-start.2 = (bf16[3,3,32,128]{3,2,1,0:T(8,128)(2,1)S(1)}, bf16[3,3,32,128]{3,2,1,0:T(8,128)(2,1)}, u32[]{:S(2)}) copy-start(bf16[3,3,32,128]{3,2,1,0:T(8,128)(2,1)} %second_k.3) | copy-start | bytes 221188
  2.8 11.8 %copy-start.3 = (bf16[3,3,32,128]{3,2,1,0:T(8,128)(2,1)S(1)}, bf16[3,3,32,128]{3,2,1,0:T(8,128)(2,1)}, u32[]{:S(2)}) copy-start(bf16[3,3,32,128]{3,2,1,0:T(8,128)(2,1)} %first_k.5) | copy-start | bytes 221188
  2.8 11.9 %copy-start.5 = (s32[1,8]{1,0:T(1,128)S(1)}, s32[1,8]{1,0:T(1,128)}, u32[]{:S(2)}) copy-start(s32[1,8]{1,0:T(1,128)} %links.5) | copy-start | bytes 100
  2.8 11.8 %collective-permute-start.1 = (bf16[2,2,128,128]{3,2,1,0:T(8,128)(2,1)}, bf16[2,2,128,128]{3,2,1,0:T(8,128)(2,1)S(1)}, u32[]{:S(2)}, u32[]{:S(2)}) collective-permute-start(bf16[2,2,128,128]{3,2,1,0:T(8,128)(2,1)} %get-tuple-element.17.after), channel_id=1, source_target_pairs={{1,2},{3,4},{5,6},{7,8},{9,10},{11,12},{13,14},{2,1},{4,3},{6,5},{... | collective-permute-start | bytes 393224 | tf_op jit(solution)/shard_map/ppermute | solution.py:409
  5.8 23.3 %all-to-all-start = ((bf16[16,2,2,32,128]{4,3,2,1,0:T(8,128)(2,1)}), bf16[16,2,2,32,128]{4,3,2,1,0:T(8,128)(2,1)S(1)}, u32[]{:S(2)}, u32[]{:S(2)}) async-start(bf16[16,2,2,32,128]{4,3,2,1,0:T(8,128)(2,1)} %get-tuple-element.19), calls=%async_computation | async-start | bytes 1048576 | tf_op jit(solution)/shard_map/all_to_all | solution.py:445
  14.6 14.5 %copy-start.4 = (bf16[2,2,2,32,128]{4,3,2,1,0:T(8,128)(2,1)S(1)}, bf16[2,2,2,32,128]{4,3,2,1,0:T(8,128)(2,1)}, u32[]{:S(2)}) copy-start(bf16[2,2,2,32,128]{4,3,2,1,0:T(8,128)(2,1)} %get-tuple-element.18.own) | copy-start | bytes 196612
  23.9 1.0 %copy-start.6 = (bf16[17,2,128,128]{3,2,1,0:T(8,128)(2,1)}, bf16[17,2,128,128]{3,2,1,0:T(8,128)(2,1)S(1)}, u32[]{:S(2)}) copy-start(bf16[17,2,128,128]{3,2,1,0:T(8,128)(2,1)S(1)} %get-tuple-element.27.grad) | copy-start | bytes 3342340
  29.1 16.3 %copy-start.7 = (bf16[17,2,128,128]{3,2,1,0:T(8,128)(2,1)S(1)}, bf16[17,2,128,128]{3,2,1,0:T(8,128)(2,1)}, u32[]{:S(2)}) copy-start(bf16[17,2,128,128]{3,2,1,0:T(8,128)(2,1)} %copy-done.6) | copy-start | bytes 3342340
  30.4 1.4 %collective-permute-start.2 = (f32[9,32,128]{2,1,0:T(8,128)S(1)}, f32[9,32,128]{2,1,0:T(8,128)S(1)}, u32[]{:S(2)}, u32[]{:S(2)}) collective-permute-start(f32[9,32,128]{2,1,0:T(8,128)S(1)} %get-tuple-element.24), channel_id=1, source_target_pairs={{0,1},{2,3},{4,5},{6,7},{8,9},{10,11},{12,13},{14,15},{1,0},{3,2},... | collective-permute-start | bytes 442376 | tf_op jit(solution)/shard_map/ppermute | solution.py:409
  31.8 6.0 %collective-permute-start.3 = (f32[9,32,128]{2,1,0:T(8,128)S(1)}, f32[9,32,128]{2,1,0:T(8,128)S(1)}, u32[]{:S(2)}, u32[]{:S(2)}) collective-permute-start(f32[9,32,128]{2,1,0:T(8,128)S(1)} %add.12), channel_id=1, source_target_pairs={{0,2},{1,3},{4,6},{5,7},{8,10},{9,11},{12,14},{13,15},{2,0},{3,1},... | collective-permute-start | bytes 442376 | tf_op jit(solution)/shard_map/ppermute | solution.py:409
  37.8 5.2 %collective-permute-start.4 = (f32[9,32,128]{2,1,0:T(8,128)S(1)}, f32[9,32,128]{2,1,0:T(8,128)S(1)}, u32[]{:S(2)}, u32[]{:S(2)}) collective-permute-start(f32[9,32,128]{2,1,0:T(8,128)S(1)} %add.13), channel_id=1, source_target_pairs={{0,4},{1,5},{2,6},{3,7},{8,12},{9,13},{10,14},{11,15},{4,0},{5,1},... | collective-permute-start | bytes 442376 | tf_op jit(solution)/shard_map/ppermute | solution.py:409
  43.1 8.1 %collective-permute-start.5 = (f32[9,32,128]{2,1,0:T(8,128)S(1)}, f32[9,32,128]{2,1,0:T(8,128)S(1)}, u32[]{:S(2)}, u32[]{:S(2)}) collective-permute-start(f32[9,32,128]{2,1,0:T(8,128)S(1)} %add.14), channel_id=1, source_target_pairs={{0,8},{1,9},{2,10},{3,11},{4,12},{5,13},{6,14},{7,15},{8,0},{9,1},... | collective-permute-start | bytes 442376 | tf_op jit(solution)/shard_map/ppermute | solution.py:409
  51.2 1.4 %collective-permute-start.6 = (f32[9,32,128]{2,1,0:T(8,128)S(1)}, f32[9,32,128]{2,1,0:T(8,128)S(1)}, u32[]{:S(2)}, u32[]{:S(2)}) collective-permute-start(f32[9,32,128]{2,1,0:T(8,128)S(1)} %add_multiply_fusion), channel_id=1, source_target_pairs={{0,1},{2,3},{4,5},{6,7},{8,9},{10,11},{12,13},{14,15},{1,0},{3,2},... | collective-permute-start | bytes 442376 | tf_op jit(solution)/shard_map/ppermute | solution.py:409

commit v3 on v2

--- a/solution.py
+++ b/solution.py
@@ -32,75 +32,79 @@
     return v * half, slope
 
 
-def row_kernel(links, me_ref, *refs):
-    blocks, outs = refs[:4], refs[4:]
-    for target, out in zip(partners(me_ref[0]), outs):
+def pack_kernel(links, me_ref, *refs):
+    blocks, (own, on_out, off_out) = refs[:8], refs[8:]
+    me = me_ref[0]
+    for f in range(2):
+        for side, first in ((0, 0), (1, 14)):
+            values = blocks[4 * f + 2 + side][...].astype(jnp.float32)
+            for c in range(2):
+                own[side, f, c] = values[:, first + c, :].astype(jnp.bfloat16)
+    odd = lax.rem(me, 2) == 1
+    other = jnp.where(odd, own[:, 0], own[:, 1])
+    on_out[4] = other.reshape(on_out.shape[1:])
+    for target, out in zip(partners(me), (on_out, off_out)):
         for f in range(2):
-            top, bottom = blocks[2 * f][...], blocks[2 * f + 1][...]
+            top, bottom = blocks[4 * f][...], blocks[4 * f + 1][...]
             rows = jnp.where(links[0, 1] == target, bottom, jnp.zeros_like(bottom))
-            out[f] = jnp.where(links[0, 0] == target, top, rows)
-
-
-def pack_rows(links, me, state, cot):
+            out[2 * f : 2 * f + 2] = jnp.where(links[0, 0] == target, top, rows)
+
+
+def pack(links, me, state, cot):
     rows_n, cols_n, chans = state.shape
     specs = [
         pl.BlockSpec((2, cols_n, chans), lambda i: (0, 0, 0)),
         pl.BlockSpec((2, cols_n, chans), lambda i: (rows_n // 2 - 1, 0, 0)),
-    ]
-    return pl.pallas_call(
-        row_kernel,
-        grid=(1,),
-        in_specs=[SMEM, SMEM] + specs * 2,
-        out_specs=[VMEM] * 2,
-        out_shape=[shape_of((2, 2, cols_n, chans), jnp.bfloat16)] * 2,
-        compiler_params=pltpu.CompilerParams(vmem_limit_bytes=60 * MIB),
-        name="pack_rows",
-    )(links, me, *([state] * 2), *([cot] * 2))
-
-
-def column_kernel(tiles, me_ref, after, *refs):
-    blocks, (send, own) = refs[:4], refs[4:]
-    me = me_ref[0]
-    for f in range(2):
-        for side, first in ((0, 0), (1, 14)):
-            values = blocks[2 * f + side][...].astype(jnp.float32)
-            for c in range(2):
-                own[side, f, c] = values[:, first + c, :].astype(jnp.bfloat16)
-    left, right = own[0], own[1]
-
-    def fill(j, carry):
-        send[j] = jnp.where(j > me, right, left)
-        return carry
-
-    lax.fori_loop(0, tiles, fill, 0)
-
-
-def pack_columns(tiles, me, after, state, cot):
-    rows_n, cols_n, chans = state.shape
-    specs = [
         pl.BlockSpec((rows_n, 16, chans), lambda i: (0, 0, 0)),
         pl.BlockSpec((rows_n, 16, chans), lambda i: (0, cols_n // 16 - 1, 0)),
     ]
     return pl.pallas_call(
-        functools.partial(column_kernel, tiles),
+        pack_kernel,
         grid=(1,),
-        in_specs=[SMEM, pl.BlockSpec(memory_space=pl.ANY)] + specs * 2,
-        out_specs=[VMEM] * 2,
+        in_specs=[SMEM, SMEM] + specs * 2,
+        out_specs=[VMEM] * 3,
         out_shape=[
-            shape_of((tiles, 2, 2, rows_n, chans), jnp.bfloat16),
             shape_of((2, 2, 2, rows_n, chans), jnp.bfloat16),
+            shape_of((5, 4 * rows_n, chans), jnp.bfloat16),
+            shape_of((4, cols_n, chans), jnp.bfloat16),
         ],
         compiler_params=pltpu.CompilerParams(vmem_limit_bytes=60 * MIB),
-        name="pack_columns",
-    )(me, after, *([state] * 2), *([cot] * 2))
+        name="pack",
+    )(links, me, *([state] * 4), *([cot] * 4))
+
+
+def slot_kernel(chips, me_ref, own, on_in, send):
+    me = me_ref[0]
+    chip, odd = me // 2, lax.rem(me, 2) == 1
+    mine = jnp.where(odd, own[:, 1], own[:, 0])
+    other = on_in[4].reshape(mine.shape)
+    low, high = jnp.where(odd, other, mine), jnp.where(odd, mine, other)
+
+    def fill(j, carry):
+        send[j, 0] = jnp.where(j >= chip, low[1], low[0])
+        send[j, 1] = jnp.where(j > chip, high[1], high[0])
+        return carry
+
+    lax.fori_loop(0, chips, fill, 0)
+
+
+def slots(chips, me, own, on_in):
+    return pl.pallas_call(
+        functools.partial(slot_kernel, chips),
+        in_specs=[SMEM] + [VMEM] * 2,
+        out_specs=VMEM,
+        out_shape=shape_of((chips, 2) + own.shape[2:], jnp.bfloat16),
+        compiler_params=pltpu.CompilerParams(vmem_limit_bytes=24 * MIB),
+        name="slots",
+    )(me, own, on_in)
 
 
 def halo_rows(links, me, on_in, off_in, f):
     found = []
     for link in (0, 1):
-        rows = jnp.zeros(on_in.shape[1:], on_in.dtype)
+        rows = jnp.zeros((2,) + off_in.shape[1:], off_in.dtype)
         for source, packet in zip(partners(me), (on_in, off_in)):
-            rows = jnp.where(links[0, link] == source, packet[f], rows)
+            rows = jnp.where(links[0, link] == source, packet[2 * f : 2 * f + 2], rows)
         found.append(rows)
     return found
 
@@ -170,7 +174,8 @@
 
 def main_kernel(
     links, me_ref, state, cot, on_in, off_in, first_k, second_k,
-    grad, first_acc, second_acc, w_pre, w_back, s3, c3, acc1, acc2,
+    grad, first_acc, second_acc,
+    w_pre, w_back, s3, c3, acc1, acc2, grad_v, sem,
 ):
     me = me_ref[0]
     rows_n, cols_n, chans = state.shape
@@ -188,7 +193,8 @@
     acc1[...] = jnp.zeros_like(acc1)
     acc2[...] = jnp.zeros_like(acc2)
     pairs_n = rows_n // 2 + 1
-    for pair, count in spans_of(pairs_n, PAIRS):
+    copies = []
+    for k, (pair, count) in enumerate(spans_of(pairs_n, PAIRS)):
         near_state, near_cot = windows(s3, pair, count), windows(c3, pair, count)
         hidden, slope = gelu_pair(dot(near_state, w_pre[...]))
         grads = dot(near_cot, w_back[...]) * slope
@@ -206,7 +212,10 @@
             grads = jnp.where(outside & (links[0, 1] < 0), 0.0, grads)
         for row in range(2):
             piece = grads[:, row * chans : (row + 1) * chans].astype(jnp.bfloat16)
-            grad[pl.ds(pair, count), row] = piece.reshape(count, cols_n, chans)
+            grad_v[pl.ds(pair, count), row] = piece.reshape(count, cols_n, chans)
+        part = pl.ds(pair, count)
+        copies.append(pltpu.make_async_copy(grad_v.at[part], grad.at[part], sem.at[k]))
+        copies[-1].start()
         grads = jnp.where(inner, grads, 0.0).astype(jnp.bfloat16)
         hidden = jnp.where(inner, hidden, 0.0).astype(jnp.bfloat16)
         acc1[...] += dot(grads.T, near_state)
@@ -217,6 +226,8 @@
         second = acc2[0:chans, one] + acc2[chans : 2 * chans, two]
         first_acc[tap] = diagonal(first.T, mask, width)
         second_acc[8 - tap] = diagonal(second, mask, width)
+    for copy in copies:
+        copy.wait()
 
 
 PAIRS = 9
@@ -229,9 +240,9 @@
     return pl.pallas_call(
         main_kernel,
         in_specs=[SMEM, SMEM] + [VMEM] * 6,
-        out_specs=[VMEM] * 3,
+        out_specs=[pl.BlockSpec(memory_space=pltpu.HBM), VMEM, VMEM],
         out_shape=[
-            shape_of((rows_n // 2 + 1, 2, cols_n, chans), jnp.bfloat16),
+            pltpu.HBM((rows_n // 2 + 1, 2, cols_n, chans), jnp.bfloat16),
             shape_of((9, width, chans), jnp.float32),
             shape_of((9, width, chans), jnp.float32),
         ],
@@ -242,8 +253,10 @@
             pltpu.VMEM((rows_n // 2 + 2, 2, cols_n, 3 * chans), jnp.bfloat16),
             pltpu.VMEM((2 * chans, 12 * chans), jnp.float32),
             pltpu.VMEM((2 * chans, 12 * chans), jnp.float32),
+            pltpu.VMEM((rows_n // 2 + 1, 2, cols_n, chans), jnp.bfloat16),
+            pltpu.SemaphoreType.DMA((len(spans_of(rows_n // 2 + 1, PAIRS)),)),
         ],
-        compiler_params=pltpu.CompilerParams(vmem_limit_bytes=24 * MIB),
+        compiler_params=pltpu.CompilerParams(vmem_limit_bytes=26 * MIB),
         cost_estimate=pl.CostEstimate(flops=20 * flops, bytes_accessed=5 << 20, transcendentals=1 << 19),
         name="main",
     )(links, me, state, cot, on_in, off_in, first_k, second_k)
@@ -253,12 +266,13 @@
 
 
 def edge_kernel(
-    links, me_ref, own, received, on_in, off_in, first_k, second_k, first_acc, second_acc,
+    links, me_ref, own, received, other_in, on_in, off_in, first_k, second_k, first_acc, second_acc,
     keep, pass_on, edge_grad, store, lhs_s, lhs_c, w_pre, w_back,
 ):
     me = me_ref[0]
     rows_n, chans = own.shape[3], own.shape[4]
-    cols_n = on_in.shape[2]
+    cols_n = off_in.shape[1]
+    odd = lax.rem(me, 2) == 1
     width = first_acc.shape[1]
     span = rows_n + 16
     mask = same_level(width, chans)
@@ -275,7 +289,9 @@
 
             def sent(entry):
                 tile = links[0, entry]
-                piece = received[jnp.maximum(tile, 0), f].astype(jnp.float32)
+                at = jnp.maximum(tile, 0)
+                pieces = (received[at], other_in[at])[:: 1 - 2 * f]
+                piece = jnp.where(odd, pieces[1], pieces[0]).astype(jnp.float32)
                 return jnp.where(tile >= 0, piece, 0.0)
 
             beside, corner_over, corner_under = sent(link), sent(over), sent(under)
@@ -337,12 +353,12 @@
         pass_on[tap] = jnp.where(even, second, first)
 
 
-def edge_part(links, me, own, received, on_in, off_in, first_k, second_k, first_acc, second_acc):
+def edge_part(links, me, own, received, other_in, on_in, off_in, first_k, second_k, first_acc, second_acc):
     rows_n, chans = own.shape[3:]
     cells = 4 * (rows_n + 16)
     return pl.pallas_call(
         edge_kernel,
-        in_specs=[SMEM, SMEM] + [VMEM] * 8,
+        in_specs=[SMEM, SMEM] + [VMEM] * 9,
         out_specs=[VMEM] * 3,
         out_shape=[
             shape_of(first_acc.shape, jnp.float32),
@@ -359,7 +375,7 @@
         compiler_params=pltpu.CompilerParams(vmem_limit_bytes=8 * MIB),
         cost_estimate=pl.CostEstimate(flops=200 << 20, bytes_accessed=3 << 20, transcendentals=1 << 15),
         name="edge",
-    )(links, me, own, received, on_in, off_in, first_k, second_k, first_acc, second_acc)
+    )(links, me, own, received, other_in, on_in, off_in, first_k, second_k, first_acc, second_acc)
 
 
 def state_kernel(grad, edge_grad, first_k, cot, out, g3, w_state):
@@ -438,16 +454,21 @@
     tiles = lax.axis_size("tiles")
     index = lax.axis_index("tiles")
     me = jnp.reshape(index, (1,)).astype(jnp.int32)
-    on_out, off_out = pack_rows(neighbours, me, state, cot)
-    on_in = exchanged(on_out, tiles, [(t, t + 1) for t in range(0, tiles, 2)])
+    own, on_out, off_out = pack(neighbours, me, state, cot)
+    on_chip = [(t, t + 1) for t in range(0, tiles, 2)]
+    on_in = exchanged(on_out, tiles, on_chip)
     off_in = exchanged(off_out, tiles, [(t, t + 1) for t in range(1, tiles, 2)])
-    send, own = pack_columns(tiles, me, off_out, state, cot)
-    received = lax.all_to_all(send, "tiles", 0, 0)
+    cores = [list(range(core, tiles, 2)) for core in range(2)]
+    sent = slots(tiles // 2, me, own, on_in)
+    received = lax.all_to_all(sent, "tiles", 0, 0, axis_index_groups=cores)
+    received = received.reshape((tiles,) + received.shape[2:])
     grad, first_acc, second_acc = main_part(
         neighbours, me, state, cot, on_in, off_in, first_kernel, second_kernel
     )
+    received, first_acc = lax.optimization_barrier((received, first_acc))
+    other_in = exchanged(received, tiles, on_chip)
     keep, pass_on, edge_grad = edge_part(
-        neighbours, me, own, received, on_in, off_in, first_kernel, second_kernel, first_acc, second_acc
+        neighbours, me, own, received, other_in, on_in, off_in, first_kernel, second_kernel, first_acc, second_acc
     )
     scale = 1.0 / math.sqrt(tiles * rows_n * cols_n)
 

time: 53.7 us -> 50.9 us (0.948)
  waiting for transfers between devices: 18.3 us -> 15.6 us
  starting transfers between devices: 15.1 us -> 15.9 us
  Pallas kernels: 17.4 us -> 16.6 us
    all_to_all x1, waiting for transfers between devices: 4.16 us -> 0.01 us  [local(): received = lax.all_to_all(sent, 'tiles', 0, 0, axis_index_groups=cores)]
    ppermute x7 -> x8, starting transfers between devices: 6.26 us -> 7.81 us  [exchanged(): return lax.ppermute(value, 'tiles', both + [(b, a) for a, b in both])]
    ppermute x7 -> x8, waiting for transfers between devices: 14.1 us -> 15.6 us  [exchanged(): return lax.ppermute(value, 'tiles', both + [(b, a) for a, b in both])]
    pallas_call x3, Pallas kernels: 5.18 us -> 4.33 us  [the longest x1 2.23 us: pack(): pl.pallas_call(pack_kernel, grid=(1,), in_specs=[SMEM, SMEM] + specs * 2,...]
    all_to_all x1, starting transfers between devices: 8.79 us -> 8.13 us  [local(): received = lax.all_to_all(sent, 'tiles', 0, 0, axis_index_groups=cores)]
  transfers between devices with their start and end apart: 8 -> 9, of which waited for: 6 -> 7; matrix products, arithmetic and copies ran while one was open for 0% -> 0% of each run, Pallas kernels for 27% -> 26%
where the time goes in v3:
time: 50.9 us; the launch traced here: 50.6 us
  Pallas kernels  16.6 us (33%)
  starting transfers between devices  15.9 us (31%)
  waiting for transfers between devices  15.6 us (31%)
  local copies, waits for them, and re-layouts  0.87 us (2%)
  other arithmetic  0.82 us (2%)
  between operations  0.8 us (2%)
    ppermute x8, waiting for transfers between devices, exchanged(): return lax.ppermute(value, 'tiles', both + [(b, a) for a, b in both])  15.6 us
    pallas_call x1, Pallas kernels, main_part(): pl.pallas_call(main_kernel, in_specs=[SMEM, SMEM] + [VMEM] * 6, out_specs...  9.2 us
    all_to_all x1, starting transfers between devices, local(): received = lax.all_to_all(sent, 'tiles', 0, 0, axis_index_groups=cores)  8.13 us
    ppermute x8, starting transfers between devices, exchanged(): return lax.ppermute(value, 'tiles', both + [(b, a) for a, b in both])  7.81 us
    pallas_call x1, Pallas kernels, state_part(): pl.pallas_call(state_kernel, in_specs=[VMEM] * 4, out_specs=VMEM, out_sha...  3.06 us
    pallas_call x1, Pallas kernels, pack(): pl.pallas_call(pack_kernel, grid=(1,), in_specs=[SMEM, SMEM] + specs * 2,...  2.23 us
    pallas_call x1, Pallas kernels, edge_part(): pl.pallas_call(edge_kernel, in_specs=[SMEM, SMEM] + [VMEM] * 9, out_specs...  1.32 us
  transfers between devices with their start and end apart: 9, of which 7 were waited for; matrix products, arithmetic and copies ran while one was open for 0% of the time, Pallas kernels for 26%

profile of v3, /device:TPU:0, one launch (start us, length us, event | category | flops | bytes accessed | tf_op | source)
XLA Modules:
  0.0 50.6 jit_solution(1192592626728606311)
XLA Ops:
  0.6 0.0 copy-start
  0.6 0.0 copy-start.1
  0.7 0.0 copy-start.4
  0.7 0.0 copy-start.5
  0.7 0.0 copy-start.6
  0.7 2.2 %pack.1 = (bf16[2,2,2,32,128]{4,3,2,1,0:T(8,128)(2,1)}, bf16[5,128,128]{2,1,0:T(8,128)(2,1)}, bf16[4,128,128]{2,1,0:T(8,128)(2,1)}) custom-call(s32[1,8]{1,0:T(1,128)} %links.5, s32[1]{0:T(128)} %bitcast.me_ref, bf16[32,128,128]{2,1,0:T(8,128)(2,1)} %bitcast.7, bf16[32,128,128]{2,1,0:T(8,128)(2,1)} %bitcast.8, bf16[32,128,128]{2,1,0:T(8,128)(2,1)} %bitcast.9, ...), custom_call_target="tpu_custom_call" | custom-call | tf_op jit(solution)/shard_map/pack/pallas_call | solution.py:61
  2.9 0.5 collective-permute-start
  3.4 0.7 %collective-permute-start.1 = (bf16[4,128,128]{2,1,0:T(8,128)(2,1)}, bf16[4,128,128]{2,1,0:T(8,128)(2,1)S(1)}, u32[]{:S(2)}, u32[]{:S(2)}) collective-permute-start(bf16[4,128,128]{2,1,0:T(8,128)(2,1)} %get-tuple-element.20), channel_id=1, source_target_pairs={{1,2},{3,4},{5,6},{7,8},{9,10},{11,12},{13,14},{2,1},{4,3},{6,5},{... | collective-permute-start | bytes 393224 | tf_op jit(solution)/shard_map/ppermute | solution.py:425
  4.0 0.6 %collective-permute-done.on_in = bf16[5,128,128]{2,1,0:T(8,128)(2,1)S(1)} collective-permute-done((bf16[5,128,128]{2,1,0:T(8,128)(2,1)}, bf16[5,128,128]{2,1,0:T(8,128)(2,1)S(1)}, u32[]{:S(2)}, u32[]{:S(2)}) %collective-permute-start) | collective-permute-done | bytes 163872 | tf_op jit(solution)/shard_map/ppermute | solution.py:425
  4.6 0.8 %copy-done.2 = bf16[2,2,2,32,128]{4,3,2,1,0:T(8,128)(2,1)S(1)} copy-done((bf16[2,2,2,32,128]{4,3,2,1,0:T(8,128)(2,1)S(1)}, bf16[2,2,2,32,128]{4,3,2,1,0:T(8,128)(2,1)}, u32[]{:S(2)}) %copy-start.2) | copy-done | bytes 65560
  5.4 0.8 %slots.1 = bf16[8,2,2,32,128]{4,3,2,1,0:T(8,128)(2,1)} custom-call(s32[1]{0:T(128)} %bitcast.me_ref, bf16[2,2,2,32,128]{4,3,2,1,0:T(8,128)(2,1)S(1)} %copy-done.2, bf16[5,128,128]{2,1,0:T(8,128)(2,1)S(1)} %collective-permute-done.on_in), custom_call_target="tpu_custom_call" | custom-call | tf_op jit(solution)/shard_map/slots/pallas_call | solution.py:92
  6.2 8.1 %all-to-all-start = ((bf16[8,2,2,32,128]{4,3,2,1,0:T(8,128)(2,1)}), bf16[8,2,2,32,128]{4,3,2,1,0:T(8,128)(2,1)S(1)}, u32[]{:S(2)}, u32[]{:S(2)}) async-start(bf16[8,2,2,32,128]{4,3,2,1,0:T(8,128)(2,1)} %slots.1), calls=%async_computation | async-start | bytes 524288 | tf_op jit(solution)/shard_map/all_to_all | solution.py:463
  14.4 0.0 collective-permute-done.1.off_in
  14.4 0.0 copy-done
  14.4 0.0 copy-done.1
  14.4 9.2 %main.1 = (bf16[17,2,128,128]{3,2,1,0:T(8,128)(2,1)}, f32[9,32,128]{2,1,0:T(8,128)S(1)}, f32[9,32,128]{2,1,0:T(8,128)S(1)}) custom-call(s32[1,8]{1,0:T(1,128)S(1)} %copy-done.6, s32[1]{0:T(128)} %bitcast.me_ref, bf16[32,128,128]{2,1,0:T(8,128)(2,1)S(1)} %bitcast.11, bf16[32,128,128]{2,1,0:T(8,128)(2,1)S(1)} %bitcast.16, ...), custom_call_target="tpu_custom_call" | custom-call | flops 96636764160 | bytes 5242880 | tf_op jit(solution)/shard_map/main/pallas_call | solution.py:240
  23.6 0.0 all-to-all-done
  23.6 0.1 collective-permute-start.2
  23.7 1.5 %collective-permute-done.2.other_in = bf16[16,2,32,128]{3,2,1,0:T(8,128)(2,1)S(1)} collective-permute-done((bf16[16,2,32,128]{3,2,1,0:T(8,128)(2,1)S(1)}, bf16[16,2,32,128]{3,2,1,0:T(8,128)(2,1)S(1)}, u32[]{:S(2)}, u32[]{:S(2)}) %collective-permute-start.2) | collective-permute-done | bytes 262176 | tf_op jit(solution)/shard_map/ppermute | solution.py:425
  25.2 1.3 %edge.1 = (f32[9,32,128]{2,1,0:T(8,128)S(1)}, f32[9,32,128]{2,1,0:T(8,128)S(1)}, f32[192,128]{1,0:T(8,128)S(1)}) custom-call(s32[1,8]{1,0:T(1,128)S(1)} %copy-done.6, s32[1]{0:T(128)} %bitcast.me_ref, bf16[2,2,2,32,128]{4,3,2,1,0:T(8,128)(2,1)S(1)} %copy-done.3, bf16[16,2,32,128]{3,2,1,0:T(8,128)(2,1)S(1)} %bitcast.19, ...), custom_call_target="tpu_custom_call" | custom-call | flops 209715200 | bytes 3145728 | tf_op jit(solution)/shard_map/edge/pallas_call | solution.py:359
  26.6 0.2 collective-permute-start.3
  26.8 1.2 %collective-permute-done.3 = f32[9,32,128]{2,1,0:T(8,128)S(1)} collective-permute-done((f32[9,32,128]{2,1,0:T(8,128)S(1)}, f32[9,32,128]{2,1,0:T(8,128)S(1)}, u32[]{:S(2)}, u32[]{:S(2)}) %collective-permute-start.3) | collective-permute-done | bytes 147488 | tf_op jit(solution)/shard_map/ppermute | solution.py:425
  28.0 2.1 %collective-permute-start.4 = (f32[9,32,128]{2,1,0:T(8,128)S(1)}, f32[9,32,128]{2,1,0:T(8,128)S(1)}, u32[]{:S(2)}, u32[]{:S(2)}) collective-permute-start(f32[9,32,128]{2,1,0:T(8,128)S(1)} %add.12), channel_id=1, source_target_pairs={{0,2},{1,3},{4,6},{5,7},{8,10},{9,11},{12,14},{13,15},{2,0},{3,1},... | collective-permute-start | bytes 442376 | tf_op jit(solution)/shard_map/ppermute | solution.py:425
  30.1 4.2 %collective-permute-done.4 = f32[9,32,128]{2,1,0:T(8,128)S(1)} collective-permute-done((f32[9,32,128]{2,1,0:T(8,128)S(1)}, f32[9,32,128]{2,1,0:T(8,128)S(1)}, u32[]{:S(2)}, u32[]{:S(2)}) %collective-permute-start.4) | collective-permute-done | bytes 147488 | tf_op jit(solution)/shard_map/ppermute | solution.py:425
  34.3 1.8 %collective-permute-start.5 = (f32[9,32,128]{2,1,0:T(8,128)S(1)}, f32[9,32,128]{2,1,0:T(8,128)S(1)}, u32[]{:S(2)}, u32[]{:S(2)}) collective-permute-start(f32[9,32,128]{2,1,0:T(8,128)S(1)} %add.13), channel_id=1, source_target_pairs={{0,4},{1,5},{2,6},{3,7},{8,12},{9,13},{10,14},{11,15},{4,0},{5,1},... | collective-permute-start | bytes 442376 | tf_op jit(solution)/shard_map/ppermute | solution.py:425
  36.1 3.6 %collective-permute-done.5 = f32[9,32,128]{2,1,0:T(8,128)S(1)} collective-permute-done((f32[9,32,128]{2,1,0:T(8,128)S(1)}, f32[9,32,128]{2,1,0:T(8,128)S(1)}, u32[]{:S(2)}, u32[]{:S(2)}) %collective-permute-start.5) | collective-permute-done | bytes 147488 | tf_op jit(solution)/shard_map/ppermute | solution.py:425
  39.8 2.5 %collective-permute-start.6 = (f32[9,32,128]{2,1,0:T(8,128)S(1)}, f32[9,32,128]{2,1,0:T(8,128)S(1)}, u32[]{:S(2)}, u32[]{:S(2)}) collective-permute-start(f32[9,32,128]{2,1,0:T(8,128)S(1)} %add.14), channel_id=1, source_target_pairs={{0,8},{1,9},{2,10},{3,11},{4,12},{5,13},{6,14},{7,15},{8,0},{9,1},... | collective-permute-start | bytes 442376 | tf_op jit(solution)/shard_map/ppermute | solution.py:425
  42.2 3.1 %state.1 = bf16[32,128,128]{2,1,0:T(8,128)(2,1)} custom-call(bf16[17,2,128,128]{3,2,1,0:T(8,128)(2,1)S(1)} %copy-done.7, f32[192,128]{1,0:T(8,128)S(1)} %get-tuple-element.30.edge_grad, bf16[3,3,32,128]{3,2,1,0:T(8,128)(2,1)S(1)} %copy-done.5, bf16[32,128,128]{2,1,0:T(8,128)(2,1)S(1)} %bitcast.17), custom_call_target="tpu_custom_call" | custom-call | flops 1258291200 | bytes 3145728 | tf_op jit(solution)/shard_map/state/pallas_call | solution.py:408
  45.3 3.1 %collective-permute-done.6 = f32[9,32,128]{2,1,0:T(8,128)S(1)} collective-permute-done((f32[9,32,128]{2,1,0:T(8,128)S(1)}, f32[9,32,128]{2,1,0:T(8,128)S(1)}, u32[]{:S(2)}, u32[]{:S(2)}) %collective-permute-start.6) | collective-permute-done | bytes 147488 | tf_op jit(solution)/shard_map/ppermute | solution.py:425
  48.4 0.1 collective-permute-start.7
  48.5 1.4 %collective-permute-done.7 = f32[9,32,128]{2,1,0:T(8,128)S(1)} collective-permute-done((f32[9,32,128]{2,1,0:T(8,128)S(1)}, f32[9,32,128]{2,1,0:T(8,128)S(1)}, u32[]{:S(2)}, u32[]{:S(2)}) %collective-permute-start.7) | collective-permute-done | bytes 147488 | tf_op jit(solution)/shard_map/ppermute | solution.py:425
  49.8 0.7 %broadcast_select_fusion = (f32[9,32,128]{2,1,0:T(8,128)}, f32[9,32,128]{2,1,0:T(8,128)}) fusion(f32[9,32,128]{2,1,0:T(8,128)S(1)} %collective-permute-done.7, f32[9,32,128]{2,1,0:T(8,128)S(1)} %add_multiply_fusion, pred[]{:T(512)S(6)} %eq.3), kind=kLoop, calls=%fused_computation.1 | loop fusion | flops 73728 | bytes 589825 | tf_op jit(solution)/shard_map/jit(_where)/select_n | solution.py:448
  (12 shorter events, 0.1 us)
Async XLA Ops:
  0.6 13.7 %copy-start = (bf16[1,32,128,128]{3,2,1,0:T(8,128)(2,1)S(1)}, bf16[1,32,128,128]{3,2,1,0:T(8,128)(2,1)}, u32[]{:S(2)}) copy-start(bf16[1,32,128,128]{3,2,1,0:T(8,128)(2,1)} %param.5) | copy-start | bytes 3145732
  0.6 13.7 %copy-start.1 = (bf16[1,32,128,128]{3,2,1,0:T(8,128)(2,1)S(1)}, bf16[1,32,128,128]{3,2,1,0:T(8,128)(2,1)}, u32[]{:S(2)}) copy-start(bf16[1,32,128,128]{3,2,1,0:T(8,128)(2,1)} %param.6) | copy-start | bytes 3145732
  0.7 13.7 %copy-start.4 = (bf16[3,3,32,128]{3,2,1,0:T(8,128)(2,1)S(1)}, bf16[3,3,32,128]{3,2,1,0:T(8,128)(2,1)}, u32[]{:S(2)}) copy-start(bf16[3,3,32,128]{3,2,1,0:T(8,128)(2,1)} %second_k.3) | copy-start | bytes 221188
  0.7 13.7 %copy-start.5 = (bf16[3,3,32,128]{3,2,1,0:T(8,128)(2,1)S(1)}, bf16[3,3,32,128]{3,2,1,0:T(8,128)(2,1)}, u32[]{:S(2)}) copy-start(bf16[3,3,32,128]{3,2,1,0:T(8,128)(2,1)} %first_k.5) | copy-start | bytes 221188
  0.7 13.7 %copy-start.6 = (s32[1,8]{1,0:T(1,128)S(1)}, s32[1,8]{1,0:T(1,128)}, u32[]{:S(2)}) copy-start(s32[1,8]{1,0:T(1,128)} %links.5) | copy-start | bytes 100
  2.9 1.7 %collective-permute-start = (bf16[5,128,128]{2,1,0:T(8,128)(2,1)}, bf16[5,128,128]{2,1,0:T(8,128)(2,1)S(1)}, u32[]{:S(2)}, u32[]{:S(2)}) collective-permute-start(bf16[5,128,128]{2,1,0:T(8,128)(2,1)} %get-tuple-element.19), channel_id=1, source_target_pairs={{0,1},{2,3},{4,5},{6,7},{8,9},{10,11},{12,13},{14,15},{1,0},{3,2},... | collective-permute-start | bytes 491528 | tf_op jit(solution)/shard_map/ppermute | solution.py:425
  3.4 11.0 %collective-permute-start.1 = (bf16[4,128,128]{2,1,0:T(8,128)(2,1)}, bf16[4,128,128]{2,1,0:T(8,128)(2,1)S(1)}, u32[]{:S(2)}, u32[]{:S(2)}) collective-permute-start(bf16[4,128,128]{2,1,0:T(8,128)(2,1)} %get-tuple-element.20), channel_id=1, source_target_pairs={{1,2},{3,4},{5,6},{7,8},{9,10},{11,12},{13,14},{2,1},{4,3},{6,5},{... | collective-permute-start | bytes 393224 | tf_op jit(solution)/shard_map/ppermute | solution.py:425
  4.6 0.8 %copy-start.2 = (bf16[2,2,2,32,128]{4,3,2,1,0:T(8,128)(2,1)S(1)}, bf16[2,2,2,32,128]{4,3,2,1,0:T(8,128)(2,1)}, u32[]{:S(2)}) copy-start(bf16[2,2,2,32,128]{4,3,2,1,0:T(8,128)(2,1)} %get-tuple-element.18.own) | copy-start | bytes 196612
  6.2 17.4 %all-to-all-start = ((bf16[8,2,2,32,128]{4,3,2,1,0:T(8,128)(2,1)}), bf16[8,2,2,32,128]{4,3,2,1,0:T(8,128)(2,1)S(1)}, u32[]{:S(2)}, u32[]{:S(2)}) async-start(bf16[8,2,2,32,128]{4,3,2,1,0:T(8,128)(2,1)} %slots.1), calls=%async_computation | async-start | bytes 524288 | tf_op jit(solution)/shard_map/all_to_all | solution.py:463
  14.4 10.9 %copy-start.3 = (bf16[2,2,2,32,128]{4,3,2,1,0:T(8,128)(2,1)S(1)}, bf16[2,2,2,32,128]{4,3,2,1,0:T(8,128)(2,1)}, u32[]{:S(2)}) copy-start(bf16[2,2,2,32,128]{4,3,2,1,0:T(8,128)(2,1)} %get-tuple-element.18.own) | copy-start | bytes 196612
  23.6 1.6 %collective-permute-start.2 = (bf16[16,2,32,128]{3,2,1,0:T(8,128)(2,1)S(1)}, bf16[16,2,32,128]{3,2,1,0:T(8,128)(2,1)S(1)}, u32[]{:S(2)}, u32[]{:S(2)}) collective-permute-start(bf16[16,2,32,128]{3,2,1,0:T(8,128)(2,1)S(1)} %bitcast.18), channel_id=1, source_target_pairs={{0,1},{2,3},{4,5},{6,7},{8,9},{10,11},{12,13},{14,15},{1,0},{3,2},... | collective-permute-start | bytes 786440 | tf_op jit(solution)/shard_map/ppermute | solution.py:425
  25.2 17.0 %copy-start.7 = (bf16[17,2,128,128]{3,2,1,0:T(8,128)(2,1)S(1)}, bf16[17,2,128,128]{3,2,1,0:T(8,128)(2,1)}, u32[]{:S(2)}) copy-start(bf16[17,2,128,128]{3,2,1,0:T(8,128)(2,1)} %get-tuple-element.29.grad) | copy-start | bytes 3342340
  26.6 1.4 %collective-permute-start.3 = (f32[9,32,128]{2,1,0:T(8,128)S(1)}, f32[9,32,128]{2,1,0:T(8,128)S(1)}, u32[]{:S(2)}, u32[]{:S(2)}) collective-permute-start(f32[9,32,128]{2,1,0:T(8,128)S(1)} %get-tuple-element.26), channel_id=1, source_target_pairs={{0,1},{2,3},{4,5},{6,7},{8,9},{10,11},{12,13},{14,15},{1,0},{3,2},... | collective-permute-start | bytes 442376 | tf_op jit(solution)/shard_map/ppermute | solution.py:425
  28.0 6.2 %collective-permute-start.4 = (f32[9,32,128]{2,1,0:T(8,128)S(1)}, f32[9,32,128]{2,1,0:T(8,128)S(1)}, u32[]{:S(2)}, u32[]{:S(2)}) collective-permute-start(f32[9,32,128]{2,1,0:T(8,128)S(1)} %add.12), channel_id=1, source_target_pairs={{0,2},{1,3},{4,6},{5,7},{8,10},{9,11},{12,14},{13,15},{2,0},{3,1},... | collective-permute-start | bytes 442376 | tf_op jit(solution)/shard_map/ppermute | solution.py:425
  34.3 5.4 %collective-permute-start.5 = (f32[9,32,128]{2,1,0:T(8,128)S(1)}, f32[9,32,128]{2,1,0:T(8,128)S(1)}, u32[]{:S(2)}, u32[]{:S(2)}) collective-permute-start(f32[9,32,128]{2,1,0:T(8,128)S(1)} %add.13), channel_id=1, source_target_pairs={{0,4},{1,5},{2,6},{3,7},{8,12},{9,13},{10,14},{11,15},{4,0},{5,1},... | collective-permute-start | bytes 442376 | tf_op jit(solution)/shard_map/ppermute | solution.py:425
  39.8 8.6 %collective-permute-start.6 = (f32[9,32,128]{2,1,0:T(8,128)S(1)}, f32[9,32,128]{2,1,0:T(8,128)S(1)}, u32[]{:S(2)}, u32[]{:S(2)}) collective-permute-start(f32[9,32,128]{2,1,0:T(8,128)S(1)} %add.14), channel_id=1, source_target_pairs={{0,8},{1,9},{2,10},{3,11},{4,12},{5,13},{6,14},{7,15},{8,0},{9,1},... | collective-permute-start | bytes 442376 | tf_op jit(solution)/shard_map/ppermute | solution.py:425
  48.4 1.4 %collective-permute-start.7 = (f32[9,32,128]{2,1,0:T(8,128)S(1)}, f32[9,32,128]{2,1,0:T(8,128)S(1)}, u32[]{:S(2)}, u32[]{:S(2)}) collective-permute-start(f32[9,32,128]{2,1,0:T(8,128)S(1)} %add_multiply_fusion), channel_id=1, source_target_pairs={{0,1},{2,3},{4,5},{6,7},{8,9},{10,11},{12,13},{14,15},{1,0},{3,2},... | collective-permute-start | bytes 442376 | tf_op jit(solution)/shard_map/ppermute | solution.py:425

commit v4 on v3

--- a/solution.py
+++ b/solution.py
@@ -11,6 +11,7 @@
 CUBE = 0.044715
 ROOT = math.sqrt(2.0 / math.pi)
 MIB = 1 << 20
+PACK = 8
 SMEM = pl.BlockSpec(memory_space=pltpu.SMEM)
 VMEM = pl.BlockSpec(memory_space=pltpu.VMEM)
 
@@ -32,12 +33,23 @@
     return v * half, slope
 
 
-def pack_kernel(links, me_ref, *refs):
-    blocks, (own, on_out, off_out) = refs[:8], refs[8:]
+def pack_kernel(links_in, me_ref, state, cot, own, on_out, off_out, rows, columns, links, sem, links_sem):
+    rows_n, cols_n, chans = state.shape
     me = me_ref[0]
+    copies = [pltpu.make_async_copy(links_in, links, links_sem)]
+    for f, field in enumerate((state, cot)):
+        for side in range(2):
+            beside = field.at[:, pl.ds(side * (cols_n - 16), 16)]
+            copies.append(pltpu.make_async_copy(beside, columns.at[f, side], sem.at[f, side]))
+            outer = field.at[pl.ds(side * (rows_n - 2), 2)]
+            copies.append(pltpu.make_async_copy(outer, rows.at[f, side], sem.at[f, 2 + side]))
+    for copy in copies:
+        copy.start()
+    for copy in copies:
+        copy.wait()
     for f in range(2):
         for side, first in ((0, 0), (1, 14)):
-            values = blocks[4 * f + 2 + side][...].astype(jnp.float32)
+            values = columns[f, side].astype(jnp.float32)
             for c in range(2):
                 own[side, f, c] = values[:, first + c, :].astype(jnp.bfloat16)
     odd = lax.rem(me, 2) == 1
@@ -45,32 +57,34 @@
     on_out[4] = other.reshape(on_out.shape[1:])
     for target, out in zip(partners(me), (on_out, off_out)):
         for f in range(2):
-            top, bottom = blocks[4 * f][...], blocks[4 * f + 1][...]
-            rows = jnp.where(links[0, 1] == target, bottom, jnp.zeros_like(bottom))
-            out[2 * f : 2 * f + 2] = jnp.where(links[0, 0] == target, top, rows)
+            top, bottom = rows[f, 0], rows[f, 1]
+            sent = jnp.where(links[0, 1] == target, bottom, jnp.zeros_like(bottom))
+            out[2 * f : 2 * f + 2] = jnp.where(links[0, 0] == target, top, sent)
 
 
 def pack(links, me, state, cot):
     rows_n, cols_n, chans = state.shape
-    specs = [
-        pl.BlockSpec((2, cols_n, chans), lambda i: (0, 0, 0)),
-        pl.BlockSpec((2, cols_n, chans), lambda i: (rows_n // 2 - 1, 0, 0)),
-        pl.BlockSpec((rows_n, 16, chans), lambda i: (0, 0, 0)),
-        pl.BlockSpec((rows_n, 16, chans), lambda i: (0, cols_n // 16 - 1, 0)),
-    ]
+    far = pl.BlockSpec(memory_space=pltpu.HBM)
+    placed = functools.partial(pltpu.with_memory_space_constraint, memory_space=pltpu.HBM)
     return pl.pallas_call(
         pack_kernel,
-        grid=(1,),
-        in_specs=[SMEM, SMEM] + specs * 2,
+        in_specs=[far, SMEM, far, far],
         out_specs=[VMEM] * 3,
         out_shape=[
             shape_of((2, 2, 2, rows_n, chans), jnp.bfloat16),
             shape_of((5, 4 * rows_n, chans), jnp.bfloat16),
             shape_of((4, cols_n, chans), jnp.bfloat16),
         ],
-        compiler_params=pltpu.CompilerParams(vmem_limit_bytes=60 * MIB),
+        scratch_shapes=[
+            pltpu.VMEM((2, 2, 2, cols_n, chans), jnp.bfloat16),
+            pltpu.VMEM((2, 2, rows_n, 16, chans), jnp.bfloat16),
+            pltpu.SMEM(links.shape, links.dtype),
+            pltpu.SemaphoreType.DMA((2, 4)),
+            pltpu.SemaphoreType.DMA,
+        ],
+        compiler_params=pltpu.CompilerParams(vmem_limit_bytes=PACK * MIB),
         name="pack",
-    )(links, me, *([state] * 4), *([cot] * 4))
+    )(placed(links), me, placed(state), placed(cot))
 
 
 def slot_kernel(chips, me_ref, own, on_in, send):
@@ -351,6 +365,12 @@
         second = second_acc[tap] + diagonal(second_p[:, turned], mask, width)
         keep[tap] = jnp.where(even, first, second)
         pass_on[tap] = jnp.where(even, second, first)
+        size = jnp.maximum(jnp.abs(first), jnp.abs(second))
+        largest = size if tap == 0 else jnp.maximum(largest, size)
+    largest = jnp.max(jnp.max(largest, 0, keepdims=True), 1, keepdims=True)
+    exponent = jnp.ceil(jnp.log2(jnp.maximum(largest, 2.0**-100)))
+    for out in (keep, pass_on):
+        out[9] = jnp.broadcast_to(exponent, out.shape[1:])
 
 
 def edge_part(links, me, own, received, other_in, on_in, off_in, first_k, second_k, first_acc, second_acc):
@@ -361,8 +381,8 @@
         in_specs=[SMEM, SMEM] + [VMEM] * 9,
         out_specs=[VMEM] * 3,
         out_shape=[
-            shape_of(first_acc.shape, jnp.float32),
-            shape_of(first_acc.shape, jnp.float32),
+            shape_of((10,) + first_acc.shape[1:], jnp.float32),
+            shape_of((10,) + first_acc.shape[1:], jnp.float32),
             shape_of((cells, chans), jnp.float32),
         ],
         scratch_shapes=[
@@ -425,23 +445,49 @@
     return lax.ppermute(value, "tiles", both + [(b, a) for a, b in both])
 
 
+STATE_AT = 2
+TOP = 13.0
+
+
+def power(k):
+    bits = (k + 126.0).astype(jnp.int32)
+    value = jnp.full_like(k, 2.0**-126)
+    for bit in range(8):
+        half = jnp.where(bits & (1 << bit) != 0, 2.0 ** min(1 << bit, 64), 1.0)
+        value = value * half * (half if bit == 7 else 1.0)
+    return value
+
+
+def packed(total, exponent):
+    values = (total * power(TOP - exponent)).astype(jnp.float16)
+    return lax.optimization_barrier(jnp.concatenate([values, exponent.astype(jnp.float16)], 0))
+
+
+def unpacked(packet):
+    exponent = packet[9:].astype(jnp.float32)
+    return packet[:9].astype(jnp.float32) * power(exponent - TOP), exponent
+
+
 def summed(keep, pass_on, me, tiles, scale, edges, state_of):
     even = lax.rem(me, 2) == 0
     if tiles & (tiles - 1):
         first, second = jnp.where(even, keep, pass_on), jnp.where(even, pass_on, keep)
-        first, second = lax.psum((first, second), "tiles")
+        first, second = lax.psum((first[:9], second[:9]), "tiles")
         return first * scale, second * scale, state_of(edges)
     on_chip = [(t, t + 1) for t in range(0, tiles, 2)]
-    total = keep + exchanged(pass_on, tiles, on_chip)
+    other = exchanged(pass_on, tiles, on_chip)
+    total, exponent = keep[:9] + other[:9], jnp.maximum(keep[9:], other[9:]) + 1.0
     distance = 2
     while distance < tiles:
-        last = 2 * distance >= tiles
-        if last:
+        here = distance == 2 if STATE_AT == 2 else 2 * distance >= tiles
+        if here:
             total, edges = lax.optimization_barrier((total, edges))
-        other = exchanged(total, tiles, [(t, t + distance) for t in range(tiles) if not t & distance])
-        if last:
+        packet = packed(total, exponent)
+        other = exchanged(packet, tiles, [(t, t + distance) for t in range(tiles) if not t & distance])
+        if here:
             other, state_grad = lax.optimization_barrier((other, state_of(edges)))
-        total = total + other
+        (total, exponent), (more, bound) = unpacked(packet), unpacked(other)
+        total, exponent = total + more, jnp.maximum(exponent, bound) + 1.0
         distance *= 2
     total = total * scale
     other = exchanged(total, tiles, on_chip)

time: 50.9 us -> 44.6 us (0.88)
  waiting for transfers between devices: 15.6 us -> 10.4 us
  local copies, waits for them, and re-layouts: 0.87 us -> 0.02 us
  Pallas kernels: 16.6 us -> 16 us
    ppermute x8, waiting for transfers between devices: 15.6 us -> 10.4 us  [exchanged(): return lax.ppermute(value, 'tiles', both + [(b, a) for a, b in both])]
    unnamed x16 -> x12, local copies, waits for them, and re-layouts: 0.87 us -> 0.02 us
    pallas_call x1, Pallas kernels: 2.23 us -> 1.58 us  [pack(): pl.pallas_call(pack_kernel, in_specs=[far, SMEM, far, far], out_specs=[VM...]
  transfers between devices with their start and end apart: 9 -> 9, of which waited for: 7 -> 6; matrix products, arithmetic and copies ran while one was open for 0% -> 0% of each run, Pallas kernels for 26% -> 29%
where the time goes in v4:
time: 44.6 us; the launch traced here: 44.4 us
  Pallas kernels  16 us (36%)
  starting transfers between devices  15.8 us (35%)
  waiting for transfers between devices  10.4 us (23%)
  other arithmetic  1.22 us (3%)
  between operations  0.84 us (2%)
    ppermute x8, waiting for transfers between devices, exchanged(): return lax.ppermute(value, 'tiles', both + [(b, a) for a, b in both])  10.4 us
    pallas_call x1, Pallas kernels, main_part(): pl.pallas_call(main_kernel, in_specs=[SMEM, SMEM] + [VMEM] * 6, out_specs...  9.2 us
    all_to_all x1, starting transfers between devices, local(): received = lax.all_to_all(sent, 'tiles', 0, 0, axis_index_groups=cores)  8.34 us
    ppermute x8, starting transfers between devices, exchanged(): return lax.ppermute(value, 'tiles', both + [(b, a) for a, b in both])  7.5 us
    pallas_call x1, Pallas kernels, state_part(): pl.pallas_call(state_kernel, in_specs=[VMEM] * 4, out_specs=VMEM, out_sha...  3.06 us
    pallas_call x1, Pallas kernels, pack(): pl.pallas_call(pack_kernel, in_specs=[far, SMEM, far, far], out_specs=[VM...  1.58 us
    pallas_call x1, Pallas kernels, edge_part(): pl.pallas_call(edge_kernel, in_specs=[SMEM, SMEM] + [VMEM] * 9, out_specs...  1.41 us
  transfers between devices with their start and end apart: 9, of which 6 were waited for; matrix products, arithmetic and copies ran while one was open for 0% of the time, Pallas kernels for 29%

profile of v4, /device:TPU:0, one launch (start us, length us, event | category | flops | bytes accessed | tf_op | source)
XLA Modules:
  0.0 44.4 jit_solution(10135418642660371054)
XLA Ops:
  0.7 1.6 %pack.1 = (bf16[2,2,2,32,128]{4,3,2,1,0:T(8,128)(2,1)S(1)}, bf16[5,128,128]{2,1,0:T(8,128)(2,1)S(1)}, bf16[4,128,128]{2,1,0:T(8,128)(2,1)S(1)}) custom-call(s32[1,8]{1,0:T(1,128)} %links.3, s32[1]{0:T(128)} %bitcast.me_ref, bf16[32,128,128]{2,1,0:T(8,128)(2,1)} %bitcast.25, bf16[32,128,128]{2,1,0:T(8,128)(2,1)} %bitcast.27), custom_call_target="tpu_custom_call" | custom-call | tf_op jit(solution)/shard_map/pack/pallas_call | solution.py:69
  2.3 0.5 %collective-permute-start = (bf16[5,128,128]{2,1,0:T(8,128)(2,1)S(1)}, bf16[5,128,128]{2,1,0:T(8,128)(2,1)S(1)}, u32[]{:S(2)}, u32[]{:S(2)}) collective-permute-start(bf16[5,128,128]{2,1,0:T(8,128)(2,1)S(1)} %get-tuple-element.19), channel_id=1, source_target_pairs={{0,1},{2,3},{4,5},{6,7},{8,9},{10,11},{12,13},{14,15},{1,0},{3,2},... | collective-permute-start | bytes 491528 | tf_op jit(solution)/shard_map/ppermute | solution.py:445
  2.8 0.7 %collective-permute-start.1 = (bf16[4,128,128]{2,1,0:T(8,128)(2,1)S(1)}, bf16[4,128,128]{2,1,0:T(8,128)(2,1)S(1)}, u32[]{:S(2)}, u32[]{:S(2)}) collective-permute-start(bf16[4,128,128]{2,1,0:T(8,128)(2,1)S(1)} %get-tuple-element.20), channel_id=1, source_target_pairs={{1,2},{3,4},{5,6},{7,8},{9,10},{11,12},{13,14},{2,1},{4,3},{6,5},{... | collective-permute-start | bytes 393224 | tf_op jit(solution)/shard_map/ppermute | solution.py:445
  3.5 0.4 collective-permute-done.on_in
  3.8 0.8 %slots.1 = bf16[8,2,2,32,128]{4,3,2,1,0:T(8,128)(2,1)} custom-call(s32[1]{0:T(128)} %bitcast.me_ref, bf16[2,2,2,32,128]{4,3,2,1,0:T(8,128)(2,1)S(1)} %get-tuple-element.18.own, bf16[5,128,128]{2,1,0:T(8,128)(2,1)S(1)} %collective-permute-done.on_in), custom_call_target="tpu_custom_call" | custom-call | tf_op jit(solution)/shard_map/slots/pallas_call | solution.py:106
  4.6 8.3 %all-to-all-start = ((bf16[8,2,2,32,128]{4,3,2,1,0:T(8,128)(2,1)}), bf16[8,2,2,32,128]{4,3,2,1,0:T(8,128)(2,1)S(1)}, u32[]{:S(2)}, u32[]{:S(2)}) async-start(bf16[8,2,2,32,128]{4,3,2,1,0:T(8,128)(2,1)} %slots.1), calls=%async_computation | async-start | bytes 524288 | tf_op jit(solution)/shard_map/all_to_all | solution.py:509
  12.9 0.0 collective-permute-done.1.off_in
  13.0 0.0 copy-done
  13.0 0.0 copy-done.1
  13.0 0.0 copy-done.2
  13.0 0.0 copy-done.3
  13.0 0.0 copy-done.4
  13.0 9.2 %main.1 = (bf16[17,2,128,128]{3,2,1,0:T(8,128)(2,1)}, f32[9,32,128]{2,1,0:T(8,128)S(1)}, f32[9,32,128]{2,1,0:T(8,128)S(1)}) custom-call(s32[1,8]{1,0:T(1,128)S(1)} %copy-done.4, s32[1]{0:T(128)} %bitcast.me_ref, bf16[32,128,128]{2,1,0:T(8,128)(2,1)S(1)} %bitcast.26, bf16[32,128,128]{2,1,0:T(8,128)(2,1)S(1)} %bitcast.28, ...), custom_call_target="tpu_custom_call" | custom-call | flops 96636764160 | bytes 5242880 | tf_op jit(solution)/shard_map/main/pallas_call | solution.py:254
  22.2 0.0 all-to-all-done
  22.2 0.1 collective-permute-start.2
  22.3 1.5 %collective-permute-done.2.other_in = bf16[16,2,32,128]{3,2,1,0:T(8,128)(2,1)S(1)} collective-permute-done((bf16[16,2,32,128]{3,2,1,0:T(8,128)(2,1)S(1)}, bf16[16,2,32,128]{3,2,1,0:T(8,128)(2,1)S(1)}, u32[]{:S(2)}, u32[]{:S(2)}) %collective-permute-start.2) | collective-permute-done | bytes 262176 | tf_op jit(solution)/shard_map/ppermute | solution.py:445
  23.8 1.4 %edge.1 = (f32[10,32,128]{2,1,0:T(8,128)S(1)}, f32[10,32,128]{2,1,0:T(8,128)S(1)}, f32[192,128]{1,0:T(8,128)S(1)}) custom-call(s32[1,8]{1,0:T(1,128)S(1)} %copy-done.4, s32[1]{0:T(128)} %bitcast.me_ref, bf16[2,2,2,32,128]{4,3,2,1,0:T(8,128)(2,1)S(1)} %get-tuple-element.18.own, bf16[16,2,32,128]{3,2,1,0:T(8,128)(2,1)S(1)} %bitcast.31, ...), custom_call_target="tpu_custom_call" | custom-call | flops 209715200 | bytes 3145728 | tf_op jit(solution)/shard_map/edge/pallas_call | solution.py:379
  25.2 0.1 collective-permute-start.3
  25.4 1.3 %collective-permute-done.3 = f32[10,32,128]{2,1,0:T(8,128)S(1)} collective-permute-done((f32[10,32,128]{2,1,0:T(8,128)S(1)}, f32[10,32,128]{2,1,0:T(8,128)S(1)}, u32[]{:S(2)}, u32[]{:S(2)}) %collective-permute-start.3) | collective-permute-done | bytes 163872 | tf_op jit(solution)/shard_map/ppermute | solution.py:445
  26.8 2.1 %collective-permute-start.4 = (f16[10,32,128]{2,1,0:T(8,128)(2,1)S(1)}, f16[10,32,128]{2,1,0:T(8,128)(2,1)S(1)}, u32[]{:S(2)}, u32[]{:S(2)}) collective-permute-start(f16[10,32,128]{2,1,0:T(8,128)(2,1)S(1)} %pad_maximum_fusion), channel_id=1, source_target_pairs={{0,2},{1,3},{4,6},{5,7},{8,10},{9,11},{12,14},{13,15},{2,0},{3,1},... | collective-permute-start | bytes 245768 | tf_op jit(solution)/shard_map/ppermute | solution.py:445
  28.9 3.1 %state.1 = bf16[32,128,128]{2,1,0:T(8,128)(2,1)} custom-call(bf16[17,2,128,128]{3,2,1,0:T(8,128)(2,1)S(1)} %copy-done.5, f32[192,128]{1,0:T(8,128)S(1)} %get-tuple-element.30.edge_grad, bf16[3,3,32,128]{3,2,1,0:T(8,128)(2,1)S(1)} %copy-done.3, bf16[32,128,128]{2,1,0:T(8,128)(2,1)S(1)} %bitcast.29), custom_call_target="tpu_custom_call" | custom-call | flops 1258291200 | bytes 3145728 | tf_op jit(solution)/shard_map/state/pallas_call | solution.py:428
  31.9 0.0 collective-permute-done.4
  31.9 0.1 fusion.73
  32.1 1.5 %collective-permute-start.5 = (f16[10,32,128]{2,1,0:T(8,128)(2,1)S(1)}, f16[10,32,128]{2,1,0:T(8,128)(2,1)S(1)}, u32[]{:S(2)}, u32[]{:S(2)}) collective-permute-start(f16[10,32,128]{2,1,0:T(8,128)(2,1)S(1)} %pad_maximum_fusion.1), channel_id=1, source_target_pairs={{0,4},{1,5},{2,6},{3,7},{8,12},{9,13},{10,14},{11,15},{4,0},{5,1},... | collective-permute-start | bytes 245768 | tf_op jit(solution)/shard_map/ppermute | solution.py:445
  33.6 3.0 %collective-permute-done.5 = f16[10,32,128]{2,1,0:T(8,128)(2,1)S(1)} collective-permute-done((f16[10,32,128]{2,1,0:T(8,128)(2,1)S(1)}, f16[10,32,128]{2,1,0:T(8,128)(2,1)S(1)}, u32[]{:S(2)}, u32[]{:S(2)}) %collective-permute-start.5) | collective-permute-done | bytes 81952 | tf_op jit(solution)/shard_map/ppermute | solution.py:445
  36.6 0.1 fusion.76
  36.7 0.1 multiply_convert_fusion
  36.7 2.4 %collective-permute-start.6 = (f16[10,32,128]{2,1,0:T(8,128)(2,1)S(1)}, f16[10,32,128]{2,1,0:T(8,128)(2,1)S(1)}, u32[]{:S(2)}, u32[]{:S(2)}) collective-permute-start(f16[10,32,128]{2,1,0:T(8,128)(2,1)S(1)} %pad_maximum_fusion.2), channel_id=1, source_target_pairs={{0,8},{1,9},{2,10},{3,11},{4,12},{5,13},{6,14},{7,15},{8,0},{9,1},... | collective-permute-start | bytes 245768 | tf_op jit(solution)/shard_map/ppermute | solution.py:445
  39.2 2.9 %collective-permute-done.6 = f16[10,32,128]{2,1,0:T(8,128)(2,1)S(1)} collective-permute-done((f16[10,32,128]{2,1,0:T(8,128)(2,1)S(1)}, f16[10,32,128]{2,1,0:T(8,128)(2,1)S(1)}, u32[]{:S(2)}, u32[]{:S(2)}) %collective-permute-start.6) | collective-permute-done | bytes 81952 | tf_op jit(solution)/shard_map/ppermute | solution.py:445
  42.2 0.1 collective-permute-start.7
  42.3 1.4 %collective-permute-done.7 = f32[9,32,128]{2,1,0:T(8,128)S(1)} collective-permute-done((f32[9,32,128]{2,1,0:T(8,128)S(1)}, f32[9,32,128]{2,1,0:T(8,128)S(1)}, u32[]{:S(2)}, u32[]{:S(2)}) %collective-permute-start.7) | collective-permute-done | bytes 147488 | tf_op jit(solution)/shard_map/ppermute | solution.py:445
  43.7 0.7 %broadcast_select_fusion = (f32[9,32,128]{2,1,0:T(8,128)}, f32[9,32,128]{2,1,0:T(8,128)}) fusion(f32[9,32,128]{2,1,0:T(8,128)S(1)} %collective-permute-done.7, f32[9,32,128]{2,1,0:T(8,128)S(1)} %add_multiply_fusion, pred[]{:T(512)S(6)} %eq.3), kind=kLoop, calls=%fused_computation.8 | loop fusion | flops 73728 | bytes 589825 | tf_op jit(solution)/shard_map/jit(_where)/select_n | solution.py:494
  (17 shorter events, 0.3 us)
Async XLA Ops:
  0.6 12.3 %copy-start = (bf16[1,32,128,128]{3,2,1,0:T(8,128)(2,1)S(1)}, bf16[1,32,128,128]{3,2,1,0:T(8,128)(2,1)}, u32[]{:S(2)}) copy-start(bf16[1,32,128,128]{3,2,1,0:T(8,128)(2,1)} %param.5) | copy-start | bytes 3145732
  0.6 12.3 %copy-start.1 = (bf16[1,32,128,128]{3,2,1,0:T(8,128)(2,1)S(1)}, bf16[1,32,128,128]{3,2,1,0:T(8,128)(2,1)}, u32[]{:S(2)}) copy-start(bf16[1,32,128,128]{3,2,1,0:T(8,128)(2,1)} %param.6) | copy-start | bytes 3145732
  0.7 12.3 %copy-start.2 = (bf16[3,3,32,128]{3,2,1,0:T(8,128)(2,1)S(1)}, bf16[3,3,32,128]{3,2,1,0:T(8,128)(2,1)}, u32[]{:S(2)}) copy-start(bf16[3,3,32,128]{3,2,1,0:T(8,128)(2,1)} %second_k.3) | copy-start | bytes 221188
  0.7 12.3 %copy-start.3 = (bf16[3,3,32,128]{3,2,1,0:T(8,128)(2,1)S(1)}, bf16[3,3,32,128]{3,2,1,0:T(8,128)(2,1)}, u32[]{:S(2)}) copy-start(bf16[3,3,32,128]{3,2,1,0:T(8,128)(2,1)} %first_k.5) | copy-start | bytes 221188
  0.7 12.3 %copy-start.4 = (s32[1,8]{1,0:T(1,128)S(1)}, s32[1,8]{1,0:T(1,128)}, u32[]{:S(2)}) copy-start(s32[1,8]{1,0:T(1,128)} %links.3) | copy-start | bytes 100
  2.3 1.5 %collective-permute-start = (bf16[5,128,128]{2,1,0:T(8,128)(2,1)S(1)}, bf16[5,128,128]{2,1,0:T(8,128)(2,1)S(1)}, u32[]{:S(2)}, u32[]{:S(2)}) collective-permute-start(bf16[5,128,128]{2,1,0:T(8,128)(2,1)S(1)} %get-tuple-element.19), channel_id=1, source_target_pairs={{0,1},{2,3},{4,5},{6,7},{8,9},{10,11},{12,13},{14,15},{1,0},{3,2},... | collective-permute-start | bytes 491528 | tf_op jit(solution)/shard_map/ppermute | solution.py:445
  2.8 10.2 %collective-permute-start.1 = (bf16[4,128,128]{2,1,0:T(8,128)(2,1)S(1)}, bf16[4,128,128]{2,1,0:T(8,128)(2,1)S(1)}, u32[]{:S(2)}, u32[]{:S(2)}) collective-permute-start(bf16[4,128,128]{2,1,0:T(8,128)(2,1)S(1)} %get-tuple-element.20), channel_id=1, source_target_pairs={{1,2},{3,4},{5,6},{7,8},{9,10},{11,12},{13,14},{2,1},{4,3},{6,5},{... | collective-permute-start | bytes 393224 | tf_op jit(solution)/shard_map/ppermute | solution.py:445
  4.6 17.6 %all-to-all-start = ((bf16[8,2,2,32,128]{4,3,2,1,0:T(8,128)(2,1)}), bf16[8,2,2,32,128]{4,3,2,1,0:T(8,128)(2,1)S(1)}, u32[]{:S(2)}, u32[]{:S(2)}) async-start(bf16[8,2,2,32,128]{4,3,2,1,0:T(8,128)(2,1)} %slots.1), calls=%async_computation | async-start | bytes 524288 | tf_op jit(solution)/shard_map/all_to_all | solution.py:509
  22.2 1.6 %collective-permute-start.2 = (bf16[16,2,32,128]{3,2,1,0:T(8,128)(2,1)S(1)}, bf16[16,2,32,128]{3,2,1,0:T(8,128)(2,1)S(1)}, u32[]{:S(2)}, u32[]{:S(2)}) collective-permute-start(bf16[16,2,32,128]{3,2,1,0:T(8,128)(2,1)S(1)} %bitcast.30), channel_id=1, source_target_pairs={{0,1},{2,3},{4,5},{6,7},{8,9},{10,11},{12,13},{14,15},{1,0},{3,2},... | collective-permute-start | bytes 786440 | tf_op jit(solution)/shard_map/ppermute | solution.py:445
  23.8 5.0 %copy-start.5 = (bf16[17,2,128,128]{3,2,1,0:T(8,128)(2,1)S(1)}, bf16[17,2,128,128]{3,2,1,0:T(8,128)(2,1)}, u32[]{:S(2)}) copy-start(bf16[17,2,128,128]{3,2,1,0:T(8,128)(2,1)} %get-tuple-element.29.grad) | copy-start | bytes 3342340
  25.2 1.4 %collective-permute-start.3 = (f32[10,32,128]{2,1,0:T(8,128)S(1)}, f32[10,32,128]{2,1,0:T(8,128)S(1)}, u32[]{:S(2)}, u32[]{:S(2)}) collective-permute-start(f32[10,32,128]{2,1,0:T(8,128)S(1)} %get-tuple-element.26), channel_id=1, source_target_pairs={{0,1},{2,3},{4,5},{6,7},{8,9},{10,11},{12,13},{14,15},{1,0},{3,2},... | collective-permute-start | bytes 491528 | tf_op jit(solution)/shard_map/ppermute | solution.py:445
  26.8 5.1 %collective-permute-start.4 = (f16[10,32,128]{2,1,0:T(8,128)(2,1)S(1)}, f16[10,32,128]{2,1,0:T(8,128)(2,1)S(1)}, u32[]{:S(2)}, u32[]{:S(2)}) collective-permute-start(f16[10,32,128]{2,1,0:T(8,128)(2,1)S(1)} %pad_maximum_fusion), channel_id=1, source_target_pairs={{0,2},{1,3},{4,6},{5,7},{8,10},{9,11},{12,14},{13,15},{2,0},{3,1},... | collective-permute-start | bytes 245768 | tf_op jit(solution)/shard_map/ppermute | solution.py:445
  32.1 4.5 %collective-permute-start.5 = (f16[10,32,128]{2,1,0:T(8,128)(2,1)S(1)}, f16[10,32,128]{2,1,0:T(8,128)(2,1)S(1)}, u32[]{:S(2)}, u32[]{:S(2)}) collective-permute-start(f16[10,32,128]{2,1,0:T(8,128)(2,1)S(1)} %pad_maximum_fusion.1), channel_id=1, source_target_pairs={{0,4},{1,5},{2,6},{3,7},{8,12},{9,13},{10,14},{11,15},{4,0},{5,1},... | collective-permute-start | bytes 245768 | tf_op jit(solution)/shard_map/ppermute | solution.py:445
  36.7 5.4 %collective-permute-start.6 = (f16[10,32,128]{2,1,0:T(8,128)(2,1)S(1)}, f16[10,32,128]{2,1,0:T(8,128)(2,1)S(1)}, u32[]{:S(2)}, u32[]{:S(2)}) collective-permute-start(f16[10,32,128]{2,1,0:T(8,128)(2,1)S(1)} %pad_maximum_fusion.2), channel_id=1, source_target_pairs={{0,8},{1,9},{2,10},{3,11},{4,12},{5,13},{6,14},{7,15},{8,0},{9,1},... | collective-permute-start | bytes 245768 | tf_op jit(solution)/shard_map/ppermute | solution.py:445
  42.2 1.4 %collective-permute-start.7 = (f32[9,32,128]{2,1,0:T(8,128)S(1)}, f32[9,32,128]{2,1,0:T(8,128)S(1)}, u32[]{:S(2)}, u32[]{:S(2)}) collective-permute-start(f32[9,32,128]{2,1,0:T(8,128)S(1)} %add_multiply_fusion), channel_id=1, source_target_pairs={{0,1},{2,3},{4,5},{6,7},{8,9},{10,11},{12,13},{14,15},{1,0},{3,2},... | collective-permute-start | bytes 442376 | tf_op jit(solution)/shard_map/ppermute | solution.py:445

commit v5 on v4

--- a/solution.py
+++ b/solution.py
@@ -33,7 +33,10 @@
     return v * half, slope
 
 
-def pack_kernel(links_in, me_ref, state, cot, own, on_out, off_out, rows, columns, links, sem, links_sem):
+def pack_kernel(
+    chips, links_in, me_ref, state, cot,
+    own, send, on_out, off_out, rows, columns, links, sem, links_sem, send_sem,
+):
     rows_n, cols_n, chans = state.shape
     me = me_ref[0]
     copies = [pltpu.make_async_copy(links_in, links, links_sem)]
@@ -52,27 +55,32 @@
             values = columns[f, side].astype(jnp.float32)
             for c in range(2):
                 own[side, f, c] = values[:, first + c, :].astype(jnp.bfloat16)
-    odd = lax.rem(me, 2) == 1
-    other = jnp.where(odd, own[:, 0], own[:, 1])
-    on_out[4] = other.reshape(on_out.shape[1:])
+    copies = []
+    for j in range(chips):
+        side = jnp.where(2 * j + 1 > me, 1, 0)
+        copies.append(pltpu.make_async_copy(own.at[side], send.at[j], send_sem.at[j]))
+        copies[-1].start()
     for target, out in zip(partners(me), (on_out, off_out)):
         for f in range(2):
             top, bottom = rows[f, 0], rows[f, 1]
             sent = jnp.where(links[0, 1] == target, bottom, jnp.zeros_like(bottom))
             out[2 * f : 2 * f + 2] = jnp.where(links[0, 0] == target, top, sent)
-
-
-def pack(links, me, state, cot):
+    for copy in copies:
+        copy.wait()
+
+
+def pack(chips, links, me, state, cot):
     rows_n, cols_n, chans = state.shape
     far = pl.BlockSpec(memory_space=pltpu.HBM)
     placed = functools.partial(pltpu.with_memory_space_constraint, memory_space=pltpu.HBM)
     return pl.pallas_call(
-        pack_kernel,
+        functools.partial(pack_kernel, chips),
         in_specs=[far, SMEM, far, far],
-        out_specs=[VMEM] * 3,
+        out_specs=[VMEM, far, VMEM, VMEM],
         out_shape=[
             shape_of((2, 2, 2, rows_n, chans), jnp.bfloat16),
-            shape_of((5, 4 * rows_n, chans), jnp.bfloat16),
+            pltpu.HBM((chips, 2, 2, rows_n, chans), jnp.bfloat16),
+            shape_of((4, cols_n, chans), jnp.bfloat16),
             shape_of((4, cols_n, chans), jnp.bfloat16),
         ],
         scratch_shapes=[
@@ -81,36 +89,11 @@
             pltpu.SMEM(links.shape, links.dtype),
             pltpu.SemaphoreType.DMA((2, 4)),
             pltpu.SemaphoreType.DMA,
+            pltpu.SemaphoreType.DMA((chips,)),
         ],
         compiler_params=pltpu.CompilerParams(vmem_limit_bytes=PACK * MIB),
         name="pack",
     )(placed(links), me, placed(state), placed(cot))
-
-
-def slot_kernel(chips, me_ref, own, on_in, send):
-    me = me_ref[0]
-    chip, odd = me // 2, lax.rem(me, 2) == 1
-    mine = jnp.where(odd, own[:, 1], own[:, 0])
-    other = on_in[4].reshape(mine.shape)
-    low, high = jnp.where(odd, other, mine), jnp.where(odd, mine, other)
-
-    def fill(j, carry):
-        send[j, 0] = jnp.where(j >= chip, low[1], low[0])
-        send[j, 1] = jnp.where(j > chip, high[1], high[0])
-        return carry
-
-    lax.fori_loop(0, chips, fill, 0)
-
-
-def slots(chips, me, own, on_in):
-    return pl.pallas_call(
-        functools.partial(slot_kernel, chips),
-        in_specs=[SMEM] + [VMEM] * 2,
-        out_specs=VMEM,
-        out_shape=shape_of((chips, 2) + own.shape[2:], jnp.bfloat16),
-        compiler_params=pltpu.CompilerParams(vmem_limit_bytes=24 * MIB),
-        name="slots",
-    )(me, own, on_in)
 
 
 def halo_rows(links, me, on_in, off_in, f):
@@ -286,7 +269,6 @@
     me = me_ref[0]
     rows_n, chans = own.shape[3], own.shape[4]
     cols_n = off_in.shape[1]
-    odd = lax.rem(me, 2) == 1
     width = first_acc.shape[1]
     span = rows_n + 16
     mask = same_level(width, chans)
@@ -304,8 +286,8 @@
             def sent(entry):
                 tile = links[0, entry]
                 at = jnp.maximum(tile, 0)
-                pieces = (received[at], other_in[at])[:: 1 - 2 * f]
-                piece = jnp.where(odd, pieces[1], pieces[0]).astype(jnp.float32)
+                chip, same = at // 2, lax.rem(at, 2) == lax.rem(me, 2)
+                piece = jnp.where(same, received[chip, f], other_in[chip, f]).astype(jnp.float32)
                 return jnp.where(tile >= 0, piece, 0.0)
 
             beside, corner_over, corner_under = sent(link), sent(over), sent(under)
@@ -500,14 +482,12 @@
     tiles = lax.axis_size("tiles")
     index = lax.axis_index("tiles")
     me = jnp.reshape(index, (1,)).astype(jnp.int32)
-    own, on_out, off_out = pack(neighbours, me, state, cot)
+    own, send, on_out, off_out = pack(tiles // 2, neighbours, me, state, cot)
     on_chip = [(t, t + 1) for t in range(0, tiles, 2)]
     on_in = exchanged(on_out, tiles, on_chip)
     off_in = exchanged(off_out, tiles, [(t, t + 1) for t in range(1, tiles, 2)])
     cores = [list(range(core, tiles, 2)) for core in range(2)]
-    sent = slots(tiles // 2, me, own, on_in)
-    received = lax.all_to_all(sent, "tiles", 0, 0, axis_index_groups=cores)
-    received = received.reshape((tiles,) + received.shape[2:])
+    received = lax.all_to_all(send, "tiles", 0, 0, axis_index_groups=cores)
     grad, first_acc, second_acc = main_part(
         neighbours, me, state, cot, on_in, off_in, first_kernel, second_kernel
     )

time: 44.6 us -> 44.6 us (level)
    pallas_call x2 -> x1, Pallas kernels: 2.36 us -> 2.26 us  [pack(): pl.pallas_call(functools.partial(pack_kernel, chips), in_specs=[far, SMEM...]
  transfers between devices with their start and end apart: 9 -> 9, of which waited for: 6 -> 5; matrix products, arithmetic and copies ran while one was open for 0% -> 0% of each run, Pallas kernels for 29% -> 28%
where the time goes in v5:
time: 44.6 us; the launch traced here: 44.3 us
  starting transfers between devices  16.2 us (36%)
  Pallas kernels  16 us (36%)
  waiting for transfers between devices  10.1 us (23%)
  other arithmetic  1.22 us (3%)
  between operations  0.85 us (2%)
    ppermute x8, waiting for transfers between devices, exchanged(): return lax.ppermute(value, 'tiles', both + [(b, a) for a, b in both])  10.1 us
    pallas_call x1, Pallas kernels, main_part(): pl.pallas_call(main_kernel, in_specs=[SMEM, SMEM] + [VMEM] * 6, out_specs...  9.23 us
    all_to_all x1, starting transfers between devices, local(): received = lax.all_to_all(send, 'tiles', 0, 0, axis_index_groups=cores)  8.7 us
    ppermute x8, starting transfers between devices, exchanged(): return lax.ppermute(value, 'tiles', both + [(b, a) for a, b in both])  7.49 us
    pallas_call x1, Pallas kernels, state_part(): pl.pallas_call(state_kernel, in_specs=[VMEM] * 4, out_specs=VMEM, out_sha...  3.06 us
    pallas_call x1, Pallas kernels, pack(): pl.pallas_call(functools.partial(pack_kernel, chips), in_specs=[far, SMEM...  2.26 us
    pallas_call x1, Pallas kernels, edge_part(): pl.pallas_call(edge_kernel, in_specs=[SMEM, SMEM] + [VMEM] * 9, out_specs...  1.41 us
  transfers between devices with their start and end apart: 9, of which 5 were waited for; matrix products, arithmetic and copies ran while one was open for 0% of the time, Pallas kernels for 28%

profile of v5, /device:TPU:0, one launch (start us, length us, event | category | flops | bytes accessed | tf_op | source)
XLA Modules:
  0.0 44.3 jit_solution(12032234607612630210)
XLA Ops:
  0.6 0.0 copy-start
  0.6 0.0 copy-start.1
  0.7 0.0 copy-start.2
  0.7 0.0 copy-start.3
  0.7 0.0 copy-start.4
  0.7 2.3 %pack.1 = (bf16[2,2,2,32,128]{4,3,2,1,0:T(8,128)(2,1)S(1)}, bf16[8,2,2,32,128]{4,3,2,1,0:T(8,128)(2,1)}, bf16[4,128,128]{2,1,0:T(8,128)(2,1)S(1)}, bf16[4,128,128]{2,1,0:T(8,128)(2,1)S(1)}) custom-call(s32[1,8]{1,0:T(1,128)} %links.3, s32[1]{0:T(128)} %bitcast.me_ref, bf16[32,128,128]{2,1,0:T(8,128)(2,1)} %bitcast.24, bf16[32,128,128]{2,1,0:T(8,128)(2,1)} %bitcast.26), custom_call_target="tpu_custom_call" | custom-call | tf_op jit(solution)/shard_map/pack/pallas_call | solution.py:76
  3.0 0.5 %collective-permute-start = (bf16[4,128,128]{2,1,0:T(8,128)(2,1)S(1)}, bf16[4,128,128]{2,1,0:T(8,128)(2,1)S(1)}, u32[]{:S(2)}, u32[]{:S(2)}) collective-permute-start(bf16[4,128,128]{2,1,0:T(8,128)(2,1)S(1)} %get-tuple-element.21), channel_id=1, source_target_pairs={{0,1},{2,3},{4,5},{6,7},{8,9},{10,11},{12,13},{14,15},{1,0},{3,2},... | collective-permute-start | bytes 393224 | tf_op jit(solution)/shard_map/ppermute | solution.py:427
  3.5 0.7 %collective-permute-start.1 = (bf16[4,128,128]{2,1,0:T(8,128)(2,1)S(1)}, bf16[4,128,128]{2,1,0:T(8,128)(2,1)S(1)}, u32[]{:S(2)}, u32[]{:S(2)}) collective-permute-start(bf16[4,128,128]{2,1,0:T(8,128)(2,1)S(1)} %get-tuple-element.22), channel_id=1, source_target_pairs={{1,2},{3,4},{5,6},{7,8},{9,10},{11,12},{13,14},{2,1},{4,3},{6,5},{... | collective-permute-start | bytes 393224 | tf_op jit(solution)/shard_map/ppermute | solution.py:427
  4.1 8.7 %all-to-all-start = ((bf16[8,2,2,32,128]{4,3,2,1,0:T(8,128)(2,1)}), bf16[8,2,2,32,128]{4,3,2,1,0:T(8,128)(2,1)S(1)}, u32[]{:S(2)}, u32[]{:S(2)}) async-start(bf16[8,2,2,32,128]{4,3,2,1,0:T(8,128)(2,1)} %get-tuple-element.20), calls=%async_computation | async-start | bytes 524288 | tf_op jit(solution)/shard_map/all_to_all | solution.py:490
  12.8 0.0 collective-permute-done.on_in
  12.8 0.0 collective-permute-done.1.off_in
  12.9 9.2 %main.1 = (bf16[17,2,128,128]{3,2,1,0:T(8,128)(2,1)}, f32[9,32,128]{2,1,0:T(8,128)S(1)}, f32[9,32,128]{2,1,0:T(8,128)S(1)}) custom-call(s32[1,8]{1,0:T(1,128)S(1)} %copy-done.4, s32[1]{0:T(128)} %bitcast.me_ref, bf16[32,128,128]{2,1,0:T(8,128)(2,1)S(1)} %bitcast.25, bf16[32,128,128]{2,1,0:T(8,128)(2,1)S(1)} %bitcast.27, ...), custom_call_target="tpu_custom_call" | custom-call | flops 96636764160 | bytes 5242880 | tf_op jit(solution)/shard_map/main/pallas_call | solution.py:237
  22.1 0.0 all-to-all-done.received
  22.2 0.1 collective-permute-start.2
  22.2 1.5 %collective-permute-done.2.other_in = bf16[8,2,2,32,128]{4,3,2,1,0:T(8,128)(2,1)S(1)} collective-permute-done((bf16[8,2,2,32,128]{4,3,2,1,0:T(8,128)(2,1)S(1)}, bf16[8,2,2,32,128]{4,3,2,1,0:T(8,128)(2,1)S(1)}, u32[]{:S(2)}, u32[]{:S(2)}) %collective-permute-start.2) | collective-permute-done | bytes 262176 | tf_op jit(solution)/shard_map/ppermute | solution.py:427
  23.8 1.4 %edge.1 = (f32[10,32,128]{2,1,0:T(8,128)S(1)}, f32[10,32,128]{2,1,0:T(8,128)S(1)}, f32[192,128]{1,0:T(8,128)S(1)}) custom-call(s32[1,8]{1,0:T(1,128)S(1)} %copy-done.4, s32[1]{0:T(128)} %bitcast.me_ref, bf16[2,2,2,32,128]{4,3,2,1,0:T(8,128)(2,1)S(1)} %get-tuple-element.19.own, bf16[8,2,2,32,128]{4,3,2,1,0:T(8,128)(2,1)S(1)} %all-to-all-done.received, ...), custom_call_target="tpu_custom_call" | custom-call | flops 209715200 | bytes 3145728 | tf_op jit(solution)/shard_map/edge/pallas_call | solution.py:361
  25.2 0.1 collective-permute-start.3
  25.3 1.3 %collective-permute-done.3 = f32[10,32,128]{2,1,0:T(8,128)S(1)} collective-permute-done((f32[10,32,128]{2,1,0:T(8,128)S(1)}, f32[10,32,128]{2,1,0:T(8,128)S(1)}, u32[]{:S(2)}, u32[]{:S(2)}) %collective-permute-start.3) | collective-permute-done | bytes 163872 | tf_op jit(solution)/shard_map/ppermute | solution.py:427
  26.7 2.1 %collective-permute-start.4 = (f16[10,32,128]{2,1,0:T(8,128)(2,1)S(1)}, f16[10,32,128]{2,1,0:T(8,128)(2,1)S(1)}, u32[]{:S(2)}, u32[]{:S(2)}) collective-permute-start(f16[10,32,128]{2,1,0:T(8,128)(2,1)S(1)} %pad_maximum_fusion), channel_id=1, source_target_pairs={{0,2},{1,3},{4,6},{5,7},{8,10},{9,11},{12,14},{13,15},{2,0},{3,1},... | collective-permute-start | bytes 245768 | tf_op jit(solution)/shard_map/ppermute | solution.py:427
  28.8 0.0 copy-done.5
  28.8 3.1 %state.1 = bf16[32,128,128]{2,1,0:T(8,128)(2,1)} custom-call(bf16[17,2,128,128]{3,2,1,0:T(8,128)(2,1)S(1)} %copy-done.5, f32[192,128]{1,0:T(8,128)S(1)} %get-tuple-element.32.edge_grad, bf16[3,3,32,128]{3,2,1,0:T(8,128)(2,1)S(1)} %copy-done.3, bf16[32,128,128]{2,1,0:T(8,128)(2,1)S(1)} %bitcast.28), custom_call_target="tpu_custom_call" | custom-call | flops 1258291200 | bytes 3145728 | tf_op jit(solution)/shard_map/state/pallas_call | solution.py:410
  31.8 0.0 collective-permute-done.4
  31.9 0.1 fusion.73
  32.0 1.5 %collective-permute-start.5 = (f16[10,32,128]{2,1,0:T(8,128)(2,1)S(1)}, f16[10,32,128]{2,1,0:T(8,128)(2,1)S(1)}, u32[]{:S(2)}, u32[]{:S(2)}) collective-permute-start(f16[10,32,128]{2,1,0:T(8,128)(2,1)S(1)} %pad_maximum_fusion.1), channel_id=1, source_target_pairs={{0,4},{1,5},{2,6},{3,7},{8,12},{9,13},{10,14},{11,15},{4,0},{5,1},... | collective-permute-start | bytes 245768 | tf_op jit(solution)/shard_map/ppermute | solution.py:427
  33.5 3.0 %collective-permute-done.5 = f16[10,32,128]{2,1,0:T(8,128)(2,1)S(1)} collective-permute-done((f16[10,32,128]{2,1,0:T(8,128)(2,1)S(1)}, f16[10,32,128]{2,1,0:T(8,128)(2,1)S(1)}, u32[]{:S(2)}, u32[]{:S(2)}) %collective-permute-start.5) | collective-permute-done | bytes 81952 | tf_op jit(solution)/shard_map/ppermute | solution.py:427
  36.5 0.1 fusion.76
  36.6 0.1 multiply_convert_fusion
  36.7 2.4 %collective-permute-start.6 = (f16[10,32,128]{2,1,0:T(8,128)(2,1)S(1)}, f16[10,32,128]{2,1,0:T(8,128)(2,1)S(1)}, u32[]{:S(2)}, u32[]{:S(2)}) collective-permute-start(f16[10,32,128]{2,1,0:T(8,128)(2,1)S(1)} %pad_maximum_fusion.2), channel_id=1, source_target_pairs={{0,8},{1,9},{2,10},{3,11},{4,12},{5,13},{6,14},{7,15},{8,0},{9,1},... | collective-permute-start | bytes 245768 | tf_op jit(solution)/shard_map/ppermute | solution.py:427
  39.1 2.9 %collective-permute-done.6 = f16[10,32,128]{2,1,0:T(8,128)(2,1)S(1)} collective-permute-done((f16[10,32,128]{2,1,0:T(8,128)(2,1)S(1)}, f16[10,32,128]{2,1,0:T(8,128)(2,1)S(1)}, u32[]{:S(2)}, u32[]{:S(2)}) %collective-permute-start.6) | collective-permute-done | bytes 81952 | tf_op jit(solution)/shard_map/ppermute | solution.py:427
  42.2 0.1 collective-permute-start.7
  42.2 1.4 %collective-permute-done.7 = f32[9,32,128]{2,1,0:T(8,128)S(1)} collective-permute-done((f32[9,32,128]{2,1,0:T(8,128)S(1)}, f32[9,32,128]{2,1,0:T(8,128)S(1)}, u32[]{:S(2)}, u32[]{:S(2)}) %collective-permute-start.7) | collective-permute-done | bytes 147488 | tf_op jit(solution)/shard_map/ppermute | solution.py:427
  43.6 0.7 %broadcast_select_fusion = (f32[9,32,128]{2,1,0:T(8,128)}, f32[9,32,128]{2,1,0:T(8,128)}) fusion(f32[9,32,128]{2,1,0:T(8,128)S(1)} %collective-permute-done.7, f32[9,32,128]{2,1,0:T(8,128)S(1)} %add_multiply_fusion, pred[]{:T(512)S(6)} %eq.3), kind=kLoop, calls=%fused_computation.8 | loop fusion | flops 73728 | bytes 589825 | tf_op jit(solution)/shard_map/jit(_where)/select_n | solution.py:476
  (16 shorter events, 0.3 us)
Async XLA Ops:
  0.6 12.2 %copy-start = (bf16[1,32,128,128]{3,2,1,0:T(8,128)(2,1)S(1)}, bf16[1,32,128,128]{3,2,1,0:T(8,128)(2,1)}, u32[]{:S(2)}) copy-start(bf16[1,32,128,128]{3,2,1,0:T(8,128)(2,1)} %param.5) | copy-start | bytes 3145732
  0.6 12.2 %copy-start.1 = (bf16[1,32,128,128]{3,2,1,0:T(8,128)(2,1)S(1)}, bf16[1,32,128,128]{3,2,1,0:T(8,128)(2,1)}, u32[]{:S(2)}) copy-start(bf16[1,32,128,128]{3,2,1,0:T(8,128)(2,1)} %param.6) | copy-start | bytes 3145732
  0.7 12.2 %copy-start.2 = (bf16[3,3,32,128]{3,2,1,0:T(8,128)(2,1)S(1)}, bf16[3,3,32,128]{3,2,1,0:T(8,128)(2,1)}, u32[]{:S(2)}) copy-start(bf16[3,3,32,128]{3,2,1,0:T(8,128)(2,1)} %second_k.3) | copy-start | bytes 221188
  0.7 12.2 %copy-start.3 = (bf16[3,3,32,128]{3,2,1,0:T(8,128)(2,1)S(1)}, bf16[3,3,32,128]{3,2,1,0:T(8,128)(2,1)}, u32[]{:S(2)}) copy-start(bf16[3,3,32,128]{3,2,1,0:T(8,128)(2,1)} %first_k.5) | copy-start | bytes 221188
  0.7 12.2 %copy-start.4 = (s32[1,8]{1,0:T(1,128)S(1)}, s32[1,8]{1,0:T(1,128)}, u32[]{:S(2)}) copy-start(s32[1,8]{1,0:T(1,128)} %links.3) | copy-start | bytes 100
  3.0 9.9 %collective-permute-start = (bf16[4,128,128]{2,1,0:T(8,128)(2,1)S(1)}, bf16[4,128,128]{2,1,0:T(8,128)(2,1)S(1)}, u32[]{:S(2)}, u32[]{:S(2)}) collective-permute-start(bf16[4,128,128]{2,1,0:T(8,128)(2,1)S(1)} %get-tuple-element.21), channel_id=1, source_target_pairs={{0,1},{2,3},{4,5},{6,7},{8,9},{10,11},{12,13},{14,15},{1,0},{3,2},... | collective-permute-start | bytes 393224 | tf_op jit(solution)/shard_map/ppermute | solution.py:427
  3.5 9.4 %collective-permute-start.1 = (bf16[4,128,128]{2,1,0:T(8,128)(2,1)S(1)}, bf16[4,128,128]{2,1,0:T(8,128)(2,1)S(1)}, u32[]{:S(2)}, u32[]{:S(2)}) collective-permute-start(bf16[4,128,128]{2,1,0:T(8,128)(2,1)S(1)} %get-tuple-element.22), channel_id=1, source_target_pairs={{1,2},{3,4},{5,6},{7,8},{9,10},{11,12},{13,14},{2,1},{4,3},{6,5},{... | collective-permute-start | bytes 393224 | tf_op jit(solution)/shard_map/ppermute | solution.py:427
  4.1 18.0 %all-to-all-start = ((bf16[8,2,2,32,128]{4,3,2,1,0:T(8,128)(2,1)}), bf16[8,2,2,32,128]{4,3,2,1,0:T(8,128)(2,1)S(1)}, u32[]{:S(2)}, u32[]{:S(2)}) async-start(bf16[8,2,2,32,128]{4,3,2,1,0:T(8,128)(2,1)} %get-tuple-element.20), calls=%async_computation | async-start | bytes 524288 | tf_op jit(solution)/shard_map/all_to_all | solution.py:490
  22.2 6.6 %copy-start.5 = (bf16[17,2,128,128]{3,2,1,0:T(8,128)(2,1)S(1)}, bf16[17,2,128,128]{3,2,1,0:T(8,128)(2,1)}, u32[]{:S(2)}) copy-start(bf16[17,2,128,128]{3,2,1,0:T(8,128)(2,1)} %get-tuple-element.31.grad) | copy-start | bytes 3342340
  22.2 1.6 %collective-permute-start.2 = (bf16[8,2,2,32,128]{4,3,2,1,0:T(8,128)(2,1)S(1)}, bf16[8,2,2,32,128]{4,3,2,1,0:T(8,128)(2,1)S(1)}, u32[]{:S(2)}, u32[]{:S(2)}) collective-permute-start(bf16[8,2,2,32,128]{4,3,2,1,0:T(8,128)(2,1)S(1)} %all-to-all-done.received), channel_id=1, source_target_pairs={{0,1},{2,3},{4,5},{6,7},{8,9},{10,11},{12,13},{14,15},{1,0},{3,2},... | collective-permute-start | bytes 786440 | tf_op jit(solution)/shard_map/ppermute | solution.py:427
  25.2 1.4 %collective-permute-start.3 = (f32[10,32,128]{2,1,0:T(8,128)S(1)}, f32[10,32,128]{2,1,0:T(8,128)S(1)}, u32[]{:S(2)}, u32[]{:S(2)}) collective-permute-start(f32[10,32,128]{2,1,0:T(8,128)S(1)} %get-tuple-element.28), channel_id=1, source_target_pairs={{0,1},{2,3},{4,5},{6,7},{8,9},{10,11},{12,13},{14,15},{1,0},{3,2},... | collective-permute-start | bytes 491528 | tf_op jit(solution)/shard_map/ppermute | solution.py:427
  26.7 5.1 %collective-permute-start.4 = (f16[10,32,128]{2,1,0:T(8,128)(2,1)S(1)}, f16[10,32,128]{2,1,0:T(8,128)(2,1)S(1)}, u32[]{:S(2)}, u32[]{:S(2)}) collective-permute-start(f16[10,32,128]{2,1,0:T(8,128)(2,1)S(1)} %pad_maximum_fusion), channel_id=1, source_target_pairs={{0,2},{1,3},{4,6},{5,7},{8,10},{9,11},{12,14},{13,15},{2,0},{3,1},... | collective-permute-start | bytes 245768 | tf_op jit(solution)/shard_map/ppermute | solution.py:427
  32.0 4.5 %collective-permute-start.5 = (f16[10,32,128]{2,1,0:T(8,128)(2,1)S(1)}, f16[10,32,128]{2,1,0:T(8,128)(2,1)S(1)}, u32[]{:S(2)}, u32[]{:S(2)}) collective-permute-start(f16[10,32,128]{2,1,0:T(8,128)(2,1)S(1)} %pad_maximum_fusion.1), channel_id=1, source_target_pairs={{0,4},{1,5},{2,6},{3,7},{8,12},{9,13},{10,14},{11,15},{4,0},{5,1},... | collective-permute-start | bytes 245768 | tf_op jit(solution)/shard_map/ppermute | solution.py:427
  36.7 5.4 %collective-permute-start.6 = (f16[10,32,128]{2,1,0:T(8,128)(2,1)S(1)}, f16[10,32,128]{2,1,0:T(8,128)(2,1)S(1)}, u32[]{:S(2)}, u32[]{:S(2)}) collective-permute-start(f16[10,32,128]{2,1,0:T(8,128)(2,1)S(1)} %pad_maximum_fusion.2), channel_id=1, source_target_pairs={{0,8},{1,9},{2,10},{3,11},{4,12},{5,13},{6,14},{7,15},{8,0},{9,1},... | collective-permute-start | bytes 245768 | tf_op jit(solution)/shard_map/ppermute | solution.py:427
  42.2 1.4 %collective-permute-start.7 = (f32[9,32,128]{2,1,0:T(8,128)S(1)}, f32[9,32,128]{2,1,0:T(8,128)S(1)}, u32[]{:S(2)}, u32[]{:S(2)}) collective-permute-start(f32[9,32,128]{2,1,0:T(8,128)S(1)} %add_multiply_fusion), channel_id=1, source_target_pairs={{0,1},{2,3},{4,5},{6,7},{8,9},{10,11},{12,13},{14,15},{1,0},{3,2},... | collective-permute-start | bytes 442376 | tf_op jit(solution)/shard_map/ppermute | solution.py:427

commit v6 on v5

--- a/solution.py
+++ b/solution.py
@@ -187,14 +187,25 @@
         for row, count in spans_of(rows_n // 2, 4):
             thirds(store, 2 * row + 2, field[pl.ds(2 * row, 2 * count)])
 
-    acc1[...] = jnp.zeros_like(acc1)
-    acc2[...] = jnp.zeros_like(acc2)
     pairs_n = rows_n // 2 + 1
+    def products(pair, grads, hidden, near_state, near_cot):
+        one, two = dot(grads.T, near_state), dot(hidden.T, near_cot)
+        if pair == 0:
+            acc1[...] = one
+            acc2[...] = two
+        else:
+            acc1[...] += one
+            acc2[...] += two
+
     copies = []
+    later = None
     for k, (pair, count) in enumerate(spans_of(pairs_n, PAIRS)):
         near_state, near_cot = windows(s3, pair, count), windows(c3, pair, count)
-        hidden, slope = gelu_pair(dot(near_state, w_pre[...]))
-        grads = dot(near_cot, w_back[...]) * slope
+        pre, back = dot(near_state, w_pre[...]), dot(near_cot, w_back[...])
+        if later is not None:
+            products(*later)
+        hidden, slope = gelu_pair(pre)
+        grads = back * slope
         cell = lax.broadcasted_iota(jnp.int32, grads.shape, 0)
         lane = lax.broadcasted_iota(jnp.int32, grads.shape, 1)
         x = lax.rem(cell, cols_n)
@@ -215,8 +226,8 @@
         copies[-1].start()
         grads = jnp.where(inner, grads, 0.0).astype(jnp.bfloat16)
         hidden = jnp.where(inner, hidden, 0.0).astype(jnp.bfloat16)
-        acc1[...] += dot(grads.T, near_state)
-        acc2[...] += dot(hidden.T, near_cot)
+        later = (pair, grads, hidden, near_state, near_cot)
+    products(*later)
     for tap in range(9):
         one, two = (slice((tap + 3 * r) * chans, (tap + 3 * r + 1) * chans) for r in range(2))
         first = acc1[0:chans, one] + acc1[chans : 2 * chans, two]
@@ -227,7 +238,7 @@
         copy.wait()
 
 
-PAIRS = 9
+PAIRS = 6
 
 
 def main_part(links, me, state, cot, on_in, off_in, first_k, second_k):

time: 44.6 us -> 44.3 us (level)
  transfers between devices with their start and end apart: 9 -> 9, of which waited for: 5 -> 6; matrix products, arithmetic and copies ran while one was open for 0% -> 0% of each run, Pallas kernels for 28% -> 27%
where the time goes in v6:
time: 44.3 us; the launch traced here: 44.1 us
  starting transfers between devices  16.1 us (36%)
  Pallas kernels  15.7 us (35%)
  waiting for transfers between devices  10.2 us (23%)
  other arithmetic  1.22 us (3%)
  between operations  0.83 us (2%)
    ppermute x8, waiting for transfers between devices, exchanged(): return lax.ppermute(value, 'tiles', both + [(b, a) for a, b in both])  10.1 us
    pallas_call x1, Pallas kernels, main_part(): pl.pallas_call(main_kernel, in_specs=[SMEM, SMEM] + [VMEM] * 6, out_specs...  8.95 us
    all_to_all x1, starting transfers between devices, local(): received = lax.all_to_all(send, 'tiles', 0, 0, axis_index_groups=cores)  8.7 us
    ppermute x8, starting transfers between devices, exchanged(): return lax.ppermute(value, 'tiles', both + [(b, a) for a, b in both])  7.38 us
    pallas_call x1, Pallas kernels, state_part(): pl.pallas_call(state_kernel, in_specs=[VMEM] * 4, out_specs=VMEM, out_sha...  3.06 us
    pallas_call x1, Pallas kernels, pack(): pl.pallas_call(functools.partial(pack_kernel, chips), in_specs=[far, SMEM...  2.26 us
    pallas_call x1, Pallas kernels, edge_part(): pl.pallas_call(edge_kernel, in_specs=[SMEM, SMEM] + [VMEM] * 9, out_specs...  1.41 us
  transfers between devices with their start and end apart: 9, of which 6 were waited for; matrix products, arithmetic and copies ran while one was open for 0% of the time, Pallas kernels for 27%

profile of v6, /device:TPU:0, one launch (start us, length us, event | category | flops | bytes accessed | tf_op | source)
XLA Modules:
  0.0 44.1 jit_solution(6917561155784203651)
XLA Ops:
  0.6 0.0 copy-start
  0.6 0.0 copy-start.1
  0.7 0.0 copy-start.2
  0.7 0.0 copy-start.3
  0.7 0.0 copy-start.4
  0.7 2.3 %pack.1 = (bf16[2,2,2,32,128]{4,3,2,1,0:T(8,128)(2,1)S(1)}, bf16[8,2,2,32,128]{4,3,2,1,0:T(8,128)(2,1)}, bf16[4,128,128]{2,1,0:T(8,128)(2,1)S(1)}, bf16[4,128,128]{2,1,0:T(8,128)(2,1)S(1)}) custom-call(s32[1,8]{1,0:T(1,128)} %links.3, s32[1]{0:T(128)} %bitcast.me_ref, bf16[32,128,128]{2,1,0:T(8,128)(2,1)} %bitcast.24, bf16[32,128,128]{2,1,0:T(8,128)(2,1)} %bitcast.26), custom_call_target="tpu_custom_call" | custom-call | tf_op jit(solution)/shard_map/pack/pallas_call | solution.py:76
  3.0 0.5 %collective-permute-start = (bf16[4,128,128]{2,1,0:T(8,128)(2,1)S(1)}, bf16[4,128,128]{2,1,0:T(8,128)(2,1)S(1)}, u32[]{:S(2)}, u32[]{:S(2)}) collective-permute-start(bf16[4,128,128]{2,1,0:T(8,128)(2,1)S(1)} %get-tuple-element.21), channel_id=1, source_target_pairs={{0,1},{2,3},{4,5},{6,7},{8,9},{10,11},{12,13},{14,15},{1,0},{3,2},... | collective-permute-start | bytes 393224 | tf_op jit(solution)/shard_map/ppermute | solution.py:438
  3.5 0.7 %collective-permute-start.1 = (bf16[4,128,128]{2,1,0:T(8,128)(2,1)S(1)}, bf16[4,128,128]{2,1,0:T(8,128)(2,1)S(1)}, u32[]{:S(2)}, u32[]{:S(2)}) collective-permute-start(bf16[4,128,128]{2,1,0:T(8,128)(2,1)S(1)} %get-tuple-element.22), channel_id=1, source_target_pairs={{1,2},{3,4},{5,6},{7,8},{9,10},{11,12},{13,14},{2,1},{4,3},{6,5},{... | collective-permute-start | bytes 393224 | tf_op jit(solution)/shard_map/ppermute | solution.py:438
  4.1 8.7 %all-to-all-start = ((bf16[8,2,2,32,128]{4,3,2,1,0:T(8,128)(2,1)}), bf16[8,2,2,32,128]{4,3,2,1,0:T(8,128)(2,1)S(1)}, u32[]{:S(2)}, u32[]{:S(2)}) async-start(bf16[8,2,2,32,128]{4,3,2,1,0:T(8,128)(2,1)} %get-tuple-element.20), calls=%async_computation | async-start | bytes 524288 | tf_op jit(solution)/shard_map/all_to_all | solution.py:501
  12.8 0.0 collective-permute-done.on_in
  12.8 0.0 collective-permute-done.1.off_in
  12.9 0.0 copy-done
  12.9 9.0 %main.1 = (bf16[17,2,128,128]{3,2,1,0:T(8,128)(2,1)}, f32[9,32,128]{2,1,0:T(8,128)S(1)}, f32[9,32,128]{2,1,0:T(8,128)S(1)}) custom-call(s32[1,8]{1,0:T(1,128)S(1)} %copy-done.4, s32[1]{0:T(128)} %bitcast.me_ref, bf16[32,128,128]{2,1,0:T(8,128)(2,1)S(1)} %bitcast.25, bf16[32,128,128]{2,1,0:T(8,128)(2,1)S(1)} %bitcast.27, ...), custom_call_target="tpu_custom_call" | custom-call | flops 96636764160 | bytes 5242880 | tf_op jit(solution)/shard_map/main/pallas_call | solution.py:248
  21.9 0.1 all-to-all-done.received
  22.0 0.0 collective-permute-start.2
  22.0 1.5 %collective-permute-done.2.other_in = bf16[8,2,2,32,128]{4,3,2,1,0:T(8,128)(2,1)S(1)} collective-permute-done((bf16[8,2,2,32,128]{4,3,2,1,0:T(8,128)(2,1)S(1)}, bf16[8,2,2,32,128]{4,3,2,1,0:T(8,128)(2,1)S(1)}, u32[]{:S(2)}, u32[]{:S(2)}) %collective-permute-start.2) | collective-permute-done | bytes 262176 | tf_op jit(solution)/shard_map/ppermute | solution.py:438
  23.5 1.4 %edge.1 = (f32[10,32,128]{2,1,0:T(8,128)S(1)}, f32[10,32,128]{2,1,0:T(8,128)S(1)}, f32[192,128]{1,0:T(8,128)S(1)}) custom-call(s32[1,8]{1,0:T(1,128)S(1)} %copy-done.4, s32[1]{0:T(128)} %bitcast.me_ref, bf16[2,2,2,32,128]{4,3,2,1,0:T(8,128)(2,1)S(1)} %get-tuple-element.19.own, bf16[8,2,2,32,128]{4,3,2,1,0:T(8,128)(2,1)S(1)} %all-to-all-done.received, ...), custom_call_target="tpu_custom_call" | custom-call | flops 209715200 | bytes 3145728 | tf_op jit(solution)/shard_map/edge/pallas_call | solution.py:372
  25.0 0.1 collective-permute-start.3
  25.1 1.3 %collective-permute-done.3 = f32[10,32,128]{2,1,0:T(8,128)S(1)} collective-permute-done((f32[10,32,128]{2,1,0:T(8,128)S(1)}, f32[10,32,128]{2,1,0:T(8,128)S(1)}, u32[]{:S(2)}, u32[]{:S(2)}) %collective-permute-start.3) | collective-permute-done | bytes 163872 | tf_op jit(solution)/shard_map/ppermute | solution.py:438
  26.5 2.0 %collective-permute-start.4 = (f16[10,32,128]{2,1,0:T(8,128)(2,1)S(1)}, f16[10,32,128]{2,1,0:T(8,128)(2,1)S(1)}, u32[]{:S(2)}, u32[]{:S(2)}) collective-permute-start(f16[10,32,128]{2,1,0:T(8,128)(2,1)S(1)} %pad_maximum_fusion), channel_id=1, source_target_pairs={{0,2},{1,3},{4,6},{5,7},{8,10},{9,11},{12,14},{13,15},{2,0},{3,1},... | collective-permute-start | bytes 245768 | tf_op jit(solution)/shard_map/ppermute | solution.py:438
  28.5 3.1 %state.1 = bf16[32,128,128]{2,1,0:T(8,128)(2,1)} custom-call(bf16[17,2,128,128]{3,2,1,0:T(8,128)(2,1)S(1)} %copy-done.5, f32[192,128]{1,0:T(8,128)S(1)} %get-tuple-element.32.edge_grad, bf16[3,3,32,128]{3,2,1,0:T(8,128)(2,1)S(1)} %copy-done.3, bf16[32,128,128]{2,1,0:T(8,128)(2,1)S(1)} %bitcast.28), custom_call_target="tpu_custom_call" | custom-call | flops 1258291200 | bytes 3145728 | tf_op jit(solution)/shard_map/state/pallas_call | solution.py:421
  31.6 0.0 collective-permute-done.4
  31.6 0.1 fusion.73
  31.7 1.5 %collective-permute-start.5 = (f16[10,32,128]{2,1,0:T(8,128)(2,1)S(1)}, f16[10,32,128]{2,1,0:T(8,128)(2,1)S(1)}, u32[]{:S(2)}, u32[]{:S(2)}) collective-permute-start(f16[10,32,128]{2,1,0:T(8,128)(2,1)S(1)} %pad_maximum_fusion.1), channel_id=1, source_target_pairs={{0,4},{1,5},{2,6},{3,7},{8,12},{9,13},{10,14},{11,15},{4,0},{5,1},... | collective-permute-start | bytes 245768 | tf_op jit(solution)/shard_map/ppermute | solution.py:438
  33.3 3.0 %collective-permute-done.5 = f16[10,32,128]{2,1,0:T(8,128)(2,1)S(1)} collective-permute-done((f16[10,32,128]{2,1,0:T(8,128)(2,1)S(1)}, f16[10,32,128]{2,1,0:T(8,128)(2,1)S(1)}, u32[]{:S(2)}, u32[]{:S(2)}) %collective-permute-start.5) | collective-permute-done | bytes 81952 | tf_op jit(solution)/shard_map/ppermute | solution.py:438
  36.2 0.1 fusion.76
  36.3 0.1 multiply_convert_fusion
  36.4 2.4 %collective-permute-start.6 = (f16[10,32,128]{2,1,0:T(8,128)(2,1)S(1)}, f16[10,32,128]{2,1,0:T(8,128)(2,1)S(1)}, u32[]{:S(2)}, u32[]{:S(2)}) collective-permute-start(f16[10,32,128]{2,1,0:T(8,128)(2,1)S(1)} %pad_maximum_fusion.2), channel_id=1, source_target_pairs={{0,8},{1,9},{2,10},{3,11},{4,12},{5,13},{6,14},{7,15},{8,0},{9,1},... | collective-permute-start | bytes 245768 | tf_op jit(solution)/shard_map/ppermute | solution.py:438
  38.9 2.9 %collective-permute-done.6 = f16[10,32,128]{2,1,0:T(8,128)(2,1)S(1)} collective-permute-done((f16[10,32,128]{2,1,0:T(8,128)(2,1)S(1)}, f16[10,32,128]{2,1,0:T(8,128)(2,1)S(1)}, u32[]{:S(2)}, u32[]{:S(2)}) %collective-permute-start.6) | collective-permute-done | bytes 81952 | tf_op jit(solution)/shard_map/ppermute | solution.py:438
  41.9 0.1 collective-permute-start.7
  42.0 1.4 %collective-permute-done.7 = f32[9,32,128]{2,1,0:T(8,128)S(1)} collective-permute-done((f32[9,32,128]{2,1,0:T(8,128)S(1)}, f32[9,32,128]{2,1,0:T(8,128)S(1)}, u32[]{:S(2)}, u32[]{:S(2)}) %collective-permute-start.7) | collective-permute-done | bytes 147488 | tf_op jit(solution)/shard_map/ppermute | solution.py:438
  43.3 0.7 %broadcast_select_fusion = (f32[9,32,128]{2,1,0:T(8,128)}, f32[9,32,128]{2,1,0:T(8,128)}) fusion(f32[9,32,128]{2,1,0:T(8,128)S(1)} %collective-permute-done.7, f32[9,32,128]{2,1,0:T(8,128)S(1)} %add_multiply_fusion, pred[]{:T(512)S(6)} %eq.3), kind=kLoop, calls=%fused_computation.8 | loop fusion | flops 73728 | bytes 589825 | tf_op jit(solution)/shard_map/jit(_where)/select_n | solution.py:487
  (16 shorter events, 0.3 us)
Async XLA Ops:
  0.6 12.2 %copy-start = (bf16[1,32,128,128]{3,2,1,0:T(8,128)(2,1)S(1)}, bf16[1,32,128,128]{3,2,1,0:T(8,128)(2,1)}, u32[]{:S(2)}) copy-start(bf16[1,32,128,128]{3,2,1,0:T(8,128)(2,1)} %param.5) | copy-start | bytes 3145732
  0.6 12.2 %copy-start.1 = (bf16[1,32,128,128]{3,2,1,0:T(8,128)(2,1)S(1)}, bf16[1,32,128,128]{3,2,1,0:T(8,128)(2,1)}, u32[]{:S(2)}) copy-start(bf16[1,32,128,128]{3,2,1,0:T(8,128)(2,1)} %param.6) | copy-start | bytes 3145732
  0.7 12.2 %copy-start.2 = (bf16[3,3,32,128]{3,2,1,0:T(8,128)(2,1)S(1)}, bf16[3,3,32,128]{3,2,1,0:T(8,128)(2,1)}, u32[]{:S(2)}) copy-start(bf16[3,3,32,128]{3,2,1,0:T(8,128)(2,1)} %second_k.3) | copy-start | bytes 221188
  0.7 12.2 %copy-start.3 = (bf16[3,3,32,128]{3,2,1,0:T(8,128)(2,1)S(1)}, bf16[3,3,32,128]{3,2,1,0:T(8,128)(2,1)}, u32[]{:S(2)}) copy-start(bf16[3,3,32,128]{3,2,1,0:T(8,128)(2,1)} %first_k.5) | copy-start | bytes 221188
  0.7 12.2 %copy-start.4 = (s32[1,8]{1,0:T(1,128)S(1)}, s32[1,8]{1,0:T(1,128)}, u32[]{:S(2)}) copy-start(s32[1,8]{1,0:T(1,128)} %links.3) | copy-start | bytes 100
  3.0 9.9 %collective-permute-start = (bf16[4,128,128]{2,1,0:T(8,128)(2,1)S(1)}, bf16[4,128,128]{2,1,0:T(8,128)(2,1)S(1)}, u32[]{:S(2)}, u32[]{:S(2)}) collective-permute-start(bf16[4,128,128]{2,1,0:T(8,128)(2,1)S(1)} %get-tuple-element.21), channel_id=1, source_target_pairs={{0,1},{2,3},{4,5},{6,7},{8,9},{10,11},{12,13},{14,15},{1,0},{3,2},... | collective-permute-start | bytes 393224 | tf_op jit(solution)/shard_map/ppermute | solution.py:438
  3.5 9.4 %collective-permute-start.1 = (bf16[4,128,128]{2,1,0:T(8,128)(2,1)S(1)}, bf16[4,128,128]{2,1,0:T(8,128)(2,1)S(1)}, u32[]{:S(2)}, u32[]{:S(2)}) collective-permute-start(bf16[4,128,128]{2,1,0:T(8,128)(2,1)S(1)} %get-tuple-element.22), channel_id=1, source_target_pairs={{1,2},{3,4},{5,6},{7,8},{9,10},{11,12},{13,14},{2,1},{4,3},{6,5},{... | collective-permute-start | bytes 393224 | tf_op jit(solution)/shard_map/ppermute | solution.py:438
  4.1 17.9 %all-to-all-start = ((bf16[8,2,2,32,128]{4,3,2,1,0:T(8,128)(2,1)}), bf16[8,2,2,32,128]{4,3,2,1,0:T(8,128)(2,1)S(1)}, u32[]{:S(2)}, u32[]{:S(2)}) async-start(bf16[8,2,2,32,128]{4,3,2,1,0:T(8,128)(2,1)} %get-tuple-element.20), calls=%async_computation | async-start | bytes 524288 | tf_op jit(solution)/shard_map/all_to_all | solution.py:501
  22.0 6.5 %copy-start.5 = (bf16[17,2,128,128]{3,2,1,0:T(8,128)(2,1)S(1)}, bf16[17,2,128,128]{3,2,1,0:T(8,128)(2,1)}, u32[]{:S(2)}) copy-start(bf16[17,2,128,128]{3,2,1,0:T(8,128)(2,1)} %get-tuple-element.31.grad) | copy-start | bytes 3342340
  22.0 1.5 %collective-permute-start.2 = (bf16[8,2,2,32,128]{4,3,2,1,0:T(8,128)(2,1)S(1)}, bf16[8,2,2,32,128]{4,3,2,1,0:T(8,128)(2,1)S(1)}, u32[]{:S(2)}, u32[]{:S(2)}) collective-permute-start(bf16[8,2,2,32,128]{4,3,2,1,0:T(8,128)(2,1)S(1)} %all-to-all-done.received), channel_id=1, source_target_pairs={{0,1},{2,3},{4,5},{6,7},{8,9},{10,11},{12,13},{14,15},{1,0},{3,2},... | collective-permute-start | bytes 786440 | tf_op jit(solution)/shard_map/ppermute | solution.py:438
  25.0 1.4 %collective-permute-start.3 = (f32[10,32,128]{2,1,0:T(8,128)S(1)}, f32[10,32,128]{2,1,0:T(8,128)S(1)}, u32[]{:S(2)}, u32[]{:S(2)}) collective-permute-start(f32[10,32,128]{2,1,0:T(8,128)S(1)} %get-tuple-element.28), channel_id=1, source_target_pairs={{0,1},{2,3},{4,5},{6,7},{8,9},{10,11},{12,13},{14,15},{1,0},{3,2},... | collective-permute-start | bytes 491528 | tf_op jit(solution)/shard_map/ppermute | solution.py:438
  26.5 5.1 %collective-permute-start.4 = (f16[10,32,128]{2,1,0:T(8,128)(2,1)S(1)}, f16[10,32,128]{2,1,0:T(8,128)(2,1)S(1)}, u32[]{:S(2)}, u32[]{:S(2)}) collective-permute-start(f16[10,32,128]{2,1,0:T(8,128)(2,1)S(1)} %pad_maximum_fusion), channel_id=1, source_target_pairs={{0,2},{1,3},{4,6},{5,7},{8,10},{9,11},{12,14},{13,15},{2,0},{3,1},... | collective-permute-start | bytes 245768 | tf_op jit(solution)/shard_map/ppermute | solution.py:438
  31.7 4.5 %collective-permute-start.5 = (f16[10,32,128]{2,1,0:T(8,128)(2,1)S(1)}, f16[10,32,128]{2,1,0:T(8,128)(2,1)S(1)}, u32[]{:S(2)}, u32[]{:S(2)}) collective-permute-start(f16[10,32,128]{2,1,0:T(8,128)(2,1)S(1)} %pad_maximum_fusion.1), channel_id=1, source_target_pairs={{0,4},{1,5},{2,6},{3,7},{8,12},{9,13},{10,14},{11,15},{4,0},{5,1},... | collective-permute-start | bytes 245768 | tf_op jit(solution)/shard_map/ppermute | solution.py:438
  36.4 5.4 %collective-permute-start.6 = (f16[10,32,128]{2,1,0:T(8,128)(2,1)S(1)}, f16[10,32,128]{2,1,0:T(8,128)(2,1)S(1)}, u32[]{:S(2)}, u32[]{:S(2)}) collective-permute-start(f16[10,32,128]{2,1,0:T(8,128)(2,1)S(1)} %pad_maximum_fusion.2), channel_id=1, source_target_pairs={{0,8},{1,9},{2,10},{3,11},{4,12},{5,13},{6,14},{7,15},{8,0},{9,1},... | collective-permute-start | bytes 245768 | tf_op jit(solution)/shard_map/ppermute | solution.py:438
  41.9 1.4 %collective-permute-start.7 = (f32[9,32,128]{2,1,0:T(8,128)S(1)}, f32[9,32,128]{2,1,0:T(8,128)S(1)}, u32[]{:S(2)}, u32[]{:S(2)}) collective-permute-start(f32[9,32,128]{2,1,0:T(8,128)S(1)} %add_multiply_fusion), channel_id=1, source_target_pairs={{0,1},{2,3},{4,5},{6,7},{8,9},{10,11},{12,13},{14,15},{1,0},{3,2},... | collective-permute-start | bytes 442376 | tf_op jit(solution)/shard_map/ppermute | solution.py:438

commit v7 on v6

--- a/solution.py
+++ b/solution.py
@@ -438,7 +438,7 @@
     return lax.ppermute(value, "tiles", both + [(b, a) for a, b in both])
 
 
-STATE_AT = 2
+STATE_AT = 8
 TOP = 13.0
 
 

time: 44.3 us -> 44.4 us (level)
  starting transfers between devices: 16.1 us -> 16.6 us
  waiting for transfers between devices: 10.2 us -> 9.73 us
    ppermute x8, starting transfers between devices: 7.38 us -> 7.93 us  [exchanged(): return lax.ppermute(value, 'tiles', both + [(b, a) for a, b in both])]
    ppermute x8, waiting for transfers between devices: 10.1 us -> 9.6 us  [exchanged(): return lax.ppermute(value, 'tiles', both + [(b, a) for a, b in both])]
where the time goes in v7:
time: 44.4 us; the launch traced here: 44.2 us
  starting transfers between devices  16.6 us (37%)
  Pallas kernels  15.8 us (36%)
  waiting for transfers between devices  9.73 us (22%)
  other arithmetic  1.21 us (3%)
  between operations  0.84 us (2%)
    ppermute x8, waiting for transfers between devices, exchanged(): return lax.ppermute(value, 'tiles', both + [(b, a) for a, b in both])  9.6 us
    pallas_call x1, Pallas kernels, main_part(): pl.pallas_call(main_kernel, in_specs=[SMEM, SMEM] + [VMEM] * 6, out_specs...  8.96 us
    all_to_all x1, starting transfers between devices, local(): received = lax.all_to_all(send, 'tiles', 0, 0, axis_index_groups=cores)  8.7 us
    ppermute x8, starting transfers between devices, exchanged(): return lax.ppermute(value, 'tiles', both + [(b, a) for a, b in both])  7.93 us
    pallas_call x1, Pallas kernels, state_part(): pl.pallas_call(state_kernel, in_specs=[VMEM] * 4, out_specs=VMEM, out_sha...  3.1 us
    pallas_call x1, Pallas kernels, pack(): pl.pallas_call(functools.partial(pack_kernel, chips), in_specs=[far, SMEM...  2.26 us
    pallas_call x1, Pallas kernels, edge_part(): pl.pallas_call(edge_kernel, in_specs=[SMEM, SMEM] + [VMEM] * 9, out_specs...  1.43 us
  transfers between devices with their start and end apart: 9, of which 6 were waited for; matrix products, arithmetic and copies ran while one was open for 0% of the time, Pallas kernels for 27%

profile of v7, /device:TPU:0, one launch (start us, length us, event | category | flops | bytes accessed | tf_op | source)
XLA Modules:
  0.0 44.2 jit_solution(1963245762982295225)
XLA Ops:
  0.6 0.0 copy-start
  0.6 0.0 copy-start.1
  0.7 0.0 copy-start.2
  0.7 0.0 copy-start.3
  0.7 0.0 copy-start.4
  0.7 2.3 %pack.1 = (bf16[2,2,2,32,128]{4,3,2,1,0:T(8,128)(2,1)S(1)}, bf16[8,2,2,32,128]{4,3,2,1,0:T(8,128)(2,1)}, bf16[4,128,128]{2,1,0:T(8,128)(2,1)S(1)}, bf16[4,128,128]{2,1,0:T(8,128)(2,1)S(1)}) custom-call(s32[1,8]{1,0:T(1,128)} %links.3, s32[1]{0:T(128)} %bitcast.me_ref, bf16[32,128,128]{2,1,0:T(8,128)(2,1)} %bitcast.24, bf16[32,128,128]{2,1,0:T(8,128)(2,1)} %bitcast.26), custom_call_target="tpu_custom_call" | custom-call | tf_op jit(solution)/shard_map/pack/pallas_call | solution.py:76
  3.0 0.5 %collective-permute-start = (bf16[4,128,128]{2,1,0:T(8,128)(2,1)S(1)}, bf16[4,128,128]{2,1,0:T(8,128)(2,1)S(1)}, u32[]{:S(2)}, u32[]{:S(2)}) collective-permute-start(bf16[4,128,128]{2,1,0:T(8,128)(2,1)S(1)} %get-tuple-element.21), channel_id=1, source_target_pairs={{0,1},{2,3},{4,5},{6,7},{8,9},{10,11},{12,13},{14,15},{1,0},{3,2},... | collective-permute-start | bytes 393224 | tf_op jit(solution)/shard_map/ppermute | solution.py:438
  3.5 0.7 %collective-permute-start.1 = (bf16[4,128,128]{2,1,0:T(8,128)(2,1)S(1)}, bf16[4,128,128]{2,1,0:T(8,128)(2,1)S(1)}, u32[]{:S(2)}, u32[]{:S(2)}) collective-permute-start(bf16[4,128,128]{2,1,0:T(8,128)(2,1)S(1)} %get-tuple-element.22), channel_id=1, source_target_pairs={{1,2},{3,4},{5,6},{7,8},{9,10},{11,12},{13,14},{2,1},{4,3},{6,5},{... | collective-permute-start | bytes 393224 | tf_op jit(solution)/shard_map/ppermute | solution.py:438
  4.1 8.7 %all-to-all-start = ((bf16[8,2,2,32,128]{4,3,2,1,0:T(8,128)(2,1)}), bf16[8,2,2,32,128]{4,3,2,1,0:T(8,128)(2,1)S(1)}, u32[]{:S(2)}, u32[]{:S(2)}) async-start(bf16[8,2,2,32,128]{4,3,2,1,0:T(8,128)(2,1)} %get-tuple-element.20), calls=%async_computation | async-start | bytes 524288 | tf_op jit(solution)/shard_map/all_to_all | solution.py:501
  12.8 0.0 collective-permute-done.on_in
  12.8 0.0 collective-permute-done.1.off_in
  12.9 0.0 copy-done
  12.9 9.0 %main.1 = (bf16[17,2,128,128]{3,2,1,0:T(8,128)(2,1)}, f32[9,32,128]{2,1,0:T(8,128)S(1)}, f32[9,32,128]{2,1,0:T(8,128)S(1)}) custom-call(s32[1,8]{1,0:T(1,128)S(1)} %copy-done.4, s32[1]{0:T(128)} %bitcast.me_ref, bf16[32,128,128]{2,1,0:T(8,128)(2,1)S(1)} %bitcast.25, bf16[32,128,128]{2,1,0:T(8,128)(2,1)S(1)} %bitcast.27, ...), custom_call_target="tpu_custom_call" | custom-call | flops 96636764160 | bytes 5242880 | tf_op jit(solution)/shard_map/main/pallas_call | solution.py:248
  21.9 0.1 all-to-all-done.received
  22.0 0.0 collective-permute-start.2
  22.0 1.5 %collective-permute-done.2.other_in = bf16[8,2,2,32,128]{4,3,2,1,0:T(8,128)(2,1)S(1)} collective-permute-done((bf16[8,2,2,32,128]{4,3,2,1,0:T(8,128)(2,1)S(1)}, bf16[8,2,2,32,128]{4,3,2,1,0:T(8,128)(2,1)S(1)}, u32[]{:S(2)}, u32[]{:S(2)}) %collective-permute-start.2) | collective-permute-done | bytes 262176 | tf_op jit(solution)/shard_map/ppermute | solution.py:438
  23.5 1.4 %edge.1 = (f32[10,32,128]{2,1,0:T(8,128)S(1)}, f32[10,32,128]{2,1,0:T(8,128)S(1)}, f32[192,128]{1,0:T(8,128)S(1)}) custom-call(s32[1,8]{1,0:T(1,128)S(1)} %copy-done.4, s32[1]{0:T(128)} %bitcast.me_ref, bf16[2,2,2,32,128]{4,3,2,1,0:T(8,128)(2,1)S(1)} %get-tuple-element.19.own, bf16[8,2,2,32,128]{4,3,2,1,0:T(8,128)(2,1)S(1)} %all-to-all-done.received, ...), custom_call_target="tpu_custom_call" | custom-call | flops 209715200 | bytes 3145728 | tf_op jit(solution)/shard_map/edge/pallas_call | solution.py:372
  25.0 0.1 collective-permute-start.3
  25.1 1.3 %collective-permute-done.3 = f32[10,32,128]{2,1,0:T(8,128)S(1)} collective-permute-done((f32[10,32,128]{2,1,0:T(8,128)S(1)}, f32[10,32,128]{2,1,0:T(8,128)S(1)}, u32[]{:S(2)}, u32[]{:S(2)}) %collective-permute-start.3) | collective-permute-done | bytes 163872 | tf_op jit(solution)/shard_map/ppermute | solution.py:438
  26.5 2.0 %collective-permute-start.4 = (f16[10,32,128]{2,1,0:T(8,128)(2,1)S(1)}, f16[10,32,128]{2,1,0:T(8,128)(2,1)S(1)}, u32[]{:S(2)}, u32[]{:S(2)}) collective-permute-start(f16[10,32,128]{2,1,0:T(8,128)(2,1)S(1)} %pad_maximum_fusion), channel_id=1, source_target_pairs={{0,2},{1,3},{4,6},{5,7},{8,10},{9,11},{12,14},{13,15},{2,0},{3,1},... | collective-permute-start | bytes 245768 | tf_op jit(solution)/shard_map/ppermute | solution.py:438
  28.5 2.8 %collective-permute-done.4 = f16[10,32,128]{2,1,0:T(8,128)(2,1)S(1)} collective-permute-done((f16[10,32,128]{2,1,0:T(8,128)(2,1)S(1)}, f16[10,32,128]{2,1,0:T(8,128)(2,1)S(1)}, u32[]{:S(2)}, u32[]{:S(2)}) %collective-permute-start.4) | collective-permute-done | bytes 81952 | tf_op jit(solution)/shard_map/ppermute | solution.py:438
  31.3 0.1 fusion.75
  31.3 0.1 multiply_convert_fusion.1
  31.4 1.8 %collective-permute-start.5 = (f16[10,32,128]{2,1,0:T(8,128)(2,1)S(1)}, f16[10,32,128]{2,1,0:T(8,128)(2,1)S(1)}, u32[]{:S(2)}, u32[]{:S(2)}) collective-permute-start(f16[10,32,128]{2,1,0:T(8,128)(2,1)S(1)} %pad_maximum_fusion.1), channel_id=1, source_target_pairs={{0,4},{1,5},{2,6},{3,7},{8,12},{9,13},{10,14},{11,15},{4,0},{5,1},... | collective-permute-start | bytes 245768 | tf_op jit(solution)/shard_map/ppermute | solution.py:438
  33.2 2.7 %collective-permute-done.5 = f16[10,32,128]{2,1,0:T(8,128)(2,1)S(1)} collective-permute-done((f16[10,32,128]{2,1,0:T(8,128)(2,1)S(1)}, f16[10,32,128]{2,1,0:T(8,128)(2,1)S(1)}, u32[]{:S(2)}, u32[]{:S(2)}) %collective-permute-start.5) | collective-permute-done | bytes 81952 | tf_op jit(solution)/shard_map/ppermute | solution.py:438
  35.9 0.1 fusion.78
  36.1 2.7 %collective-permute-start.6 = (f16[10,32,128]{2,1,0:T(8,128)(2,1)S(1)}, f16[10,32,128]{2,1,0:T(8,128)(2,1)S(1)}, u32[]{:S(2)}, u32[]{:S(2)}) collective-permute-start(f16[10,32,128]{2,1,0:T(8,128)(2,1)S(1)} %pad_maximum_fusion.2), channel_id=1, source_target_pairs={{0,8},{1,9},{2,10},{3,11},{4,12},{5,13},{6,14},{7,15},{8,0},{9,1},... | collective-permute-start | bytes 245768 | tf_op jit(solution)/shard_map/ppermute | solution.py:438
  38.8 3.1 %state.1 = bf16[32,128,128]{2,1,0:T(8,128)(2,1)} custom-call(bf16[17,2,128,128]{3,2,1,0:T(8,128)(2,1)S(1)} %copy-done.5, f32[192,128]{1,0:T(8,128)S(1)} %get-tuple-element.32.edge_grad, bf16[3,3,32,128]{3,2,1,0:T(8,128)(2,1)S(1)} %copy-done.3, bf16[32,128,128]{2,1,0:T(8,128)(2,1)S(1)} %bitcast.28), custom_call_target="tpu_custom_call" | custom-call | flops 1258291200 | bytes 3145728 | tf_op jit(solution)/shard_map/state/pallas_call | solution.py:421
  41.9 0.0 collective-permute-done.6
  42.0 0.1 collective-permute-start.7
  42.1 1.4 %collective-permute-done.7 = f32[9,32,128]{2,1,0:T(8,128)S(1)} collective-permute-done((f32[9,32,128]{2,1,0:T(8,128)S(1)}, f32[9,32,128]{2,1,0:T(8,128)S(1)}, u32[]{:S(2)}, u32[]{:S(2)}) %collective-permute-start.7) | collective-permute-done | bytes 147488 | tf_op jit(solution)/shard_map/ppermute | solution.py:438
  43.5 0.7 %broadcast_select_fusion = (f32[9,32,128]{2,1,0:T(8,128)}, f32[9,32,128]{2,1,0:T(8,128)}) fusion(f32[9,32,128]{2,1,0:T(8,128)S(1)} %collective-permute-done.7, f32[9,32,128]{2,1,0:T(8,128)S(1)} %add_multiply_fusion, pred[]{:T(512)S(6)} %eq.3), kind=kLoop, calls=%fused_computation.10 | loop fusion | flops 73728 | bytes 589825 | tf_op jit(solution)/shard_map/jit(_where)/select_n | solution.py:487
  (16 shorter events, 0.3 us)
Async XLA Ops:
  0.6 12.2 %copy-start = (bf16[1,32,128,128]{3,2,1,0:T(8,128)(2,1)S(1)}, bf16[1,32,128,128]{3,2,1,0:T(8,128)(2,1)}, u32[]{:S(2)}) copy-start(bf16[1,32,128,128]{3,2,1,0:T(8,128)(2,1)} %param.5) | copy-start | bytes 3145732
  0.6 12.2 %copy-start.1 = (bf16[1,32,128,128]{3,2,1,0:T(8,128)(2,1)S(1)}, bf16[1,32,128,128]{3,2,1,0:T(8,128)(2,1)}, u32[]{:S(2)}) copy-start(bf16[1,32,128,128]{3,2,1,0:T(8,128)(2,1)} %param.6) | copy-start | bytes 3145732
  0.7 12.2 %copy-start.2 = (bf16[3,3,32,128]{3,2,1,0:T(8,128)(2,1)S(1)}, bf16[3,3,32,128]{3,2,1,0:T(8,128)(2,1)}, u32[]{:S(2)}) copy-start(bf16[3,3,32,128]{3,2,1,0:T(8,128)(2,1)} %second_k.3) | copy-start | bytes 221188
  0.7 12.2 %copy-start.3 = (bf16[3,3,32,128]{3,2,1,0:T(8,128)(2,1)S(1)}, bf16[3,3,32,128]{3,2,1,0:T(8,128)(2,1)}, u32[]{:S(2)}) copy-start(bf16[3,3,32,128]{3,2,1,0:T(8,128)(2,1)} %first_k.5) | copy-start | bytes 221188
  0.7 12.2 %copy-start.4 = (s32[1,8]{1,0:T(1,128)S(1)}, s32[1,8]{1,0:T(1,128)}, u32[]{:S(2)}) copy-start(s32[1,8]{1,0:T(1,128)} %links.3) | copy-start | bytes 100
  3.0 9.9 %collective-permute-start = (bf16[4,128,128]{2,1,0:T(8,128)(2,1)S(1)}, bf16[4,128,128]{2,1,0:T(8,128)(2,1)S(1)}, u32[]{:S(2)}, u32[]{:S(2)}) collective-permute-start(bf16[4,128,128]{2,1,0:T(8,128)(2,1)S(1)} %get-tuple-element.21), channel_id=1, source_target_pairs={{0,1},{2,3},{4,5},{6,7},{8,9},{10,11},{12,13},{14,15},{1,0},{3,2},... | collective-permute-start | bytes 393224 | tf_op jit(solution)/shard_map/ppermute | solution.py:438
  3.5 9.4 %collective-permute-start.1 = (bf16[4,128,128]{2,1,0:T(8,128)(2,1)S(1)}, bf16[4,128,128]{2,1,0:T(8,128)(2,1)S(1)}, u32[]{:S(2)}, u32[]{:S(2)}) collective-permute-start(bf16[4,128,128]{2,1,0:T(8,128)(2,1)S(1)} %get-tuple-element.22), channel_id=1, source_target_pairs={{1,2},{3,4},{5,6},{7,8},{9,10},{11,12},{13,14},{2,1},{4,3},{6,5},{... | collective-permute-start | bytes 393224 | tf_op jit(solution)/shard_map/ppermute | solution.py:438
  4.1 17.9 %all-to-all-start = ((bf16[8,2,2,32,128]{4,3,2,1,0:T(8,128)(2,1)}), bf16[8,2,2,32,128]{4,3,2,1,0:T(8,128)(2,1)S(1)}, u32[]{:S(2)}, u32[]{:S(2)}) async-start(bf16[8,2,2,32,128]{4,3,2,1,0:T(8,128)(2,1)} %get-tuple-element.20), calls=%async_computation | async-start | bytes 524288 | tf_op jit(solution)/shard_map/all_to_all | solution.py:501
  22.0 1.5 %collective-permute-start.2 = (bf16[8,2,2,32,128]{4,3,2,1,0:T(8,128)(2,1)S(1)}, bf16[8,2,2,32,128]{4,3,2,1,0:T(8,128)(2,1)S(1)}, u32[]{:S(2)}, u32[]{:S(2)}) collective-permute-start(bf16[8,2,2,32,128]{4,3,2,1,0:T(8,128)(2,1)S(1)} %all-to-all-done.received), channel_id=1, source_target_pairs={{0,1},{2,3},{4,5},{6,7},{8,9},{10,11},{12,13},{14,15},{1,0},{3,2},... | collective-permute-start | bytes 786440 | tf_op jit(solution)/shard_map/ppermute | solution.py:438
  25.0 13.9 %copy-start.5 = (bf16[17,2,128,128]{3,2,1,0:T(8,128)(2,1)S(1)}, bf16[17,2,128,128]{3,2,1,0:T(8,128)(2,1)}, u32[]{:S(2)}) copy-start(bf16[17,2,128,128]{3,2,1,0:T(8,128)(2,1)} %get-tuple-element.31.grad) | copy-start | bytes 3342340
  25.0 1.4 %collective-permute-start.3 = (f32[10,32,128]{2,1,0:T(8,128)S(1)}, f32[10,32,128]{2,1,0:T(8,128)S(1)}, u32[]{:S(2)}, u32[]{:S(2)}) collective-permute-start(f32[10,32,128]{2,1,0:T(8,128)S(1)} %get-tuple-element.28), channel_id=1, source_target_pairs={{0,1},{2,3},{4,5},{6,7},{8,9},{10,11},{12,13},{14,15},{1,0},{3,2},... | collective-permute-start | bytes 491528 | tf_op jit(solution)/shard_map/ppermute | solution.py:438
  26.5 4.8 %collective-permute-start.4 = (f16[10,32,128]{2,1,0:T(8,128)(2,1)S(1)}, f16[10,32,128]{2,1,0:T(8,128)(2,1)S(1)}, u32[]{:S(2)}, u32[]{:S(2)}) collective-permute-start(f16[10,32,128]{2,1,0:T(8,128)(2,1)S(1)} %pad_maximum_fusion), channel_id=1, source_target_pairs={{0,2},{1,3},{4,6},{5,7},{8,10},{9,11},{12,14},{13,15},{2,0},{3,1},... | collective-permute-start | bytes 245768 | tf_op jit(solution)/shard_map/ppermute | solution.py:438
  31.4 4.5 %collective-permute-start.5 = (f16[10,32,128]{2,1,0:T(8,128)(2,1)S(1)}, f16[10,32,128]{2,1,0:T(8,128)(2,1)S(1)}, u32[]{:S(2)}, u32[]{:S(2)}) collective-permute-start(f16[10,32,128]{2,1,0:T(8,128)(2,1)S(1)} %pad_maximum_fusion.1), channel_id=1, source_target_pairs={{0,4},{1,5},{2,6},{3,7},{8,12},{9,13},{10,14},{11,15},{4,0},{5,1},... | collective-permute-start | bytes 245768 | tf_op jit(solution)/shard_map/ppermute | solution.py:438
  36.1 5.9 %collective-permute-start.6 = (f16[10,32,128]{2,1,0:T(8,128)(2,1)S(1)}, f16[10,32,128]{2,1,0:T(8,128)(2,1)S(1)}, u32[]{:S(2)}, u32[]{:S(2)}) collective-permute-start(f16[10,32,128]{2,1,0:T(8,128)(2,1)S(1)} %pad_maximum_fusion.2), channel_id=1, source_target_pairs={{0,8},{1,9},{2,10},{3,11},{4,12},{5,13},{6,14},{7,15},{8,0},{9,1},... | collective-permute-start | bytes 245768 | tf_op jit(solution)/shard_map/ppermute | solution.py:438
  42.0 1.4 %collective-permute-start.7 = (f32[9,32,128]{2,1,0:T(8,128)S(1)}, f32[9,32,128]{2,1,0:T(8,128)S(1)}, u32[]{:S(2)}, u32[]{:S(2)}) collective-permute-start(f32[9,32,128]{2,1,0:T(8,128)S(1)} %add_multiply_fusion), channel_id=1, source_target_pairs={{0,1},{2,3},{4,5},{6,7},{8,9},{10,11},{12,13},{14,15},{1,0},{3,2},... | collective-permute-start | bytes 442376 | tf_op jit(solution)/shard_map/ppermute | solution.py:438
